TPU v7x, 128 devices: a whole 4x4x4 slice. The times are simulated.
128 devices in a mesh: gx: 32 (over y, z, core), gy: 4 (over x).
Axes of the slice: x: 4, y: 4, z: 4, core: 2. Of those that a mesh axis runs over, the one named last changes fastest.
Arguments:
- cotangent: float32 [9, 256, 256, 256], P(None, 'gx', 'gy'), may hold values from -6 to 6
- fields_one: float32 [9, 256, 256, 256], P(None, 'gx', 'gy'), may hold values from 0 to 1
- fields_zero: float32 [9, 256, 256, 256], P(None, 'gx', 'gy'), may hold values from 0 to 1
- slot_grain: int32 [32, 32, 8], P('gx', 'gy'), may hold values from 0 to 1023, as said below
Outputs:
- adjoint_fields: float32 [9, 256, 256, 256], P(None, 'gx', 'gy')
- grain_grad: float32 [1024, 256], P(('gx', 'gy'))
Inputs may be any that keep to these rules, and one draw needn't show every extreme that they name: `slot_grain`: grain g is owned by device g // 8, devices counted with gx slowest. Every slot of a tile names a grain whose owner has the tile's index along gy. At most 4 of the slots of one device name grains of one owner, and in every draw some owner receives exactly 4 from every device of its gy group.
All inputs are finite; a program needn't handle non-finite values.
Results may differ from a plain program's by a relative error of at most 0.000096.
Values sent between devices are 32-bit elements; how exact they have to be, the bound alone decides.
No kernel may reach another device: no remote copies, remote signals or barrier semaphores. Data moves between devices by JAX's collectives and lax.ppermute only.
A program may use at most 128 MiB of HBM per device.

v0:
```python
import jax
import jax.numpy as jnp
from jax import lax
from jax.sharding import PartitionSpec as P

TILE = 8
GRAIN_DEV = 8


time_step = 0.05
well_height = 16.0
barrier = 1.0


def extended_2(block, sides, width):
    for axis, dim in sides:
        count = lax.axis_size(axis)
        forward = [(i, i + 1) for i in range(count - 1)]
        backward = [(target, source) for source, target in forward]
        low = lax.ppermute(
            lax.slice_in_dim(block, block.shape[dim] - width, None, axis=dim), axis, forward
        )
        high = lax.ppermute(lax.slice_in_dim(block, 0, width, axis=dim), axis, backward)
        block = jnp.concatenate([low, block, high], axis=dim)
    return block


def laplace(padded, margin):
    extended = jnp.pad(padded, [(0, 0)] * (padded.ndim - 1) + [(1, 1)])
    span_x = padded.shape[-3] - 2 * margin
    span_y = padded.shape[-2] - 2 * margin
    depth = padded.shape[-1]

    def shifted(step_x, step_y, step_z):
        return extended[
            ...,
            margin + step_x : margin + step_x + span_x,
            margin + step_y : margin + step_y + span_y,
            1 + step_z : 1 + step_z + depth,
        ]

    total = shifted(1, 0, 0) + shifted(-1, 0, 0) + shifted(0, 1, 0) + shifted(0, -1, 0)
    total = total + shifted(0, 0, 1) + shifted(0, 0, -1)
    return total - 6.0 * shifted(0, 0, 0)


def pointwise(costate, fields, lap_costate, lam_mu, lap_mu):
    density = fields[0]
    phases = fields[1:]
    lam_c = costate[0]
    lam_e = costate[1:]
    square_sum = jnp.sum(phases * phases, axis=0)
    weighted = jnp.sum(lam_e * phases, axis=0)
    coupled = jnp.sum(lam_e * (phases * phases - phases), axis=0)
    curvature = well_height * (2.0 - 12.0 * density + 12.0 * density * density) + 2.0 * barrier
    new_density = lam_c + lam_mu * curvature - lap_mu - 12.0 * barrier * time_step * coupled
    inner = (
        lam_e * (1.0 - density - 2.0 * (2.0 - density) * phases + square_sum)
        + 2.0 * phases * weighted
    )
    new_phases = lam_e - 12.0 * barrier * time_step * inner + time_step * lap_costate[1:]
    new_phases = new_phases + 12.0 * barrier * lam_mu * (phases * phases - phases)
    return jnp.concatenate([new_density[None], new_phases], axis=0)


def adjoint_step(costate, fields):
    extended = extended_2(costate, (("gx", 1), ("gy", 2)), 1)
    lap_costate = laplace(extended, 1)
    lam_mu = time_step * lap_costate[0]
    mu_padded = extended_2(lam_mu, (("gx", 0), ("gy", 1)), 1)
    lap_mu = laplace(mu_padded, 1)
    return pointwise(costate, fields, lap_costate, lam_mu, lap_mu)


def tile_rows(phase_costate):
    slots, size_x, size_y, depth = phase_costate.shape
    blocks = phase_costate.reshape(slots, size_x // TILE, TILE, size_y // TILE, TILE, depth)
    summed = jnp.sum(blocks, axis=(2, 4))
    return jnp.transpose(summed, (1, 2, 0, 3)).reshape(-1, depth)


def pack_rows(partial_value, slot_grain):
    grains = slot_grain.reshape(-1)
    row_count = grains.shape[0]
    peer_count = lax.axis_size("gx")
    groups = lax.axis_size("gy")
    capacity = max(2, 2 * row_count // peer_count)
    peer_gx = grains // GRAIN_DEV // groups
    local_id = grains % GRAIN_DEV
    row_index = jnp.arange(row_count)
    before = (peer_gx[None, :] == peer_gx[:, None]) & (row_index[None, :] < row_index[:, None])
    position = jnp.sum(before.astype(jnp.int32), axis=1)
    target = peer_gx * capacity + position
    selector = (jnp.arange(peer_count * capacity)[:, None] == target[None, :]).astype(jnp.float32)
    send_rows = jnp.dot(selector, partial_value, precision=lax.Precision.HIGHEST).reshape(
        peer_count, capacity, -1
    )
    labels = jnp.dot(selector, (local_id + 1).astype(jnp.float32), precision=lax.Precision.HIGHEST)
    return (send_rows, labels.reshape(peer_count, capacity))


def unpack_rows(got_rows, got_labels):
    wanted = (jnp.arange(GRAIN_DEV) + 1).astype(jnp.float32)
    selector = (got_labels.reshape(-1)[None, :] == wanted[:, None]).astype(jnp.float32)
    flat_rows = got_rows.reshape(-1, got_rows.shape[-1])
    return jnp.dot(selector, flat_rows, precision=lax.Precision.HIGHEST)


def shards(cotangent, fields_one, fields_zero, slot_grain):
    costate_one = adjoint_step(cotangent, fields_one)
    adjoint_fields = adjoint_step(costate_one, fields_zero)
    partial_value = time_step * tile_rows(cotangent[1:]) + time_step * tile_rows(costate_one[1:])
    send_rows, labels = pack_rows(partial_value, slot_grain)
    got_rows, got_labels = (
        lax.all_to_all(send_rows, "gx", split_axis=0, concat_axis=0, tiled=True),
        lax.all_to_all(labels, "gx", split_axis=0, concat_axis=0, tiled=True),
    )
    grain_grad = unpack_rows(got_rows, got_labels)
    return (adjoint_fields, grain_grad)


def solution(mesh):
    placed = (
        P(None, "gx", "gy", None),
        P(None, "gx", "gy", None),
        P(None, "gx", "gy", None),
        P("gx", "gy", None),
    )
    return jax.shard_map(
        shards,
        mesh=mesh,
        in_specs=placed,
        out_specs=(P(None, "gx", "gy", None), P(("gx", "gy"), None)),
        check_vma=False,
    )
```

profile of v0, /device:TPU:28, one launch (start us, length us, event | category | flops | bytes accessed | tf_op | source)
XLA Modules:
  0.0 158.7 jit_solution(296224551623722996)
XLA Ops:
  0.6 2.4 %fusion.62 = (f32[9,1,64,256]{3,2,1,0:T(8,128)}, f32[9,1,64,256]{3,2,1,0:T(8,128)}) fusion(f32[9,8,64,256]{3,2,1,0:T(8,128)} %param.4), kind=kLoop, calls=%fused_computation.187 | loop fusion | bytes 2359296 | tf_op jit(solution)/shard_map/slice | solution.py:23
  3.0 1.9 %collective-permute-start.1 = (f32[9,1,64,256]{3,2,1,0:T(8,128)}, f32[9,1,64,256]{3,2,1,0:T(8,128)S(1)}, u32[]{:S(2)}, u32[]{:S(2)}) collective-permute-start(f32[9,1,64,256]{3,2,1,0:T(8,128)} %get-tuple-element.30), channel_id=1, source_target_pairs={{0,4},{4,8},{8,12},{12,16},{16,20},{20,24},{24,28},{28,32},{32,36}... | collective-permute-start | bytes 1769480 | tf_op jit(solution)/shard_map/ppermute | solution.py:20
  4.9 5.8 %collective-permute-start = (f32[9,1,64,256]{3,2,1,0:T(8,128)}, f32[9,1,64,256]{3,2,1,0:T(8,128)S(1)}, u32[]{:S(2)}, u32[]{:S(2)}) collective-permute-start(f32[9,1,64,256]{3,2,1,0:T(8,128)} %get-tuple-element.29), channel_id=1, source_target_pairs={{4,0},{8,4},{12,8},{16,12},{20,16},{24,20},{28,24},{32,28},{36,32}... | collective-permute-start | bytes 1769480 | tf_op jit(solution)/shard_map/ppermute | solution.py:23
  10.7 0.8 reshape.180
  12.7 0.7 copy.86
  13.5 6.4 %all-to-all-start = ((f32[32,1,4]{2,1,0:T(1,128)}), f32[32,1,4]{2,1,0:T(1,128)S(1)}, u32[]{:S(2)}, u32[]{:S(2)}) async-start(f32[32,1,4]{2,1,0:T(1,128)} %copy.86), calls=%async_computation | async-start | bytes 32768 | tf_op jit(solution)/shard_map/all_to_all | solution.py:116
  19.9 5.2 %multiply_reduce_fusion.4 = (f32[8,64,256]{2,1,0:T(8,128)S(1)}, f32[8,64,256]{2,1,0:T(8,128)S(1)}, f32[8,64,256]{2,1,0:T(8,128)S(1)}, f32[8,64,256]{2,1,0:T(8,128)}) fusion(f32[9,8,64,256]{3,2,1,0:T(8,128)} %param.5, f32[9,8,64,256]{3,2,1,0:T(8,128)} %param.4), kind=kLoop, calls=%fused_computation.57 | loop fusion | flops 7864320 | bytes 10485760 | tf_op jit(solution)/shard_map/reduce_sum | solution.py:53
  25.1 2.1 %subtract_bitcast_fusion.1 = (f32[8,64,256]{2,1,0:T(8,128)}, f32[8,64,256]{2,1,0:T(8,128)}) fusion(f32[9,8,64,256]{3,2,1,0:T(8,128)} %param.5), kind=kLoop, calls=%fused_computation.127 | loop fusion | flops 393216 | bytes 1572864 | tf_op jit(solution)/shard_map/sub | solution.py:58
  27.2 1.9 %subtract_bitcast_fusion = (f32[8,64,256]{2,1,0:T(8,128)S(1)}, f32[8,64,256]{2,1,0:T(8,128)}) fusion(f32[9,8,64,256]{3,2,1,0:T(8,128)} %param.6), kind=kLoop, calls=%fused_computation.124 | loop fusion | flops 393216 | bytes 1572864 | tf_op jit(solution)/shard_map/sub | solution.py:58
  29.1 0.8 broadcast_multiply_fusion
  30.9 2.4 %collective-permute-start.2 = (f32[9,10,1,256]{3,1,2,0:T(8,128)S(1)}, f32[9,10,1,256]{3,1,2,0:T(8,128)S(1)}, u32[]{:S(2)}, u32[]{:S(2)}) collective-permute-start(f32[9,10,1,256]{3,1,2,0:T(8,128)S(1)} %copy.74), channel_id=1, source_target_pairs={{1,0},{2,1},{3,2},{5,4},{6,5},{7,6},{9,8},{10,9},{11,10},{13,12},{... | collective-permute-start | bytes 276488 | tf_op jit(solution)/shard_map/ppermute | solution.py:23
  33.4 3.4 %collective-permute-start.3 = (f32[9,10,1,256]{3,1,2,0:T(8,128)S(1)}, f32[9,10,1,256]{3,1,2,0:T(8,128)S(1)}, u32[]{:S(2)}, u32[]{:S(2)}) collective-permute-start(f32[9,10,1,256]{3,1,2,0:T(8,128)S(1)} %copy.76), channel_id=1, source_target_pairs={{0,1},{1,2},{2,3},{4,5},{5,6},{6,7},{8,9},{9,10},{10,11},{12,13},{... | collective-permute-start | bytes 276488 | tf_op jit(solution)/shard_map/ppermute | solution.py:20
  37.0 1.8 %collective-permute-done.2 = f32[9,10,1,256]{3,1,2,0:T(8,128)S(1)} collective-permute-done((f32[9,10,1,256]{3,1,2,0:T(8,128)S(1)}, f32[9,10,1,256]{3,1,2,0:T(8,128)S(1)}, u32[]{:S(2)}, u32[]{:S(2)}) %collective-permute-start.2) | collective-permute-done | bytes 92192 | tf_op jit(solution)/shard_map/ppermute | solution.py:23
  38.8 2.1 %collective-permute-done.3 = f32[9,10,1,256]{3,1,2,0:T(8,128)S(1)} collective-permute-done((f32[9,10,1,256]{3,1,2,0:T(8,128)S(1)}, f32[9,10,1,256]{3,1,2,0:T(8,128)S(1)}, u32[]{:S(2)}, u32[]{:S(2)}) %collective-permute-start.3) | collective-permute-done | bytes 92192 | tf_op jit(solution)/shard_map/ppermute | solution.py:20
  41.0 4.9 %select_maximum_fusion.5 = f32[9,10,66,258]{3,2,1,0:T(8,128)S(1)} fusion(f32[9,10,1,256]{3,2,1,0:T(1,128)S(1)} %copy.75, f32[9,10,64,256]{3,2,1,0:T(8,128)S(1)} %constant_dynamic-update-slice_fusion, f32[9,10,1,256]{3,2,1,0:T(1,128)S(1)} %copy.77), kind=kLoop, calls=%fused_computation.7 | loop fusion | flops 12260160 | bytes 12212640 | tf_op jit(solution)/shard_map/concatenate | solution.py:24
  45.9 6.2 %fusion.6 = f32[9,8,64,256]{3,2,1,0:T(8,128)} fusion(f32[9,10,66,258]{3,2,1,0:T(8,128)S(1)} %select_maximum_fusion.5, f32[9,10,64,256]{3,2,1,0:T(8,128)S(1)} %constant_dynamic-update-slice_fusion, f32[9,10,1,256]{3,2,1,0:T(1,128)S(1)} %copy.77, f32[9,10,1,256]{3,2,1,0:T(1,128)S(1)} %copy.75, f32[9,8,64,256]{3,2,1,0:T(8,128)S(1)} %bitcast.57, ...), kind=kLoop, calls=%fused_computation.37 | loop fusion | flops 12976128 | bytes 26136576 | tf_op jit(solution)/shard_map/sub | solution.py:44
  52.1 1.2 multiply_bitcast_fusion.2
  53.3 3.5 %collective-permute-start.4 = (f32[1,64,256]{2,1,0:T(8,128)S(1)}, f32[1,64,256]{2,1,0:T(8,128)S(1)}, u32[]{:S(2)}, u32[]{:S(2)}) collective-permute-start(f32[1,64,256]{2,1,0:T(8,128)S(1)} %get-tuple-element.38), channel_id=1, source_target_pairs={{4,0},{8,4},{12,8},{16,12},{20,16},{24,20},{28,24},{32,28},{36,32}... | collective-permute-start | bytes 196616 | tf_op jit(solution)/shard_map/ppermute | solution.py:23
  56.8 1.9 %collective-permute-start.5 = (f32[1,64,256]{2,1,0:T(8,128)S(1)}, f32[1,64,256]{2,1,0:T(8,128)S(1)}, u32[]{:S(2)}, u32[]{:S(2)}) collective-permute-start(f32[1,64,256]{2,1,0:T(8,128)S(1)} %get-tuple-element.37), channel_id=1, source_target_pairs={{0,4},{4,8},{8,12},{12,16},{16,20},{20,24},{24,28},{28,32},{32,36}... | collective-permute-start | bytes 196616 | tf_op jit(solution)/shard_map/ppermute | solution.py:20
  60.1 4.4 %collective-permute-done.5 = f32[1,64,256]{2,1,0:T(8,128)S(1)} collective-permute-done((f32[1,64,256]{2,1,0:T(8,128)S(1)}, f32[1,64,256]{2,1,0:T(8,128)S(1)}, u32[]{:S(2)}, u32[]{:S(2)}) %collective-permute-start.5) | collective-permute-done | bytes 65568 | tf_op jit(solution)/shard_map/ppermute | solution.py:20
  64.5 2.4 %collective-permute-start.6 = (f32[10,1,256]{2,1,0:T(1,128)S(1)}, f32[10,1,256]{2,1,0:T(1,128)S(1)}, u32[]{:S(2)}, u32[]{:S(2)}) collective-permute-start(f32[10,1,256]{2,1,0:T(1,128)S(1)} %get-tuple-element.34), channel_id=1, source_target_pairs={{1,0},{2,1},{3,2},{5,4},{6,5},{7,6},{9,8},{10,9},{11,10},{13,12},{... | collective-permute-start | bytes 30728 | tf_op jit(solution)/shard_map/ppermute | solution.py:23
  67.0 3.4 %collective-permute-start.7 = (f32[10,1,256]{2,1,0:T(1,128)S(1)}, f32[10,1,256]{2,1,0:T(1,128)S(1)}, u32[]{:S(2)}, u32[]{:S(2)}) collective-permute-start(f32[10,1,256]{2,1,0:T(1,128)S(1)} %get-tuple-element.33), channel_id=1, source_target_pairs={{0,1},{1,2},{2,3},{4,5},{5,6},{6,7},{8,9},{9,10},{10,11},{12,13},{... | collective-permute-start | bytes 30728 | tf_op jit(solution)/shard_map/ppermute | solution.py:20
  70.4 9.5 %multiply_reduce_fusion.3 = (f32[8,64,256]{2,1,0:T(8,128)}, f32[8,64,256]{2,1,0:T(8,128)}, f32[8,64,256]{2,1,0:T(8,128)}, f32[8,64,256]{2,1,0:T(8,128)S(1)}, f32[8,8,64,256]{3,2,1,0:T(8,128)S(1)}) fusion(f32[9,8,64,256]{3,2,1,0:T(8,128)} %param.6, f32[8,64,256]{2,1,0:T(8,128)S(1)} %get-tuple-element.26, f32[9,8,64,256]{3,2,1,0:T(8,128)} %fusion.6, ...), kind=kLoop, calls=%fused_computation.56 | loop fusion | flops 22544384 | bytes 25690112 | tf_op jit(solution)/shard_map/reduce_sum | solution.py:54
  80.3 2.9 %fusion.23 = f32[8,64,256]{2,1,0:T(8,128)S(1)} fusion(f32[8,64,256]{2,1,0:T(8,128)S(1)} %get-tuple-element.27, f32[10,66,258]{2,1,0:T(8,128)S(1)} %select_maximum_fusion.11, f32[10,1,256]{2,1,0:T(1,128)S(1)} %collective-permute-done.7, f32[1,64,256]{2,1,0:T(8,128)S(1)} %collective-permute-done.4, f32[1,64,256]{2,1,0:T(8,128)S(1)} %collective-permute-done.5, ...), kind=kLoop, calls=%fused_computation.83 | loop fusion | flops 3407872 | bytes 4345856 | tf_op jit(solution)/shard_map/sub | solution.py:56
  83.3 1.1 fusion.16
  84.3 2.0 %collective-permute-start.8 = (f32[9,1,64,256]{3,2,1,0:T(8,128)}, f32[9,1,64,256]{3,2,1,0:T(8,128)S(1)}, u32[]{:S(2)}, u32[]{:S(2)}) collective-permute-start(f32[9,1,64,256]{3,2,1,0:T(8,128)} %get-tuple-element.23), channel_id=1, source_target_pairs={{4,0},{8,4},{12,8},{16,12},{20,16},{24,20},{28,24},{32,28},{36,32}... | collective-permute-start | bytes 1769480 | tf_op jit(solution)/shard_map/ppermute | solution.py:23
  86.4 2.4 %collective-permute-start.9 = (f32[9,1,64,256]{3,2,1,0:T(8,128)}, f32[9,1,64,256]{3,2,1,0:T(8,128)S(1)}, u32[]{:S(2)}, u32[]{:S(2)}) collective-permute-start(f32[9,1,64,256]{3,2,1,0:T(8,128)} %get-tuple-element.22), channel_id=1, source_target_pairs={{0,4},{4,8},{8,12},{12,16},{16,20},{20,24},{24,28},{28,32},{32,36}... | collective-permute-start | bytes 1769480 | tf_op jit(solution)/shard_map/ppermute | solution.py:20
  89.2 0.8 copy.88
  90.0 7.5 %all-to-all-start.1 = ((f32[32,4,256]{2,1,0:T(4,128)}), f32[32,4,256]{2,1,0:T(4,128)S(1)}, u32[]{:S(2)}, u32[]{:S(2)}) async-start(f32[32,4,256]{2,1,0:T(4,128)} %copy.88), calls=%async_computation.1 | async-start | bytes 262144 | tf_op jit(solution)/shard_map/all_to_all | solution.py:115
  97.5 2.4 %collective-permute-done.9 = f32[9,1,64,256]{3,2,1,0:T(8,128)S(1)} collective-permute-done((f32[9,1,64,256]{3,2,1,0:T(8,128)}, f32[9,1,64,256]{3,2,1,0:T(8,128)S(1)}, u32[]{:S(2)}, u32[]{:S(2)}) %collective-permute-start.9) | collective-permute-done | bytes 589856 | tf_op jit(solution)/shard_map/ppermute | solution.py:20
  99.9 1.3 pad_maximum_fusion.34
  101.3 2.4 %collective-permute-start.10 = (f32[9,10,1,256]{3,1,2,0:T(8,128)S(1)}, f32[9,10,1,256]{3,1,2,0:T(8,128)S(1)}, u32[]{:S(2)}, u32[]{:S(2)}) collective-permute-start(f32[9,10,1,256]{3,1,2,0:T(8,128)S(1)} %copy.80), channel_id=1, source_target_pairs={{1,0},{2,1},{3,2},{5,4},{6,5},{7,6},{9,8},{10,9},{11,10},{13,12},{... | collective-permute-start | bytes 276488 | tf_op jit(solution)/shard_map/ppermute | solution.py:23
  104.4 3.6 %collective-permute-start.11 = (f32[9,10,1,256]{3,1,2,0:T(8,128)}, f32[9,10,1,256]{3,1,2,0:T(8,128)S(1)}, u32[]{:S(2)}, u32[]{:S(2)}) collective-permute-start(f32[9,10,1,256]{3,1,2,0:T(8,128)} %copy.82), channel_id=1, source_target_pairs={{0,1},{1,2},{2,3},{4,5},{5,6},{6,7},{8,9},{9,10},{10,11},{12,13},{... | collective-permute-start | bytes 276488 | tf_op jit(solution)/shard_map/ppermute | solution.py:20
  108.0 0.8 broadcast_multiply_fusion.1
  108.9 0.7 reshape.181
  109.7 2.0 %collective-permute-done.11 = f32[9,10,1,256]{3,1,2,0:T(8,128)S(1)} collective-permute-done((f32[9,10,1,256]{3,1,2,0:T(8,128)}, f32[9,10,1,256]{3,1,2,0:T(8,128)S(1)}, u32[]{:S(2)}, u32[]{:S(2)}) %collective-permute-start.11) | collective-permute-done | bytes 92192 | tf_op jit(solution)/shard_map/ppermute | solution.py:20
  111.8 10.3 %select_maximum_fusion = f32[9,10,66,258]{3,2,1,0:T(8,128)} fusion(f32[9,10,1,256]{3,2,1,0:T(1,128)S(1)} %copy.81, f32[9,10,1,256]{3,2,1,0:T(1,128)S(1)} %copy.83, f32[9,1,64,256]{3,2,1,0:T(8,128)S(1)} %collective-permute-done.8, f32[9,1,64,256]{3,2,1,0:T(8,128)S(1)} %collective-permute-done.9, f32[8,8,64,256]{3,2,1,0:T(8,128)} %copy-done, ...), kind=kLoop, calls=%fused_computation.2 | loop fusion | flops 21455280 | bytes 12212640 | tf_op jit(solution)/shard_map/concatenate | solution.py:24
  122.1 10.3 %fusion.2 = f32[9,8,64,256]{3,2,1,0:T(8,128)} fusion(f32[1,8,64,256]{3,2,1,0:T(8,128)S(1)} %bitcast.61, f32[9,10,66,258]{3,2,1,0:T(8,128)} %select_maximum_fusion, f32[9,10,1,256]{3,2,1,0:T(1,128)S(1)} %copy.83, f32[9,1,64,256]{3,2,1,0:T(8,128)S(1)} %collective-permute-done.8, f32[9,1,64,256]{3,2,1,0:T(8,128)S(1)} %collective-permute-done.9, ...), kind=kLoop, calls=%fused_computation.18 | loop fusion | flops 23592960 | bytes 20238336 | tf_op jit(solution)/shard_map/sub | solution.py:44
  132.4 1.2 slice_multiply_fusion.2
  133.6 1.9 %collective-permute-start.12 = (f32[1,64,256]{2,1,0:T(8,128)S(1)}, f32[1,64,256]{2,1,0:T(8,128)S(1)}, u32[]{:S(2)}, u32[]{:S(2)}) collective-permute-start(f32[1,64,256]{2,1,0:T(8,128)S(1)} %get-tuple-element.36), channel_id=1, source_target_pairs={{4,0},{8,4},{12,8},{16,12},{20,16},{24,20},{28,24},{32,28},{36,32}... | collective-permute-start | bytes 196616 | tf_op jit(solution)/shard_map/ppermute | solution.py:23
  135.5 2.4 %collective-permute-start.13 = (f32[1,64,256]{2,1,0:T(8,128)S(1)}, f32[1,64,256]{2,1,0:T(8,128)S(1)}, u32[]{:S(2)}, u32[]{:S(2)}) collective-permute-start(f32[1,64,256]{2,1,0:T(8,128)S(1)} %get-tuple-element.35), channel_id=1, source_target_pairs={{0,4},{4,8},{8,12},{12,16},{16,20},{20,24},{24,28},{28,32},{32,36}... | collective-permute-start | bytes 196616 | tf_op jit(solution)/shard_map/ppermute | solution.py:20
  138.0 1.7 %fusion.54 = f32[8,256]{1,0:T(8,128)} fusion(f32[128,256]{1,0:T(8,128)} %reshape.181, f32[128]{0:T(128)S(1)} %eq.65, f32[8]{0:T(128)S(1)} %add_convert_fusion), kind=kOutput, calls=%fused_computation.169 | convolution fusion | flops 3146752 | bytes 139808 | tf_op jit(solution)/shard_map/dot_general | solution.py:106
  139.7 3.6 %collective-permute-done.13 = f32[1,64,256]{2,1,0:T(8,128)S(1)} collective-permute-done((f32[1,64,256]{2,1,0:T(8,128)S(1)}, f32[1,64,256]{2,1,0:T(8,128)S(1)}, u32[]{:S(2)}, u32[]{:S(2)}) %collective-permute-start.13) | collective-permute-done | bytes 65568 | tf_op jit(solution)/shard_map/ppermute | solution.py:20
  143.3 2.2 %collective-permute-start.14 = (f32[10,1,256]{2,1,0:T(1,128)S(1)}, f32[10,1,256]{2,1,0:T(1,128)S(1)}, u32[]{:S(2)}, u32[]{:S(2)}) collective-permute-start(f32[10,1,256]{2,1,0:T(1,128)S(1)} %get-tuple-element.32), channel_id=1, source_target_pairs={{1,0},{2,1},{3,2},{5,4},{6,5},{7,6},{9,8},{10,9},{11,10},{13,12},{... | collective-permute-start | bytes 30728 | tf_op jit(solution)/shard_map/ppermute | solution.py:23
  145.4 3.7 %collective-permute-start.15 = (f32[10,1,256]{2,1,0:T(1,128)S(1)}, f32[10,1,256]{2,1,0:T(1,128)S(1)}, u32[]{:S(2)}, u32[]{:S(2)}) collective-permute-start(f32[10,1,256]{2,1,0:T(1,128)S(1)} %get-tuple-element.31), channel_id=1, source_target_pairs={{0,1},{1,2},{2,3},{4,5},{5,6},{6,7},{8,9},{9,10},{10,11},{12,13},{... | collective-permute-start | bytes 30728 | tf_op jit(solution)/shard_map/ppermute | solution.py:20
  149.1 4.9 %fusion.11 = f32[8,8,64,256]{3,2,1,0:T(8,128)S(1)} fusion(f32[9,8,64,256]{3,2,1,0:T(8,128)} %fusion.2, f32[8,8,64,256]{3,2,1,0:T(8,128)S(1)} %copy-done.1, f32[9,8,64,256]{3,2,1,0:T(8,128)} %param.6, f32[8,64,256]{2,1,0:T(8,128)S(1)} %get-tuple-element.19, f32[8,64,256]{2,1,0:T(8,128)} %broadcast_multiply_fusion.1, f32[8,64,256]{2,1,0:T(8,128)} %get-tuple-element.10, ...), kind=kLoop, calls=%fused_computation.51 | loop fusion | flops 14680064 | bytes 19398656 | tf_op jit(solution)/shard_map/add | solution.py:62
  154.5 1.8 %fusion.31 = f32[1,8,64,256]{3,2,1,0:T(8,128)S(1)} fusion(f32[8,64,256]{2,1,0:T(8,128)S(1)} %fusion.23, f32[8,64,256]{2,1,0:T(8,128)S(1)} %get-tuple-element.18, f32[10,66,258]{2,1,0:T(8,128)S(1)} %select_maximum_fusion.7, f32[10,1,256]{2,1,0:T(1,128)S(1)} %collective-permute-done.15, f32[1,64,256]{2,1,0:T(8,128)S(1)} %collective-permute-done.12, ...), kind=kLoop, calls=%fused_computation.91 | loop fusion | flops 3407872 | bytes 4345856 | tf_op jit(solution)/shard_map/broadcast_in_dim | solution.py:63
  156.2 2.5 %pad_maximum_fusion.17 = f32[9,8,64,256]{3,2,1,0:T(8,128)} fusion(f32[8,8,64,256]{3,2,1,0:T(8,128)S(1)} %fusion.11, f32[1,8,64,256]{3,2,1,0:T(8,128)S(1)} %fusion.31), kind=kLoop, calls=%fused_computation.46 | loop fusion | flops 1179648 | bytes 9437184 | tf_op jit(solution)/shard_map/concatenate | solution.py:63
  (58 shorter events, 6.1 us)
Async XLA Ops:
  3.0 27.0 %collective-permute-start.1 = (f32[9,1,64,256]{3,2,1,0:T(8,128)}, f32[9,1,64,256]{3,2,1,0:T(8,128)S(1)}, u32[]{:S(2)}, u32[]{:S(2)}) collective-permute-start(f32[9,1,64,256]{3,2,1,0:T(8,128)} %get-tuple-element.30), channel_id=1, source_target_pairs={{0,4},{4,8},{8,12},{12,16},{16,20},{20,24},{24,28},{28,32},{32,36}... | collective-permute-start | bytes 1769480 | tf_op jit(solution)/shard_map/ppermute | solution.py:20
  4.9 25.8 %collective-permute-start = (f32[9,1,64,256]{3,2,1,0:T(8,128)}, f32[9,1,64,256]{3,2,1,0:T(8,128)S(1)}, u32[]{:S(2)}, u32[]{:S(2)}) collective-permute-start(f32[9,1,64,256]{3,2,1,0:T(8,128)} %get-tuple-element.29), channel_id=1, source_target_pairs={{4,0},{8,4},{12,8},{16,12},{20,16},{24,20},{28,24},{32,28},{36,32}... | collective-permute-start | bytes 1769480 | tf_op jit(solution)/shard_map/ppermute | solution.py:23
  13.5 16.6 %slice-start = ((s8[4718592]{0:T(1024)(128)(4,1)}), s8[524288]{0:T(1024)(128)(4,1)S(1)}, s32[]{:S(2)}) async-start(s8[4718592]{0:T(1024)(128)(4,1)} %bitcast.56), calls=%async_computation.2 | async-start | bytes 1048576
  13.5 45.3 %all-to-all-start = ((f32[32,1,4]{2,1,0:T(1,128)}), f32[32,1,4]{2,1,0:T(1,128)S(1)}, u32[]{:S(2)}, u32[]{:S(2)}) async-start(f32[32,1,4]{2,1,0:T(1,128)} %copy.86), calls=%async_computation | async-start | bytes 32768 | tf_op jit(solution)/shard_map/all_to_all | solution.py:116
  19.9 10.2 %slice-start.1 = ((s8[4718592]{0:T(1024)(128)(4,1)}), s8[4194304]{0:T(1024)(128)(4,1)S(1)}, s32[]{:S(2)}) async-start(s8[4718592]{0:T(1024)(128)(4,1)} %bitcast.56), calls=%async_computation.3 | async-start | bytes 8388608
  30.9 7.8 %collective-permute-start.2 = (f32[9,10,1,256]{3,1,2,0:T(8,128)S(1)}, f32[9,10,1,256]{3,1,2,0:T(8,128)S(1)}, u32[]{:S(2)}, u32[]{:S(2)}) collective-permute-start(f32[9,10,1,256]{3,1,2,0:T(8,128)S(1)} %copy.74), channel_id=1, source_target_pairs={{1,0},{2,1},{3,2},{5,4},{6,5},{7,6},{9,8},{10,9},{11,10},{13,12},{... | collective-permute-start | bytes 276488 | tf_op jit(solution)/shard_map/ppermute | solution.py:23
  33.4 7.5 %collective-permute-start.3 = (f32[9,10,1,256]{3,1,2,0:T(8,128)S(1)}, f32[9,10,1,256]{3,1,2,0:T(8,128)S(1)}, u32[]{:S(2)}, u32[]{:S(2)}) collective-permute-start(f32[9,10,1,256]{3,1,2,0:T(8,128)S(1)} %copy.76), channel_id=1, source_target_pairs={{0,1},{1,2},{2,3},{4,5},{5,6},{6,7},{8,9},{9,10},{10,11},{12,13},{... | collective-permute-start | bytes 276488 | tf_op jit(solution)/shard_map/ppermute | solution.py:20
  53.3 6.7 %collective-permute-start.4 = (f32[1,64,256]{2,1,0:T(8,128)S(1)}, f32[1,64,256]{2,1,0:T(8,128)S(1)}, u32[]{:S(2)}, u32[]{:S(2)}) collective-permute-start(f32[1,64,256]{2,1,0:T(8,128)S(1)} %get-tuple-element.38), channel_id=1, source_target_pairs={{4,0},{8,4},{12,8},{16,12},{20,16},{24,20},{28,24},{32,28},{36,32}... | collective-permute-start | bytes 196616 | tf_op jit(solution)/shard_map/ppermute | solution.py:23
  56.8 7.7 %collective-permute-start.5 = (f32[1,64,256]{2,1,0:T(8,128)S(1)}, f32[1,64,256]{2,1,0:T(8,128)S(1)}, u32[]{:S(2)}, u32[]{:S(2)}) collective-permute-start(f32[1,64,256]{2,1,0:T(8,128)S(1)} %get-tuple-element.37), channel_id=1, source_target_pairs={{0,4},{4,8},{8,12},{12,16},{16,20},{20,24},{24,28},{28,32},{32,36}... | collective-permute-start | bytes 196616 | tf_op jit(solution)/shard_map/ppermute | solution.py:20
  64.5 15.3 %collective-permute-start.6 = (f32[10,1,256]{2,1,0:T(1,128)S(1)}, f32[10,1,256]{2,1,0:T(1,128)S(1)}, u32[]{:S(2)}, u32[]{:S(2)}) collective-permute-start(f32[10,1,256]{2,1,0:T(1,128)S(1)} %get-tuple-element.34), channel_id=1, source_target_pairs={{1,0},{2,1},{3,2},{5,4},{6,5},{7,6},{9,8},{10,9},{11,10},{13,12},{... | collective-permute-start | bytes 30728 | tf_op jit(solution)/shard_map/ppermute | solution.py:23
  67.0 12.9 %collective-permute-start.7 = (f32[10,1,256]{2,1,0:T(1,128)S(1)}, f32[10,1,256]{2,1,0:T(1,128)S(1)}, u32[]{:S(2)}, u32[]{:S(2)}) collective-permute-start(f32[10,1,256]{2,1,0:T(1,128)S(1)} %get-tuple-element.33), channel_id=1, source_target_pairs={{0,1},{1,2},{2,3},{4,5},{5,6},{6,7},{8,9},{9,10},{10,11},{12,13},{... | collective-permute-start | bytes 30728 | tf_op jit(solution)/shard_map/ppermute | solution.py:20
  79.9 4.5 %copy-start = (f32[8,8,64,256]{3,2,1,0:T(8,128)}, f32[8,8,64,256]{3,2,1,0:T(8,128)S(1)}, u32[]{:S(2)}) copy-start(f32[8,8,64,256]{3,2,1,0:T(8,128)S(1)} %get-tuple-element.12) | copy-start | bytes 12582916
  84.3 23.6 %copy-start.3 = (f32[8,64,256]{2,1,0:T(8,128)S(1)}, f32[8,64,256]{2,1,0:T(8,128)}, u32[]{:S(2)}) copy-start(f32[8,64,256]{2,1,0:T(8,128)} %get-tuple-element.7) | copy-start | bytes 1572868
  84.3 13.2 %collective-permute-start.8 = (f32[9,1,64,256]{3,2,1,0:T(8,128)}, f32[9,1,64,256]{3,2,1,0:T(8,128)S(1)}, u32[]{:S(2)}, u32[]{:S(2)}) collective-permute-start(f32[9,1,64,256]{3,2,1,0:T(8,128)} %get-tuple-element.23), channel_id=1, source_target_pairs={{4,0},{8,4},{12,8},{16,12},{20,16},{24,20},{28,24},{32,28},{36,32}... | collective-permute-start | bytes 1769480 | tf_op jit(solution)/shard_map/ppermute | solution.py:23
  86.4 13.5 %collective-permute-start.9 = (f32[9,1,64,256]{3,2,1,0:T(8,128)}, f32[9,1,64,256]{3,2,1,0:T(8,128)S(1)}, u32[]{:S(2)}, u32[]{:S(2)}) collective-permute-start(f32[9,1,64,256]{3,2,1,0:T(8,128)} %get-tuple-element.22), channel_id=1, source_target_pairs={{0,4},{4,8},{8,12},{12,16},{16,20},{20,24},{24,28},{28,32},{32,36}... | collective-permute-start | bytes 1769480 | tf_op jit(solution)/shard_map/ppermute | solution.py:20
  90.0 18.9 %all-to-all-start.1 = ((f32[32,4,256]{2,1,0:T(4,128)}), f32[32,4,256]{2,1,0:T(4,128)S(1)}, u32[]{:S(2)}, u32[]{:S(2)}) async-start(f32[32,4,256]{2,1,0:T(4,128)} %copy.88), calls=%async_computation.1 | async-start | bytes 262144 | tf_op jit(solution)/shard_map/all_to_all | solution.py:115
  101.3 8.3 %collective-permute-start.10 = (f32[9,10,1,256]{3,1,2,0:T(8,128)S(1)}, f32[9,10,1,256]{3,1,2,0:T(8,128)S(1)}, u32[]{:S(2)}, u32[]{:S(2)}) collective-permute-start(f32[9,10,1,256]{3,1,2,0:T(8,128)S(1)} %copy.80), channel_id=1, source_target_pairs={{1,0},{2,1},{3,2},{5,4},{6,5},{7,6},{9,8},{10,9},{11,10},{13,12},{... | collective-permute-start | bytes 276488 | tf_op jit(solution)/shard_map/ppermute | solution.py:23
  104.4 7.2 %collective-permute-start.11 = (f32[9,10,1,256]{3,1,2,0:T(8,128)}, f32[9,10,1,256]{3,1,2,0:T(8,128)S(1)}, u32[]{:S(2)}, u32[]{:S(2)}) collective-permute-start(f32[9,10,1,256]{3,1,2,0:T(8,128)} %copy.82), channel_id=1, source_target_pairs={{0,1},{1,2},{2,3},{4,5},{5,6},{6,7},{8,9},{9,10},{10,11},{12,13},{... | collective-permute-start | bytes 276488 | tf_op jit(solution)/shard_map/ppermute | solution.py:20
  111.8 10.3 %copy-start.1 = (f32[8,8,64,256]{3,2,1,0:T(8,128)S(1)}, f32[8,8,64,256]{3,2,1,0:T(8,128)}, u32[]{:S(2)}) copy-start(f32[8,8,64,256]{3,2,1,0:T(8,128)} %copy-done) | copy-start | bytes 12582916
  133.6 6.1 %collective-permute-start.12 = (f32[1,64,256]{2,1,0:T(8,128)S(1)}, f32[1,64,256]{2,1,0:T(8,128)S(1)}, u32[]{:S(2)}, u32[]{:S(2)}) collective-permute-start(f32[1,64,256]{2,1,0:T(8,128)S(1)} %get-tuple-element.36), channel_id=1, source_target_pairs={{4,0},{8,4},{12,8},{16,12},{20,16},{24,20},{28,24},{32,28},{36,32}... | collective-permute-start | bytes 196616 | tf_op jit(solution)/shard_map/ppermute | solution.py:23
  135.5 7.7 %collective-permute-start.13 = (f32[1,64,256]{2,1,0:T(8,128)S(1)}, f32[1,64,256]{2,1,0:T(8,128)S(1)}, u32[]{:S(2)}, u32[]{:S(2)}) collective-permute-start(f32[1,64,256]{2,1,0:T(8,128)S(1)} %get-tuple-element.35), channel_id=1, source_target_pairs={{0,4},{4,8},{8,12},{12,16},{16,20},{20,24},{24,28},{28,32},{32,36}... | collective-permute-start | bytes 196616 | tf_op jit(solution)/shard_map/ppermute | solution.py:20
  143.3 10.7 %collective-permute-start.14 = (f32[10,1,256]{2,1,0:T(1,128)S(1)}, f32[10,1,256]{2,1,0:T(1,128)S(1)}, u32[]{:S(2)}, u32[]{:S(2)}) collective-permute-start(f32[10,1,256]{2,1,0:T(1,128)S(1)} %get-tuple-element.32), channel_id=1, source_target_pairs={{1,0},{2,1},{3,2},{5,4},{6,5},{7,6},{9,8},{10,9},{11,10},{13,12},{... | collective-permute-start | bytes 30728 | tf_op jit(solution)/shard_map/ppermute | solution.py:23
  145.4 8.6 %collective-permute-start.15 = (f32[10,1,256]{2,1,0:T(1,128)S(1)}, f32[10,1,256]{2,1,0:T(1,128)S(1)}, u32[]{:S(2)}, u32[]{:S(2)}) collective-permute-start(f32[10,1,256]{2,1,0:T(1,128)S(1)} %get-tuple-element.31), channel_id=1, source_target_pairs={{0,1},{1,2},{2,3},{4,5},{5,6},{6,7},{8,9},{9,10},{10,11},{12,13},{... | collective-permute-start | bytes 30728 | tf_op jit(solution)/shard_map/ppermute | solution.py:20
  149.1 5.4 %copy-start.2 = (f32[8,64,256]{2,1,0:T(8,128)S(1)}, f32[8,64,256]{2,1,0:T(8,128)}, u32[]{:S(2)}) copy-start(f32[8,64,256]{2,1,0:T(8,128)} %get-tuple-element.6) | copy-start | bytes 1572868
where the time goes:
time: 160 us; the launch traced here: 159 us
  other arithmetic  71.8 us (45%)
  starting transfers between devices  59.3 us (37%)
  waiting for transfers between devices  16.3 us (10%)
  local copies, waits for them, and re-layouts  8.04 us (5%)
  matrix products  2.24 us (1%)
    ppermute x8, starting transfers between devices, extended_2(): lax.ppermute(lax.slice_in_dim(block, block.shape[dim] - width, None, axis...  22.7 us
    ppermute x8, starting transfers between devices, extended_2(): lax.ppermute(lax.slice_in_dim(block, 0, width, axis=dim), axis, backward)  22.7 us
    concatenate x7, other arithmetic, extended_2(): block = jnp.concatenate([low, block, high], axis=dim)  17.4 us
    sub x2, other arithmetic, laplace(): return total - 6.0 * shifted(0, 0, 0)  16.6 us
    ppermute x8, waiting for transfers between devices, extended_2(): lax.ppermute(lax.slice_in_dim(block, block.shape[dim] - width, None, axis...  14.5 us
    reduce_sum x1, other arithmetic, pointwise(): coupled = jnp.sum(lam_e * (phases * phases - phases), axis=0)  9.47 us
    all_to_all x1, starting transfers between devices, shards(): lax.all_to_all(send_rows, 'gx', split_axis=0, concat_axis=0, tiled=True)  7.51 us
    all_to_all x1, starting transfers between devices, shards(): lax.all_to_all(labels, 'gx', split_axis=0, concat_axis=0, tiled=True)  6.39 us
  transfers between devices with their start and end apart: 18, of which 6 were waited for; matrix products, arithmetic and copies ran while one was open for 31% of the time, Pallas kernels for 0%

commit v1 on v0

v1 whole, which is shorter than its diff:
```python
import functools

import jax
import jax.numpy as jnp
from jax import lax
from jax.experimental import pallas as pl
from jax.experimental.pallas import tpu as pltpu
from jax.sharding import PartitionSpec as P

DT = 0.05
SLOTS = 8
NF = SLOTS + 1
CX, CY, NZ = 8, 64, 256
LN = 128
HALF = NZ // LN
GRAIN_DEV = 8
PAD = 8
ROWS = CY + 2 * PAD
FACE = (SLOTS + 2) * CY
FACE_ROWS = FACE + 8
SIDE_ROWS = (SLOTS + 2) * CX
F32 = jnp.float32
ANY = pl.BlockSpec(memory_space=pl.ANY)
VM = pl.BlockSpec(memory_space=pltpu.VMEM)
SM = pl.BlockSpec(memory_space=pltpu.SMEM)


def lanes(half):
    return slice(half * LN, (half + 1) * LN)


def z_sum(first, second):
    lane = lax.broadcasted_iota(jnp.int32, first.shape, first.ndim - 1)
    axis = first.ndim - 1
    low, high = lane == 0, lane == LN - 1
    from_low = pltpu.roll(first, 1, axis)
    from_high = pltpu.roll(second, LN - 1, axis)
    left = jnp.where(low, 0.0, from_low), jnp.where(low, from_low, pltpu.roll(second, 1, axis))
    right = jnp.where(high, from_high, pltpu.roll(first, LN - 1, axis)), jnp.where(high, 0.0, from_high)
    return left[0] + right[0], left[1] + right[1]


def start_all(copies):
    for copy in copies:
        copy.start()
    return copies


def wait_all(copies):
    for copy in copies:
        copy.wait()


def local_kernel(with_sums, cos, fld, out, *rest):
    if with_sums:
        sums, value, field, result, potential, sem_c, sem_e, sem_f, sem_o = rest
    else:
        value, field, result, potential, sem_c, sem_e, sem_f, sem_o = rest
        sums = None

    def copy_c(h):
        return pltpu.make_async_copy(
            cos.at[0, :, :, lanes(h)], value.at[0, h, 1 : CX + 1, PAD : PAD + CY, :], sem_c.at[h]
        )

    def copy_e(x, h):
        return pltpu.make_async_copy(
            cos.at[1:NF, x, :, lanes(h)],
            value.at[1:NF, h, x + 1, PAD : PAD + CY, :],
            sem_e.at[x, h],
        )

    def copy_f(x, h):
        return pltpu.make_async_copy(fld.at[:, x, :, lanes(h)], field.at[:, h, x], sem_f.at[x, h])

    def copy_o(x, h):
        return pltpu.make_async_copy(result.at[:, h, x], out.at[:, x, :, lanes(h)], sem_o.at[x, h])

    for h in range(HALF):
        copy_c(h).start()
    for x in range(CX):
        for h in range(HALF):
            copy_e(x, h).start()
            copy_f(x, h).start()

    tile = jnp.zeros((8, LN), F32)
    plane = jnp.zeros((CY, LN), F32)
    for h in range(HALF):
        for ref in [value.at[s] for s in range(NF)] + [potential]:
            ref[h, 0, PAD : PAD + CY, :] = plane
            ref[h, CX + 1, PAD : PAD + CY, :] = plane
            for x in range(1, CX + 1):
                ref[h, x, 0:PAD, :] = tile
                ref[h, x, PAD + CY : ROWS, :] = tile
    if sums is not None:
        sums[...] = jnp.zeros(sums.shape, F32)

    def around(ref, x, row):
        own = [ref[h, x + 1, row : row + 8, :] for h in range(HALF)]
        along_z = z_sum(*own)
        total = [
            (ref[h, x, row : row + 8, :] + ref[h, x + 2, row : row + 8, :])
            + (ref[h, x + 1, row - 1 : row + 7, :] + ref[h, x + 1, row + 1 : row + 9, :])
            + along_z[h]
            for h in range(HALF)
        ]
        return own, total

    for h in range(HALF):
        copy_c(h).wait()

    def potential_plane(x, carry):
        for part in range(CY // 8):
            row = PAD + part * 8
            own, total = around(value.at[0], x, row)
            for h in range(HALF):
                potential[h, x + 1, row : row + 8, :] = DT * total[h] - (6.0 * DT) * own[h]
        return carry

    lax.fori_loop(0, CX, potential_plane, 0)

    for h in range(HALF):
        copy_e(0, h).wait()

    def step_plane(x, carry):
        @pl.when(x < CX - 1)
        def _():
            for h in range(HALF):
                copy_e(x + 1, h).wait()

        for h in range(HALF):
            copy_f(x, h).wait()
        for part in range(CY // 8):
            row = PAD + part * 8
            here = slice(part * 8, part * 8 + 8)
            both = range(HALF)
            square = [None] * HALF
            weighted = [None] * HALF
            curved = [None] * HALF
            for s in range(1, NF):
                for h in both:
                    eta = field[s, h, x, here, :]
                    lam = value[s, h, x + 1, row : row + 8, :]
                    eta_eta = eta * eta
                    lam_eta = lam * eta
                    cubic = lam_eta * eta
                    square[h] = eta_eta if square[h] is None else square[h] + eta_eta
                    weighted[h] = lam_eta if weighted[h] is None else weighted[h] + lam_eta
                    curved[h] = cubic if curved[h] is None else curved[h] + cubic
            mu, mu_total = around(potential, x, row)
            scale, slope, mu_twelve, linear = [], [], [], []
            for h in both:
                density = field[0, h, x, here, :]
                lam_c = value[0, h, x + 1, row : row + 8, :]
                curvature = 34.0 + density * (192.0 * density - 192.0)
                result[0, h, x, here, :] = (
                    lam_c
                    + mu[h] * (curvature + 6.0)
                    - mu_total[h]
                    - (12.0 * DT) * (curved[h] - weighted[h])
                )
                scale.append((1.0 - 18.0 * DT) + (12.0 * DT) * (density - square[h]))
                slope.append((48.0 * DT) - (24.0 * DT) * density)
                mu_twelve.append(12.0 * mu[h])
                linear.append((24.0 * DT) * weighted[h] + mu_twelve[h])
            for s in range(1, NF):
                lam, total = around(value.at[s], x, row)
                for h in both:
                    eta = field[s, h, x, here, :]
                    new = (
                        lam[h] * (scale[h] + slope[h] * eta)
                        + eta * (mu_twelve[h] * eta - linear[h])
                        + DT * total[h]
                    )
                    result[s, h, x, here, :] = new
                    if sums is not None:
                        sums[s - 1, h, here, :] += lam[h] + new
        for h in range(HALF):
            copy_o(x, h).start()
        return carry

    lax.fori_loop(0, CX, step_plane, 0)
    for x in range(CX):
        for h in range(HALF):
            copy_o(x, h).wait()


def local_step(cos, fld, with_sums):
    out_shape = [jax.ShapeDtypeStruct((NF, CX, CY, NZ), F32)]
    out_specs = [ANY]
    if with_sums:
        out_shape.append(jax.ShapeDtypeStruct((SLOTS, HALF, CY, LN), F32))
        out_specs.append(VM)
    return pl.pallas_call(
        functools.partial(local_kernel, with_sums),
        out_shape=out_shape,
        in_specs=[ANY, ANY],
        out_specs=out_specs,
        scratch_shapes=[
            pltpu.VMEM((NF, HALF, CX + 2, ROWS, LN), F32),
            pltpu.VMEM((NF, HALF, CX, CY, LN), F32),
            pltpu.VMEM((NF, HALF, CX, CY, LN), F32),
            pltpu.VMEM((HALF, CX + 2, ROWS, LN), F32),
            pltpu.SemaphoreType.DMA((HALF,)),
            pltpu.SemaphoreType.DMA((CX, HALF)),
            pltpu.SemaphoreType.DMA((CX, HALF)),
            pltpu.SemaphoreType.DMA((CX, HALF)),
        ],
        compiler_params=pltpu.CompilerParams(vmem_limit_bytes=28 << 20),
        cost_estimate=pl.CostEstimate(flops=250 * CX * CY * NZ, bytes_accessed=3 * 4 * NF * CX * CY * NZ, transcendentals=0),
        name="local_step",
    )(cos, fld)


def pack_kernel(place, cos, face_a, face_b, side_a, side_b, tiles, sem_p, sem_t):
    even_x = place[0] == 0
    even_y = place[1] == 0
    out_a = jnp.where(even_x, CX - 1, 0)
    in_a = jnp.where(even_x, CX - 2, 1)
    loads = start_all(
        [
            pltpu.make_async_copy(
                cos.at[:, :, edge * (CY - 8) : edge * (CY - 8) + 8, :], tiles.at[edge], sem_t.at[edge]
            )
            for edge in range(2)
        ]
    )
    copies = []
    for which, face, outer, inner in ((0, face_a, out_a, in_a), (1, face_b, CX - 1 - out_a, CX - 1 - in_a)):
        for h in range(HALF):
            for k in range(SLOTS + 2):
                s = k + 1 if k < SLOTS else 0
                x = inner if k == SLOTS + 1 else outer
                copies.append(
                    pltpu.make_async_copy(
                        cos.at[s, x, :, lanes(h)],
                        face.at[h, k * CY : (k + 1) * CY, :],
                        sem_p.at[which, h, k],
                    )
                )
    start_all(copies)
    wait_all(loads)
    for h in range(HALF):
        for k in range(SLOTS + 2):
            s = k + 1 if k < SLOTS else 0
            depth = 1 if k == SLOTS + 1 else 0
            low = tiles[0, s, :, depth, lanes(h)]
            high = tiles[1, s, :, 7 - depth, lanes(h)]
            side_a[h, k * CX : (k + 1) * CX, :] = jnp.where(even_y, high, low)
            side_b[h, k * CX : (k + 1) * CX, :] = jnp.where(even_y, low, high)
    wait_all(copies)


def pack(place, cos):
    face = jax.ShapeDtypeStruct((HALF, FACE_ROWS, LN), F32)
    side = jax.ShapeDtypeStruct((HALF, SIDE_ROWS, LN), F32)
    return pl.pallas_call(
        pack_kernel,
        out_shape=[face, face, side, side],
        in_specs=[SM, ANY],
        out_specs=[ANY, ANY, VM, VM],
        scratch_shapes=[
            pltpu.VMEM((2, NF, CX, 8, NZ), F32),
            pltpu.SemaphoreType.DMA((2, HALF, SLOTS + 2)),
            pltpu.SemaphoreType.DMA((2,)),
        ],
        compiler_params=pltpu.CompilerParams(vmem_limit_bytes=8 << 20),
        name="pack",
    )(place, cos)


def corner_kernel(place, got_a, got_b, face_a, face_b, out_a, out_b, tiles, sem):
    del face_a, face_b
    even_x = place[0] == 0
    even_y = place[1] == 0
    row = lax.broadcasted_iota(jnp.int32, (8, LN), 0)
    copies = []
    for h in range(HALF):
        here = slice(SLOTS * CX, SLOTS * CX + CX)
        first, second = got_a[h, here, :], got_b[h, here, :]
        low = jnp.where(even_y, second, first)
        high = jnp.where(even_y, first, second)

        def ends(x):
            return jnp.where(row == 0, low[x : x + 1, :], high[x : x + 1, :])

        at_low, at_high = ends(0), ends(CX - 1)
        tiles[0, h] = jnp.where(even_x, at_high, at_low)
        tiles[1, h] = jnp.where(even_x, at_low, at_high)
        for which, out in ((0, out_a), (1, out_b)):
            copies.append(
                pltpu.make_async_copy(tiles.at[which, h], out.at[h, FACE:FACE_ROWS, :], sem.at[which, h])
            )
    start_all(copies)
    wait_all(copies)


def corner(place, got, faces):
    face = jax.ShapeDtypeStruct((HALF, FACE_ROWS, LN), F32)
    return pl.pallas_call(
        corner_kernel,
        out_shape=[face, face],
        in_specs=[SM, VM, VM, ANY, ANY],
        out_specs=[ANY, ANY],
        scratch_shapes=[pltpu.VMEM((2, HALF, 8, LN), F32), pltpu.SemaphoreType.DMA((2, HALF))],
        input_output_aliases={3: 0, 4: 1},
        name="corner",
    )(place, *got, *faces)


def fix_kernel(first_step, place, cos, fld, got_fa, got_fb, got_sa, got_sb, base, *rest):
    if first_step:
        sums_in, out, face_a, face_b, side_a, side_b, sums, work, field, own_c, edge, sem_w, sem_f, sem_c, sem_o = rest
    else:
        out, work, field, own_c, edge, sem_w, sem_f, sem_c, sem_o = rest
        sums = None
    even_x = place[0] == 0
    even_y = place[1] == 0
    del base

    def ring(hbm, vmem, sem, whole):
        parts = []
        count = 0
        for h in range(HALF):
            for x in (0, CX - 1):
                parts.append((hbm.at[:, x, :, lanes(h)], vmem.at[:, h, x], sem.at[count]))
                count += 1
            for y in (0, CY - 8):
                rows = slice(y, y + 8)
                first = 0 if whole else 1
                parts.append(
                    (
                        hbm.at[first:NF, 1 : CX - 1, rows, lanes(h)],
                        vmem.at[first:NF, h, 1 : CX - 1, rows, :],
                        sem.at[count],
                    )
                )
                count += 1
                if not whole:
                    parts.append(
                        (
                            hbm.at[0, 2 : CX - 2, rows, lanes(h)],
                            vmem.at[0, h, 2 : CX - 2, rows, :],
                            sem.at[count],
                        )
                    )
                    count += 1
            if not whole:
                for x in (1, CX - 2):
                    parts.append((hbm.at[0, x, :, lanes(h)], vmem.at[0, h, x], sem.at[count]))
                    count += 1
        return parts

    loads = [pltpu.make_async_copy(a, b, c) for a, b, c in ring(out, work, sem_w, False)]
    loads += [pltpu.make_async_copy(a, b, c) for a, b, c in ring(fld, field, sem_f, True)]
    loads += [
        pltpu.make_async_copy(cos.at[0, :, :, lanes(h)], own_c.at[h], sem_c.at[h]) for h in range(HALF)
    ]
    start_all(loads)
    if first_step:
        sums[...] = sums_in[...]
    wait_all(loads)
    both = range(HALF)

    for x, inner, present in ((0, 1, place[2]), (CX - 1, CX - 2, place[3])):

        def got(h, start, size):
            a = got_fa[h, start : start + size, :]
            b = got_fb[h, start : start + size, :]
            return jnp.where(even_x, b, a) if x == 0 else jnp.where(even_x, a, b)

        exists = present.astype(F32) * DT
        delta = []
        for h in both:
            d = DT * got(h, SLOTS * CY, CY)
            ends = DT * got(h, FACE, 8)
            delta.append(d)
            edge[h, 8 : 8 + CY, :] = d
            edge[h, 7:8, :] = ends[0:1, :]
            edge[h, 8 + CY : 9 + CY, :] = ends[1:2, :]
        along_z = z_sum(*delta)
        twelve = []
        for h in both:
            total = along_z[h] + edge[h, 9 : 9 + CY, :] + edge[h, 7 : 7 + CY, :] - 6.0 * delta[h]
            density = field[0, h, x]
            curvature = 34.0 + density * (192.0 * density - 192.0)
            work[0, h, x] += (
                delta[h] * curvature
                - 2.0 * total
                - DT * got(h, (SLOTS + 1) * CY, CY)
                - exists * own_c[h, x]
            )
            work[0, h, inner] -= delta[h]
            twelve.append(12.0 * delta[h])
        for s in range(1, NF):
            for h in both:
                eta = field[s, h, x]
                change = DT * got(h, (s - 1) * CY, CY) + twelve[h] * (eta * eta - eta)
                work[s, h, x] += change
                if sums is not None:
                    sums[s - 1, h] += change

    row = lax.broadcasted_iota(jnp.int32, (CX, LN), 0)
    for y, inner, present in ((0, 1, place[4]), (CY - 1, CY - 2, place[5])):

        def got(h, start):
            a = got_sa[h, start : start + CX, :]
            b = got_sb[h, start : start + CX, :]
            return jnp.where(even_y, b, a) if y == 0 else jnp.where(even_y, a, b)

        exists = present.astype(F32) * DT
        delta = [DT * got(h, SLOTS * CX) for h in both]
        along_z = z_sum(*delta)
        twelve = []
        for h in both:
            d = delta[h]
            along_x = jnp.where(row == 0, 0.0, pltpu.roll(d, 1, 0)) + jnp.where(
                row == CX - 1, 0.0, pltpu.roll(d, CX - 1, 0)
            )
            total = along_z[h] + along_x - 6.0 * d
            density = field[0, h, :, y, :]
            curvature = 34.0 + density * (192.0 * density - 192.0)
            work[0, h, :, y, :] = work[0, h, :, y, :] + (
                d * curvature
                - 2.0 * total
                - DT * got(h, (SLOTS + 1) * CX)
                - exists * own_c[h, :, y, :]
            )
            work[0, h, :, inner, :] = work[0, h, :, inner, :] - d
            twelve.append(12.0 * d)
        for s in range(1, NF):
            for h in both:
                eta = field[s, h, :, y, :]
                change = DT * got(h, (s - 1) * CX) + twelve[h] * (eta * eta - eta)
                work[s, h, :, y, :] = work[s, h, :, y, :] + change
                if sums is not None:
                    sums[s - 1, h, y : y + 1, :] += jnp.sum(change, axis=0, keepdims=True)

    stores = start_all(
        [pltpu.make_async_copy(b, a, c) for a, b, c in ring(out, work, sem_o, False)]
    )
    if first_step:
        for h in both:
            for k in range(SLOTS + 2):
                s = k + 1 if k < SLOTS else 0
                depth = 1 if k == SLOTS + 1 else 0
                low, high = work[s, h, depth], work[s, h, CX - 1 - depth]
                face_a[h, k * CY : (k + 1) * CY, :] = jnp.where(even_x, high, low)
                face_b[h, k * CY : (k + 1) * CY, :] = jnp.where(even_x, low, high)
                low, high = work[s, h, :, depth, :], work[s, h, :, CY - 1 - depth, :]
                side_a[h, k * CX : (k + 1) * CX, :] = jnp.where(even_y, high, low)
                side_b[h, k * CX : (k + 1) * CX, :] = jnp.where(even_y, low, high)
    wait_all(stores)


def fix(place, cos, fld, got_faces, got_sides, base, sums=None):
    first_step = sums is not None
    face = jax.ShapeDtypeStruct((HALF, FACE_ROWS, LN), F32)
    side = jax.ShapeDtypeStruct((HALF, SIDE_ROWS, LN), F32)
    args = [place, cos, fld, *got_faces, *got_sides, base]
    in_specs = [SM, ANY, ANY, VM, VM, VM, VM, ANY]
    out_shape = [jax.ShapeDtypeStruct(base.shape, F32)]
    out_specs = [ANY]
    if first_step:
        args.append(sums)
        in_specs.append(VM)
        out_shape += [face, face, side, side, jax.ShapeDtypeStruct(sums.shape, F32)]
        out_specs += [VM] * 5
    return pl.pallas_call(
        functools.partial(fix_kernel, first_step),
        out_shape=out_shape,
        in_specs=in_specs,
        out_specs=out_specs,
        scratch_shapes=[
            pltpu.VMEM((NF, HALF, CX, CY, LN), F32),
            pltpu.VMEM((NF, HALF, CX, CY, LN), F32),
            pltpu.VMEM((HALF, CX, CY, LN), F32),
            pltpu.VMEM((HALF, ROWS, LN), F32),
            pltpu.SemaphoreType.DMA((16,)),
            pltpu.SemaphoreType.DMA((8,)),
            pltpu.SemaphoreType.DMA((HALF,)),
            pltpu.SemaphoreType.DMA((16,)),
        ],
        input_output_aliases={7: 0},
        compiler_params=pltpu.CompilerParams(vmem_limit_bytes=20 << 20),
        name="halo_fix",
    )(*args)


def grain_kernel(groups, grains, sums, rows):
    rows[...] = jnp.zeros(rows.shape, F32)
    row = lax.broadcasted_iota(jnp.int32, (GRAIN_DEV, LN), 0)
    for t in range(CY // 8):
        for s in range(SLOTS):
            grain = grains[0, t, s]
            start = pl.multiple_of(grain // (GRAIN_DEV * groups) * GRAIN_DEV, GRAIN_DEV)
            chosen = row == grain % GRAIN_DEV
            for h in range(HALF):
                total = DT * jnp.sum(sums[s, h, t * 8 : t * 8 + 8, :], axis=0, keepdims=True)
                rows[pl.ds(start, GRAIN_DEV), lanes(h)] += jnp.where(chosen, total, 0.0)


def grain_rows(slot_grain, sums, peers, groups):
    return pl.pallas_call(
        functools.partial(grain_kernel, groups),
        out_shape=jax.ShapeDtypeStruct((peers * GRAIN_DEV, NZ), F32),
        in_specs=[SM, VM],
        out_specs=VM,
        name="grain_rows",
    )(slot_grain, sums)


def swaps(axis, count, first, second):
    near = [(i, i ^ 1) for i in range(count)]
    far = [(i, ((i + 1) ^ 1) - 1) for i in range(1, count - 1)]
    return lax.ppermute(first, axis, near), lax.ppermute(second, axis, far)


def shards(n_gx, n_gy, cotangent, fields_one, fields_zero, slot_grain):
    gx, gy = lax.axis_index("gx"), lax.axis_index("gy")
    place = jnp.stack(
        [gx % 2, gy % 2, gx > 0, gx < n_gx - 1, gy > 0, gy < n_gy - 1]
    ).astype(jnp.int32)

    def exchange(faces, sides):
        got_sides = swaps("gy", n_gy, *sides)
        faces = corner(place, got_sides, faces)
        return swaps("gx", n_gx, *faces), got_sides

    face_a, face_b, side_a, side_b = pack(place, cotangent)
    got_faces, got_sides = exchange((face_a, face_b), (side_a, side_b))
    base, sums = local_step(cotangent, fields_one, True)
    costate, face_a, face_b, side_a, side_b, sums = fix(
        place, cotangent, fields_one, got_faces, got_sides, base, sums
    )

    got_faces, got_sides = exchange((face_a, face_b), (side_a, side_b))
    rows = grain_rows(slot_grain, sums, n_gx, n_gy).reshape(n_gx, GRAIN_DEV, NZ)
    got_rows = lax.all_to_all(rows, "gx", split_axis=0, concat_axis=0, tiled=True)
    (base,) = local_step(costate, fields_zero, False)
    (adjoint,) = fix(place, costate, fields_zero, got_faces, got_sides, base)
    grain_grad = jnp.sum(got_rows.reshape(n_gx, GRAIN_DEV, NZ), axis=0)
    return adjoint, grain_grad


def solution(mesh):
    placed = (
        P(None, "gx", "gy", None),
        P(None, "gx", "gy", None),
        P(None, "gx", "gy", None),
        P("gx", "gy", None),
    )
    return jax.shard_map(
        functools.partial(shards, mesh.shape["gx"], mesh.shape["gy"]),
        mesh=mesh,
        in_specs=placed,
        out_specs=(P(None, "gx", "gy", None), P(("gx", "gy"), None)),
        check_vma=False,
    )
```

time: 160 us -> 87.3 us (0.55)
  the two profiles are of different devices: /device:TPU:28 before, /device:TPU:11 now
where the time goes in v1:
time: 87.3 us; the launch traced here: 86.1 us
  Pallas kernels  28.6 us (33%)
  starting transfers between devices  26.2 us (30%)
  local copies, waits for them, and re-layouts  25.8 us (30%)
  waiting for transfers between devices  3.9 us (4%)
  between operations  0.91 us (1%)
    unnamed x52, local copies, waits for them, and re-layouts  25.7 us
    ppermute x8, starting transfers between devices, swaps(): return (lax.ppermute(first, axis, near), lax.ppermute(second, axis, far))  18.1 us
    pallas_call x2, Pallas kernels, local_step(): pl.pallas_call(functools.partial(local_kernel, with_sums), out_shape=out_...  14 us
    all_to_all x1, starting transfers between devices, shards(): lax.all_to_all(rows, 'gx', split_axis=0, concat_axis=0, tiled=True)  8.13 us
    pallas_call x2, Pallas kernels, fix(): pl.pallas_call(functools.partial(fix_kernel, first_step), out_shape=out_s...  7.7 us
    ppermute x8, waiting for transfers between devices, swaps(): return (lax.ppermute(first, axis, near), lax.ppermute(second, axis, far))  3.9 us
    pallas_call x2, Pallas kernels, corner(): pl.pallas_call(corner_kernel, out_shape=[face, face], in_specs=[SM, VM, V...  3.16 us
    pallas_call x1, Pallas kernels, grain_rows(): pl.pallas_call(functools.partial(grain_kernel, groups), out_shape=jax.Sha...  2.22 us
  transfers between devices with their start and end apart: 9, of which 2 were waited for; matrix products, arithmetic and copies ran while one was open for 1% of the time, Pallas kernels for 19%

profile of v1, /device:TPU:11, one launch (start us, length us, event | category | flops | bytes accessed | tf_op | source)
XLA Modules:
  0.0 86.1 jit_solution(14280093126073684304)
XLA Ops:
  0.7 0.1 stack.43.place
  0.7 2.3 %copy-done.3 = f32[9,8,64,256]{3,2,1,0:T(8,128)S(1)} copy-done((f32[9,8,64,256]{3,2,1,0:T(8,128)S(1)}, f32[9,8,64,256]{3,2,1,0:T(8,128)}, u32[]{:S(2)}) %copy-start.3) | copy-done | bytes 4718616
  3.1 1.5 %pack.1 = (f32[2,648,128]{2,1,0:T(8,128)S(1)}, f32[2,648,128]{2,1,0:T(8,128)S(1)}, f32[2,80,128]{2,1,0:T(8,128)S(1)}, f32[2,80,128]{2,1,0:T(8,128)S(1)}) custom-call(s32[6]{0:T(128)S(1)} %stack.43.place, f32[9,8,64,256]{3,2,1,0:T(8,128)S(1)} %copy-done.3), custom_call_target="tpu_custom_call" | custom-call | tf_op jit(solution)/shard_map/pack/pallas_call | solution.py:257
  4.6 0.0 copy-start.12
  4.6 0.8 copy-done.12
  5.4 0.9 copy-done.13
  6.3 0.3 collective-permute-start
  6.5 3.8 %collective-permute-start.1 = (f32[2,80,128]{2,1,0:T(8,128)S(1)}, f32[2,80,128]{2,1,0:T(8,128)S(1)}, u32[]{:S(2)}, u32[]{:S(2)}) collective-permute-start(f32[2,80,128]{2,1,0:T(8,128)S(1)} %get-tuple-element.19), channel_id=1, source_target_pairs={{1,2},{2,1},{5,6},{6,5},{9,10},{10,9},{13,14},{14,13},{17,18},{18,... | collective-permute-start | bytes 245768 | tf_op jit(solution)/shard_map/ppermute | solution.py:516
  10.3 0.0 collective-permute-done.got_a.got_sa
  10.3 1.8 %collective-permute-done.1.got_b.got_sb = f32[2,80,128]{2,1,0:T(8,128)S(1)} collective-permute-done((f32[2,80,128]{2,1,0:T(8,128)S(1)}, f32[2,80,128]{2,1,0:T(8,128)S(1)}, u32[]{:S(2)}, u32[]{:S(2)}) %collective-permute-start.1) | collective-permute-done | bytes 81952 | tf_op jit(solution)/shard_map/ppermute | solution.py:516
  12.1 0.0 copy-done.23
  12.1 0.6 copy-done.21
  12.7 1.6 %corner.2 = (f32[2,648,128]{2,1,0:T(8,128)}, f32[2,648,128]{2,1,0:T(8,128)}) custom-call(s32[6]{0:T(128)} %copy-done.23, f32[2,80,128]{2,1,0:T(8,128)} %copy-done.19, f32[2,80,128]{2,1,0:T(8,128)} %copy-done.21, f32[2,648,128]{2,1,0:T(8,128)} %copy-done.12, f32[2,648,128]{2,1,0:T(8,128)} %copy-done.13), custom_call_target="tpu_custom_call", output_to_operand_aliasing={{0}: (3, {}), {1}: (4, {})} | custom-call | tf_op jit(solution)/shard_map/corner/pallas_call | solution.py:300
  14.3 1.9 %collective-permute-start.2 = (f32[2,648,128]{2,1,0:T(8,128)}, f32[2,648,128]{2,1,0:T(8,128)S(1)}, u32[]{:S(2)}, u32[]{:S(2)}) collective-permute-start(f32[2,648,128]{2,1,0:T(8,128)} %get-tuple-element.22), channel_id=1, source_target_pairs={{0,4},{4,0},{8,12},{12,8},{16,20},{20,16},{24,28},{28,24},{32,36},... | collective-permute-start | bytes 1990664 | tf_op jit(solution)/shard_map/ppermute | solution.py:516
  16.2 3.4 %collective-permute-start.3 = (f32[2,648,128]{2,1,0:T(8,128)}, f32[2,648,128]{2,1,0:T(8,128)S(1)}, u32[]{:S(2)}, u32[]{:S(2)}) collective-permute-start(f32[2,648,128]{2,1,0:T(8,128)} %get-tuple-element.23), channel_id=1, source_target_pairs={{4,8},{8,4},{12,16},{16,12},{20,24},{24,20},{28,32},{32,28},{36,40... | collective-permute-start | bytes 1990664 | tf_op jit(solution)/shard_map/ppermute | solution.py:516
  19.7 0.0 copy-start.4
  19.7 2.3 %copy-done.4 = f32[9,8,64,256]{3,2,1,0:T(8,128)S(1)} copy-done((f32[9,8,64,256]{3,2,1,0:T(8,128)S(1)}, f32[9,8,64,256]{3,2,1,0:T(8,128)}, u32[]{:S(2)}) %copy-start.4) | copy-done | bytes 4718616
  22.0 2.3 %copy-done.8 = f32[9,8,64,256]{3,2,1,0:T(8,128)S(1)} copy-done((f32[9,8,64,256]{3,2,1,0:T(8,128)S(1)}, f32[9,8,64,256]{3,2,1,0:T(8,128)}, u32[]{:S(2)}) %copy-start.8) | copy-done | bytes 4718616
  24.4 7.1 %local_step.2 = (f32[9,8,64,256]{3,2,1,0:T(8,128)S(1)}, f32[8,2,64,128]{3,2,1,0:T(8,128)S(1)}) custom-call(f32[9,8,64,256]{3,2,1,0:T(8,128)S(1)} %copy-done.4, f32[9,8,64,256]{3,2,1,0:T(8,128)S(1)} %copy-done.8), custom_call_target="tpu_custom_call" | custom-call | flops 32768000 | bytes 14155776 | tf_op jit(solution)/shard_map/local_step/pallas_call | solution.py:194
  31.4 0.0 collective-permute-done.2.got_fa
  31.4 0.0 collective-permute-done.3.got_fb
  31.5 0.9 %copy-done.20 = f32[2,80,128]{2,1,0:T(8,128)S(1)} copy-done((f32[2,80,128]{2,1,0:T(8,128)S(1)}, f32[2,80,128]{2,1,0:T(8,128)}, u32[]{:S(2)}) %copy-start.20) | copy-done | bytes 81944
  32.4 0.9 %copy-done.22 = f32[2,80,128]{2,1,0:T(8,128)S(1)} copy-done((f32[2,80,128]{2,1,0:T(8,128)S(1)}, f32[2,80,128]{2,1,0:T(8,128)}, u32[]{:S(2)}) %copy-start.22) | copy-done | bytes 81944
  33.3 3.0 %halo_fix.2 = (f32[9,8,64,256]{3,2,1,0:T(8,128)S(1)}, f32[2,648,128]{2,1,0:T(8,128)S(1)}, f32[2,648,128]{2,1,0:T(8,128)S(1)}, f32[2,80,128]{2,1,0:T(8,128)S(1)},...) custom-call(s32[6]{0:T(128)S(1)} %copy-done.24, ...), custom_call_target="tpu_custom_call", output_to_operand_aliasing={{0}: (7, {})} | custom-call | tf_op jit(solution)/shard_map/halo_fix/pallas_call | solution.py:469
  36.2 2.1 %copy-done = f32[9,8,64,256]{3,2,1,0:T(8,128)} copy-done((f32[9,8,64,256]{3,2,1,0:T(8,128)}, f32[9,8,64,256]{3,2,1,0:T(8,128)S(1)}, u32[]{:S(2)}) %copy-start) | copy-done | bytes 4718616
  38.4 0.9 %copy-done.10 = f32[2,648,128]{2,1,0:T(8,128)} copy-done((f32[2,648,128]{2,1,0:T(8,128)}, f32[2,648,128]{2,1,0:T(8,128)S(1)}, u32[]{:S(2)}) %copy-start.10) | copy-done | bytes 663576
  39.3 0.9 copy-done.11
  40.1 0.8 copy-done.14
  40.9 0.0 collective-permute-start.4
  40.9 3.6 %collective-permute-start.5 = (f32[2,80,128]{2,1,0:T(8,128)S(1)}, f32[2,80,128]{2,1,0:T(8,128)S(1)}, u32[]{:S(2)}, u32[]{:S(2)}) collective-permute-start(f32[2,80,128]{2,1,0:T(8,128)S(1)} %get-tuple-element.28), channel_id=1, source_target_pairs={{1,2},{2,1},{5,6},{6,5},{9,10},{10,9},{13,14},{14,13},{17,18},{18,... | collective-permute-start | bytes 245768 | tf_op jit(solution)/shard_map/ppermute | solution.py:516
  44.5 0.0 collective-permute-done.4.got_a.got_sa
  44.6 2.1 %collective-permute-done.5.got_b.got_sb = f32[2,80,128]{2,1,0:T(8,128)S(1)} collective-permute-done((f32[2,80,128]{2,1,0:T(8,128)S(1)}, f32[2,80,128]{2,1,0:T(8,128)S(1)}, u32[]{:S(2)}, u32[]{:S(2)}) %collective-permute-start.5) | collective-permute-done | bytes 81952 | tf_op jit(solution)/shard_map/ppermute | solution.py:516
  46.7 0.6 copy-done.17
  47.3 1.6 %corner.3 = (f32[2,648,128]{2,1,0:T(8,128)}, f32[2,648,128]{2,1,0:T(8,128)}) custom-call(s32[6]{0:T(128)} %copy-done.23, f32[2,80,128]{2,1,0:T(8,128)} %copy-done.15, f32[2,80,128]{2,1,0:T(8,128)} %copy-done.17, f32[2,648,128]{2,1,0:T(8,128)} %copy-done.10, f32[2,648,128]{2,1,0:T(8,128)} %copy-done.11), custom_call_target="tpu_custom_call", output_to_operand_aliasing={{0}: (3, {}), {1}: (4, {})} | custom-call | tf_op jit(solution)/shard_map/corner/pallas_call | solution.py:300
  48.9 3.1 %collective-permute-start.6 = (f32[2,648,128]{2,1,0:T(8,128)}, f32[2,648,128]{2,1,0:T(8,128)S(1)}, u32[]{:S(2)}, u32[]{:S(2)}) collective-permute-start(f32[2,648,128]{2,1,0:T(8,128)} %get-tuple-element.31), channel_id=1, source_target_pairs={{0,4},{4,0},{8,12},{12,8},{16,20},{20,16},{24,28},{28,24},{32,36},... | collective-permute-start | bytes 1990664 | tf_op jit(solution)/shard_map/ppermute | solution.py:516
  52.0 1.9 %collective-permute-start.7 = (f32[2,648,128]{2,1,0:T(8,128)}, f32[2,648,128]{2,1,0:T(8,128)S(1)}, u32[]{:S(2)}, u32[]{:S(2)}) collective-permute-start(f32[2,648,128]{2,1,0:T(8,128)} %get-tuple-element.32), channel_id=1, source_target_pairs={{4,8},{8,4},{12,16},{16,12},{20,24},{24,20},{28,32},{32,28},{36,40... | collective-permute-start | bytes 1990664 | tf_op jit(solution)/shard_map/ppermute | solution.py:516
  53.9 2.2 %grain_rows.1 = f32[256,256]{1,0:T(8,128)} custom-call(s32[1,8,8]{2,1,0:T(8,128)} %grains.1, f32[8,2,64,128]{3,2,1,0:T(8,128)} %copy-done.14), custom_call_target="tpu_custom_call" | custom-call | tf_op jit(solution)/shard_map/grain_rows/pallas_call | solution.py:504
  56.2 8.1 %all-to-all-start = ((f32[32,8,256]{2,1,0:T(8,128)}), f32[32,8,256]{2,1,0:T(8,128)S(1)}, u32[]{:S(2)}, u32[]{:S(2)}) async-start(f32[32,8,256]{2,1,0:T(8,128)} %bitcast.7), calls=%async_computation | async-start | bytes 524288 | tf_op jit(solution)/shard_map/all_to_all | solution.py:539
  64.3 2.3 %copy-done.1 = f32[9,8,64,256]{3,2,1,0:T(8,128)S(1)} copy-done((f32[9,8,64,256]{3,2,1,0:T(8,128)S(1)}, f32[9,8,64,256]{3,2,1,0:T(8,128)}, u32[]{:S(2)}) %copy-start.1) | copy-done | bytes 4718616
  66.6 2.3 %copy-done.6 = f32[9,8,64,256]{3,2,1,0:T(8,128)S(1)} copy-done((f32[9,8,64,256]{3,2,1,0:T(8,128)S(1)}, f32[9,8,64,256]{3,2,1,0:T(8,128)}, u32[]{:S(2)}) %copy-start.6) | copy-done | bytes 4718616
  69.0 7.0 %local_step.3.base = f32[9,8,64,256]{3,2,1,0:T(8,128)} custom-call(f32[9,8,64,256]{3,2,1,0:T(8,128)S(1)} %copy-done.1, f32[9,8,64,256]{3,2,1,0:T(8,128)S(1)} %copy-done.6), custom_call_target="tpu_custom_call" | custom-call | flops 32768000 | bytes 14155776 | tf_op jit(solution)/shard_map/local_step/pallas_call | solution.py:194
  76.0 0.0 all-to-all-done
  76.0 0.6 reduce_sum.9
  76.6 0.0 collective-permute-done.6.got_fa
  76.6 0.0 collective-permute-done.7.got_fb
  76.7 2.3 %copy-done.2 = f32[9,8,64,256]{3,2,1,0:T(8,128)S(1)} copy-done((f32[9,8,64,256]{3,2,1,0:T(8,128)S(1)}, f32[9,8,64,256]{3,2,1,0:T(8,128)}, u32[]{:S(2)}) %copy-start.2) | copy-done | bytes 4718616
  79.0 2.3 %copy-done.7 = f32[9,8,64,256]{3,2,1,0:T(8,128)S(1)} copy-done((f32[9,8,64,256]{3,2,1,0:T(8,128)S(1)}, f32[9,8,64,256]{3,2,1,0:T(8,128)}, u32[]{:S(2)}) %copy-start.7) | copy-done | bytes 4718616
  81.3 4.7 %halo_fix.3 = f32[9,8,64,256]{3,2,1,0:T(8,128)} custom-call(s32[6]{0:T(128)S(1)} %copy-done.25, f32[9,8,64,256]{3,2,1,0:T(8,128)S(1)} %copy-done.2, f32[9,8,64,256]{3,2,1,0:T(8,128)S(1)} %copy-done.7, f32[2,648,128]{2,1,0:T(8,128)S(1)} %collective-permute-done.6.got_fa, ...), custom_call_target="tpu_custom_call", output_to_operand_aliasing={{}: (7, {})} | custom-call | tf_op jit(solution)/shard_map/halo_fix/pallas_call | solution.py:469
  (32 shorter events, 0.1 us)
Async XLA Ops:
  0.7 2.3 %copy-start.3 = (f32[9,8,64,256]{3,2,1,0:T(8,128)S(1)}, f32[9,8,64,256]{3,2,1,0:T(8,128)}, u32[]{:S(2)}) copy-start(f32[9,8,64,256]{3,2,1,0:T(8,128)} %cos.5) | copy-start | bytes 14155780
  3.1 9.0 %copy-start.23 = (s32[6]{0:T(128)}, s32[6]{0:T(128)S(1)}, u32[]{:S(2)}) copy-start(s32[6]{0:T(128)S(1)} %stack.43.place) | copy-start | bytes 76
  4.6 0.8 copy-start.12
  5.4 0.9 copy-start.13
  6.3 4.0 %collective-permute-start = (f32[2,80,128]{2,1,0:T(8,128)S(1)}, f32[2,80,128]{2,1,0:T(8,128)S(1)}, u32[]{:S(2)}, u32[]{:S(2)}) collective-permute-start(f32[2,80,128]{2,1,0:T(8,128)S(1)} %get-tuple-element.18), channel_id=1, source_target_pairs={{0,1},{1,0},{2,3},{3,2},{4,5},{5,4},{6,7},{7,6},{8,9},{9,8},{10,11... | collective-permute-start | bytes 245768 | tf_op jit(solution)/shard_map/ppermute | solution.py:516
  6.5 5.6 %collective-permute-start.1 = (f32[2,80,128]{2,1,0:T(8,128)S(1)}, f32[2,80,128]{2,1,0:T(8,128)S(1)}, u32[]{:S(2)}, u32[]{:S(2)}) collective-permute-start(f32[2,80,128]{2,1,0:T(8,128)S(1)} %get-tuple-element.19), channel_id=1, source_target_pairs={{1,2},{2,1},{5,6},{6,5},{9,10},{10,9},{13,14},{14,13},{17,18},{18,... | collective-permute-start | bytes 245768 | tf_op jit(solution)/shard_map/ppermute | solution.py:516
  10.3 1.8 %copy-start.19 = (f32[2,80,128]{2,1,0:T(8,128)}, f32[2,80,128]{2,1,0:T(8,128)S(1)}, u32[]{:S(2)}) copy-start(f32[2,80,128]{2,1,0:T(8,128)S(1)} %collective-permute-done.got_a.got_sa) | copy-start | bytes 245764
  12.1 0.6 copy-start.21
  14.3 17.1 %collective-permute-start.2 = (f32[2,648,128]{2,1,0:T(8,128)}, f32[2,648,128]{2,1,0:T(8,128)S(1)}, u32[]{:S(2)}, u32[]{:S(2)}) collective-permute-start(f32[2,648,128]{2,1,0:T(8,128)} %get-tuple-element.22), channel_id=1, source_target_pairs={{0,4},{4,0},{8,12},{12,8},{16,20},{20,16},{24,28},{28,24},{32,36},... | collective-permute-start | bytes 1990664 | tf_op jit(solution)/shard_map/ppermute | solution.py:516
  16.2 15.2 %collective-permute-start.3 = (f32[2,648,128]{2,1,0:T(8,128)}, f32[2,648,128]{2,1,0:T(8,128)S(1)}, u32[]{:S(2)}, u32[]{:S(2)}) collective-permute-start(f32[2,648,128]{2,1,0:T(8,128)} %get-tuple-element.23), channel_id=1, source_target_pairs={{4,8},{8,4},{12,16},{16,12},{20,24},{24,20},{28,32},{32,28},{36,40... | collective-permute-start | bytes 1990664 | tf_op jit(solution)/shard_map/ppermute | solution.py:516
  19.7 2.3 %copy-start.4 = (f32[9,8,64,256]{3,2,1,0:T(8,128)S(1)}, f32[9,8,64,256]{3,2,1,0:T(8,128)}, u32[]{:S(2)}) copy-start(f32[9,8,64,256]{3,2,1,0:T(8,128)} %cos.5) | copy-start | bytes 14155780
  22.0 2.3 %copy-start.8 = (f32[9,8,64,256]{3,2,1,0:T(8,128)S(1)}, f32[9,8,64,256]{3,2,1,0:T(8,128)}, u32[]{:S(2)}) copy-start(f32[9,8,64,256]{3,2,1,0:T(8,128)} %fld.5) | copy-start | bytes 14155780
  24.4 7.1 %copy-start.5 = (f32[9,8,64,256]{3,2,1,0:T(8,128)S(1)}, f32[9,8,64,256]{3,2,1,0:T(8,128)}, u32[]{:S(2)}) copy-start(f32[9,8,64,256]{3,2,1,0:T(8,128)} %cos.5) | copy-start | bytes 14155780
  24.4 7.1 %copy-start.9 = (f32[9,8,64,256]{3,2,1,0:T(8,128)S(1)}, f32[9,8,64,256]{3,2,1,0:T(8,128)}, u32[]{:S(2)}) copy-start(f32[9,8,64,256]{3,2,1,0:T(8,128)} %fld.5) | copy-start | bytes 14155780
  24.4 7.1 %copy-start.24 = (s32[6]{0:T(128)S(1)}, s32[6]{0:T(128)}, u32[]{:S(2)}) copy-start(s32[6]{0:T(128)} %copy-done.23) | copy-start | bytes 76
  31.5 0.9 %copy-start.20 = (f32[2,80,128]{2,1,0:T(8,128)S(1)}, f32[2,80,128]{2,1,0:T(8,128)}, u32[]{:S(2)}) copy-start(f32[2,80,128]{2,1,0:T(8,128)} %copy-done.19) | copy-start | bytes 245764
  32.4 0.9 %copy-start.22 = (f32[2,80,128]{2,1,0:T(8,128)S(1)}, f32[2,80,128]{2,1,0:T(8,128)}, u32[]{:S(2)}) copy-start(f32[2,80,128]{2,1,0:T(8,128)} %copy-done.21) | copy-start | bytes 245764
  36.2 2.2 %copy-start = (f32[9,8,64,256]{3,2,1,0:T(8,128)}, f32[9,8,64,256]{3,2,1,0:T(8,128)S(1)}, u32[]{:S(2)}) copy-start(f32[9,8,64,256]{3,2,1,0:T(8,128)S(1)} %get-tuple-element.26.cos) | copy-start | bytes 14155780
  38.4 0.9 %copy-start.10 = (f32[2,648,128]{2,1,0:T(8,128)}, f32[2,648,128]{2,1,0:T(8,128)S(1)}, u32[]{:S(2)}) copy-start(f32[2,648,128]{2,1,0:T(8,128)S(1)} %get-tuple-element.29.face_a) | copy-start | bytes 1990660
  39.3 0.9 copy-start.11
  40.1 0.8 copy-start.14
  40.9 3.6 %collective-permute-start.4 = (f32[2,80,128]{2,1,0:T(8,128)S(1)}, f32[2,80,128]{2,1,0:T(8,128)S(1)}, u32[]{:S(2)}, u32[]{:S(2)}) collective-permute-start(f32[2,80,128]{2,1,0:T(8,128)S(1)} %get-tuple-element.27), channel_id=1, source_target_pairs={{0,1},{1,0},{2,3},{3,2},{4,5},{5,4},{6,7},{7,6},{8,9},{9,8},{10,11... | collective-permute-start | bytes 245768 | tf_op jit(solution)/shard_map/ppermute | solution.py:516
  40.9 5.7 %collective-permute-start.5 = (f32[2,80,128]{2,1,0:T(8,128)S(1)}, f32[2,80,128]{2,1,0:T(8,128)S(1)}, u32[]{:S(2)}, u32[]{:S(2)}) collective-permute-start(f32[2,80,128]{2,1,0:T(8,128)S(1)} %get-tuple-element.28), channel_id=1, source_target_pairs={{1,2},{2,1},{5,6},{6,5},{9,10},{10,9},{13,14},{14,13},{17,18},{18,... | collective-permute-start | bytes 245768 | tf_op jit(solution)/shard_map/ppermute | solution.py:516
  44.6 2.1 %copy-start.15 = (f32[2,80,128]{2,1,0:T(8,128)}, f32[2,80,128]{2,1,0:T(8,128)S(1)}, u32[]{:S(2)}) copy-start(f32[2,80,128]{2,1,0:T(8,128)S(1)} %collective-permute-done.4.got_a.got_sa) | copy-start | bytes 245764
  46.7 0.6 copy-start.17
  48.9 27.8 %collective-permute-start.6 = (f32[2,648,128]{2,1,0:T(8,128)}, f32[2,648,128]{2,1,0:T(8,128)S(1)}, u32[]{:S(2)}, u32[]{:S(2)}) collective-permute-start(f32[2,648,128]{2,1,0:T(8,128)} %get-tuple-element.31), channel_id=1, source_target_pairs={{0,4},{4,0},{8,12},{12,8},{16,20},{20,16},{24,28},{28,24},{32,36},... | collective-permute-start | bytes 1990664 | tf_op jit(solution)/shard_map/ppermute | solution.py:516
  52.0 24.6 %collective-permute-start.7 = (f32[2,648,128]{2,1,0:T(8,128)}, f32[2,648,128]{2,1,0:T(8,128)S(1)}, u32[]{:S(2)}, u32[]{:S(2)}) collective-permute-start(f32[2,648,128]{2,1,0:T(8,128)} %get-tuple-element.32), channel_id=1, source_target_pairs={{4,8},{8,4},{12,16},{16,12},{20,24},{24,20},{28,32},{32,28},{36,40... | collective-permute-start | bytes 1990664 | tf_op jit(solution)/shard_map/ppermute | solution.py:516
  56.2 19.8 %all-to-all-start = ((f32[32,8,256]{2,1,0:T(8,128)}), f32[32,8,256]{2,1,0:T(8,128)S(1)}, u32[]{:S(2)}, u32[]{:S(2)}) async-start(f32[32,8,256]{2,1,0:T(8,128)} %bitcast.7), calls=%async_computation | async-start | bytes 524288 | tf_op jit(solution)/shard_map/all_to_all | solution.py:539
  64.3 2.3 %copy-start.1 = (f32[9,8,64,256]{3,2,1,0:T(8,128)S(1)}, f32[9,8,64,256]{3,2,1,0:T(8,128)}, u32[]{:S(2)}) copy-start(f32[9,8,64,256]{3,2,1,0:T(8,128)} %copy-done) | copy-start | bytes 14155780
  66.6 2.3 %copy-start.6 = (f32[9,8,64,256]{3,2,1,0:T(8,128)S(1)}, f32[9,8,64,256]{3,2,1,0:T(8,128)}, u32[]{:S(2)}) copy-start(f32[9,8,64,256]{3,2,1,0:T(8,128)} %fld.7) | copy-start | bytes 14155780
  69.0 7.7 %copy-start.16 = (f32[2,80,128]{2,1,0:T(8,128)S(1)}, f32[2,80,128]{2,1,0:T(8,128)}, u32[]{:S(2)}) copy-start(f32[2,80,128]{2,1,0:T(8,128)} %copy-done.15) | copy-start | bytes 245764
  69.0 7.7 %copy-start.18 = (f32[2,80,128]{2,1,0:T(8,128)S(1)}, f32[2,80,128]{2,1,0:T(8,128)}, u32[]{:S(2)}) copy-start(f32[2,80,128]{2,1,0:T(8,128)} %copy-done.17) | copy-start | bytes 245764
  69.0 7.7 %copy-start.25 = (s32[6]{0:T(128)S(1)}, s32[6]{0:T(128)}, u32[]{:S(2)}) copy-start(s32[6]{0:T(128)} %copy-done.23) | copy-start | bytes 76
  76.6 2.3 %copy-start.2 = (f32[9,8,64,256]{3,2,1,0:T(8,128)S(1)}, f32[9,8,64,256]{3,2,1,0:T(8,128)}, u32[]{:S(2)}) copy-start(f32[9,8,64,256]{3,2,1,0:T(8,128)} %copy-done) | copy-start | bytes 14155780
  79.0 2.3 %copy-start.7 = (f32[9,8,64,256]{3,2,1,0:T(8,128)S(1)}, f32[9,8,64,256]{3,2,1,0:T(8,128)}, u32[]{:S(2)}) copy-start(f32[9,8,64,256]{3,2,1,0:T(8,128)} %fld.7) | copy-start | bytes 14155780

commit v2 on v1

v2 whole, which is shorter than its diff:
```python
import functools

import jax
import jax.numpy as jnp
from jax import lax
from jax.experimental import pallas as pl
from jax.experimental.pallas import tpu as pltpu
from jax.sharding import PartitionSpec as P

DT = 0.05
SLOTS = 8
NF = SLOTS + 1
CX, CY, NZ = 8, 64, 256
LN = 128
HALF = NZ // LN
GRAIN_DEV = 8
PAD = 8
ROWS = CY + 2 * PAD
FACE = (SLOTS + 2) * CY
FACE_ROWS = FACE + 8
SIDE_ROWS = (SLOTS + 2) * CX
F32 = jnp.float32
BOTH = range(HALF)
LIMIT = 4 << 20
HBM = pl.BlockSpec(memory_space=pltpu.HBM)
VM = pl.BlockSpec(memory_space=pltpu.VMEM)
SM = pl.BlockSpec(memory_space=pltpu.SMEM)


def lanes(half):
    return slice(half * LN, (half + 1) * LN)


def z_sum(first, second):
    lane = lax.broadcasted_iota(jnp.int32, first.shape, first.ndim - 1)
    axis = first.ndim - 1
    low, high = lane == 0, lane == LN - 1
    from_low = pltpu.roll(first, 1, axis)
    from_high = pltpu.roll(second, LN - 1, axis)
    left = jnp.where(low, 0.0, from_low), jnp.where(low, from_low, pltpu.roll(second, 1, axis))
    right = jnp.where(high, from_high, pltpu.roll(first, LN - 1, axis)), jnp.where(high, 0.0, from_high)
    return left[0] + right[0], left[1] + right[1]


def start_all(copies):
    for copy in copies:
        copy.start()
    return copies


def wait_all(copies):
    for copy in copies:
        copy.wait()


def around(ref, x, row):
    own = [ref[h, x + 1, row : row + 8, :] for h in BOTH]
    along_z = z_sum(*own)
    total = [
        (ref[h, x, row : row + 8, :] + ref[h, x + 2, row : row + 8, :])
        + (ref[h, x + 1, row - 1 : row + 7, :] + ref[h, x + 1, row + 1 : row + 9, :])
        + along_z[h]
        for h in BOTH
    ]
    return own, total


def clear_edges(ref):
    tile = jnp.zeros((8, LN), F32)
    plane = jnp.zeros((CY, LN), F32)
    for h in BOTH:
        ref[h, 0, PAD : PAD + CY, :] = plane
        ref[h, CX + 1, PAD : PAD + CY, :] = plane
        for x in range(1, CX + 1):
            ref[h, x, 0:PAD, :] = tile
            ref[h, x, PAD + CY : ROWS, :] = tile


def local_kernel(with_sums, cos, fld, out, density_value, field, result, *rest):
    if with_sums:
        sums, *rest = rest
    phases, potential, sem_c, sem_e, sem_f, sem_o, sem_d = rest

    def copy_c(h):
        return pltpu.make_async_copy(
            cos.at[0, :, :, lanes(h)],
            density_value.at[h, 1 : CX + 1, PAD : PAD + CY, :],
            sem_c.at[h],
        )

    def copy_e(x, h):
        return pltpu.make_async_copy(
            cos.at[1:NF, x, :, lanes(h)], phases.at[:, h, x + 1, PAD : PAD + CY, :], sem_e.at[x, h]
        )

    def copy_f(x, h):
        return pltpu.make_async_copy(fld.at[:, x, :, lanes(h)], field.at[:, h, x], sem_f.at[x, h])

    inside = slice(8, CY - 8)

    def copy_o(x, h):
        return pltpu.make_async_copy(
            result.at[1:NF, h, x, inside, :], out.at[1:NF, x, inside, lanes(h)], sem_o.at[x, h]
        )

    def copy_d(x, h):
        return pltpu.make_async_copy(
            result.at[0, h, x, inside, :], out.at[0, x, inside, lanes(h)], sem_d.at[x, h]
        )

    for h in BOTH:
        copy_c(h).start()
    for x in range(CX):
        for h in BOTH:
            copy_e(x, h).start()
            copy_f(x, h).start()

    clear_edges(potential)
    clear_edges(density_value)
    for s in range(SLOTS):
        clear_edges(phases.at[s])
    if with_sums:
        sums[...] = jnp.zeros(sums.shape, F32)
    for h in BOTH:
        copy_c(h).wait()

    def potential_plane(x, carry):
        for part in range(CY // 8):
            row = PAD + part * 8
            own, total = around(density_value, x, row)
            for h in BOTH:
                potential[h, x + 1, row : row + 8, :] = DT * total[h] - (6.0 * DT) * own[h]
        return carry

    lax.fori_loop(0, CX, potential_plane, 0)

    for h in BOTH:
        copy_e(0, h).wait()

    def step_plane(x, carry):
        @pl.when(x < CX - 1)
        def _():
            for h in BOTH:
                copy_e(x + 1, h).wait()

        for h in BOTH:
            copy_f(x, h).wait()
        for part in range(CY // 8):
            row = PAD + part * 8
            here = slice(part * 8, part * 8 + 8)
            square = [None] * HALF
            weighted = [None] * HALF
            curved = [None] * HALF
            for s in range(SLOTS):
                for h in BOTH:
                    eta = field[s + 1, h, x, here, :]
                    lam = phases[s, h, x + 1, row : row + 8, :]
                    eta_eta = eta * eta
                    lam_eta = lam * eta
                    cubic = lam_eta * eta
                    square[h] = eta_eta if square[h] is None else square[h] + eta_eta
                    weighted[h] = lam_eta if weighted[h] is None else weighted[h] + lam_eta
                    curved[h] = cubic if curved[h] is None else curved[h] + cubic
            mu, mu_total = around(potential, x, row)
            scale, slope, mu_twelve, linear = [], [], [], []
            for h in BOTH:
                density = field[0, h, x, here, :]
                lam_c = density_value[h, x + 1, row : row + 8, :]
                curvature = 34.0 + density * (192.0 * density - 192.0)
                result[0, h, x, here, :] = (
                    lam_c
                    + mu[h] * (curvature + 6.0)
                    - mu_total[h]
                    - (12.0 * DT) * (curved[h] - weighted[h])
                )
                scale.append((1.0 - 18.0 * DT) + (12.0 * DT) * (density - square[h]))
                slope.append((48.0 * DT) - (24.0 * DT) * density)
                mu_twelve.append(12.0 * mu[h])
                linear.append((24.0 * DT) * weighted[h] + mu_twelve[h])
            for s in range(SLOTS):
                lam, total = around(phases.at[s], x, row)
                for h in BOTH:
                    eta = field[s + 1, h, x, here, :]
                    new = (
                        lam[h] * (scale[h] + slope[h] * eta)
                        + eta * (mu_twelve[h] * eta - linear[h])
                        + DT * total[h]
                    )
                    result[s + 1, h, x, here, :] = new
                    if with_sums:
                        sums[s, h, here, :] += lam[h] + new

        @pl.when((x > 0) & (x < CX - 1))
        def _():
            for h in BOTH:
                copy_o(x, h).start()

        @pl.when((x > 1) & (x < CX - 2))
        def _():
            for h in BOTH:
                copy_d(x, h).start()

        return carry

    lax.fori_loop(0, CX, step_plane, 0)
    for h in BOTH:
        for x in range(1, CX - 1):
            copy_o(x, h).wait()
        for x in range(2, CX - 2):
            copy_d(x, h).wait()


PADDED = jax.ShapeDtypeStruct((HALF, CX + 2, ROWS, LN), F32)
BLOCK = jax.ShapeDtypeStruct((NF, HALF, CX, CY, LN), F32)
SUMS = jax.ShapeDtypeStruct((SLOTS, HALF, CY, LN), F32)
WHOLE = pltpu.HBM((NF, CX, CY, NZ), F32)


def local_step(cos, fld, with_sums):
    extra = [SUMS] if with_sums else []
    return pl.pallas_call(
        functools.partial(local_kernel, with_sums),
        out_shape=[WHOLE, PADDED, BLOCK, BLOCK] + extra,
        in_specs=[HBM, HBM],
        out_specs=[HBM, VM, VM, VM] + [VM] * len(extra),
        scratch_shapes=[
            pltpu.VMEM((SLOTS, HALF, CX + 2, ROWS, LN), F32),
            pltpu.VMEM((HALF, CX + 2, ROWS, LN), F32),
            pltpu.SemaphoreType.DMA((HALF,)),
            pltpu.SemaphoreType.DMA((CX, HALF)),
            pltpu.SemaphoreType.DMA((CX, HALF)),
            pltpu.SemaphoreType.DMA((CX, HALF)),
            pltpu.SemaphoreType.DMA((CX, HALF)),
        ],
        compiler_params=pltpu.CompilerParams(vmem_limit_bytes=12 << 20),
        cost_estimate=pl.CostEstimate(
            flops=250 * CX * CY * NZ, bytes_accessed=3 * 4 * NF * CX * CY * NZ, transcendentals=0
        ),
        name="local_step",
    )(cos, fld)


def pack_kernel(place, cos, face_a, face_b, side_a, side_b, tiles, sem_p, sem_t):
    even_x = place[0] == 0
    even_y = place[1] == 0
    out_a = jnp.where(even_x, CX - 1, 0)
    in_a = jnp.where(even_x, CX - 2, 1)
    loads = start_all(
        [
            pltpu.make_async_copy(
                cos.at[:, :, edge * (CY - 8) : edge * (CY - 8) + 8, :], tiles.at[edge], sem_t.at[edge]
            )
            for edge in range(2)
        ]
    )
    copies = []
    for which, face, outer, inner in ((0, face_a, out_a, in_a), (1, face_b, CX - 1 - out_a, CX - 1 - in_a)):
        for h in range(HALF):
            for k in range(SLOTS + 2):
                s = k + 1 if k < SLOTS else 0
                x = inner if k == SLOTS + 1 else outer
                copies.append(
                    pltpu.make_async_copy(
                        cos.at[s, x, :, lanes(h)],
                        face.at[h, k * CY : (k + 1) * CY, :],
                        sem_p.at[which, h, k],
                    )
                )
    start_all(copies)
    wait_all(loads)
    for h in range(HALF):
        for k in range(SLOTS + 2):
            s = k + 1 if k < SLOTS else 0
            depth = 1 if k == SLOTS + 1 else 0
            low = tiles[0, s, :, depth, lanes(h)]
            high = tiles[1, s, :, 7 - depth, lanes(h)]
            side_a[h, k * CX : (k + 1) * CX, :] = jnp.where(even_y, high, low)
            side_b[h, k * CX : (k + 1) * CX, :] = jnp.where(even_y, low, high)
    wait_all(copies)


def pack(place, cos):
    face = jax.ShapeDtypeStruct((HALF, FACE_ROWS, LN), F32)
    side = jax.ShapeDtypeStruct((HALF, SIDE_ROWS, LN), F32)
    return pl.pallas_call(
        pack_kernel,
        out_shape=[face, face, side, side],
        in_specs=[SM, HBM],
        out_specs=[VM] * 4,
        scratch_shapes=[
            pltpu.VMEM((2, NF, CX, 8, NZ), F32),
            pltpu.SemaphoreType.DMA((2, HALF, SLOTS + 2)),
            pltpu.SemaphoreType.DMA((2,)),
        ],
        compiler_params=pltpu.CompilerParams(vmem_limit_bytes=8 << 20),
        name="pack",
    )(place, cos)


def corner_kernel(place, got_a, got_b, face_a, face_b, out_a, out_b):
    del face_a, face_b
    even_x = place[0] == 0
    even_y = place[1] == 0
    row = lax.broadcasted_iota(jnp.int32, (8, LN), 0)
    for h in BOTH:
        here = slice(SLOTS * CX, SLOTS * CX + CX)
        first, second = got_a[h, here, :], got_b[h, here, :]
        low = jnp.where(even_y, second, first)
        high = jnp.where(even_y, first, second)
        at_low = jnp.where(row == 0, low[0:1, :], high[0:1, :])
        at_high = jnp.where(row == 0, low[CX - 1 : CX, :], high[CX - 1 : CX, :])
        out_a[h, FACE:FACE_ROWS, :] = jnp.where(even_x, at_high, at_low)
        out_b[h, FACE:FACE_ROWS, :] = jnp.where(even_x, at_low, at_high)


FACE_MESSAGE = jax.ShapeDtypeStruct((HALF, FACE_ROWS, LN), F32)
SIDE_MESSAGE = jax.ShapeDtypeStruct((HALF, SIDE_ROWS, LN), F32)


def corner(place, got, faces):
    return pl.pallas_call(
        corner_kernel,
        out_shape=[FACE_MESSAGE] * 2,
        in_specs=[SM] + [VM] * 4,
        out_specs=[VM] * 2,
        input_output_aliases={3: 0, 4: 1},
        compiler_params=pltpu.CompilerParams(vmem_limit_bytes=LIMIT),
        name="corner",
    )(place, *got, *faces)


def fix_kernel(first_step, place, value, field, got_fa, got_fb, got_sa, got_sb, *rest):
    if first_step:
        _, _, _, work, out, sums, face_a, face_b, side_a, side_b, edge, sem = rest
    else:
        _, _, work, out, edge, sem = rest
    even_x = place[0] == 0
    even_y = place[1] == 0
    stores = []

    def store(*where):
        s, x, y = where
        for h in BOTH:
            stores.append(
                pltpu.make_async_copy(work.at[s, h, x, y, :], out.at[s, x, y, lanes(h)], sem.at[len(stores)])
            )
            stores[-1].start()

    row = lax.broadcasted_iota(jnp.int32, (CX, LN), 0)
    for y, inner, present in ((0, 1, place[4]), (CY - 1, CY - 2, place[5])):

        def got(h, start):
            a = got_sa[h, start : start + CX, :]
            b = got_sb[h, start : start + CX, :]
            return jnp.where(even_y, b, a) if y == 0 else jnp.where(even_y, a, b)

        exists = present.astype(F32) * DT
        delta = [DT * got(h, SLOTS * CX) for h in BOTH]
        along_z = z_sum(*delta)
        twelve = []
        for h in BOTH:
            d = delta[h]
            along_x = jnp.where(row == 0, 0.0, pltpu.roll(d, 1, 0)) + jnp.where(
                row == CX - 1, 0.0, pltpu.roll(d, CX - 1, 0)
            )
            total = along_z[h] + along_x - 6.0 * d
            density = field[0, h, :, y, :]
            curvature = 34.0 + density * (192.0 * density - 192.0)
            work[0, h, :, y, :] = work[0, h, :, y, :] + (
                d * curvature
                - 2.0 * total
                - DT * got(h, (SLOTS + 1) * CX)
                - exists * value[h, 1 : CX + 1, PAD + y, :]
            )
            work[0, h, :, inner, :] = work[0, h, :, inner, :] - d
            twelve.append(12.0 * d)
        for s in range(1, NF):
            for h in BOTH:
                eta = field[s, h, :, y, :]
                change = DT * got(h, (s - 1) * CX) + twelve[h] * (eta * eta - eta)
                work[s, h, :, y, :] = work[s, h, :, y, :] + change
                if first_step:
                    sums[s - 1, h, y : y + 1, :] += jnp.sum(change, axis=0, keepdims=True)
        near = slice(0, 8) if y == 0 else slice(CY - 8, CY)
        store(slice(1, NF), slice(1, CX - 1), near)
        store(0, slice(2, CX - 2), near)

    for x, inner, present in ((0, 1, place[2]), (CX - 1, CX - 2, place[3])):

        def got(h, start, size):
            a = got_fa[h, start : start + size, :]
            b = got_fb[h, start : start + size, :]
            return jnp.where(even_x, b, a) if x == 0 else jnp.where(even_x, a, b)

        exists = present.astype(F32) * DT
        delta = []
        for h in BOTH:
            d = DT * got(h, SLOTS * CY, CY)
            ends = DT * got(h, FACE, 8)
            delta.append(d)
            edge[h, 8 : 8 + CY, :] = d
            edge[h, 7:8, :] = ends[0:1, :]
            edge[h, 8 + CY : 9 + CY, :] = ends[1:2, :]
        along_z = z_sum(*delta)
        twelve = []
        for h in BOTH:
            total = along_z[h] + edge[h, 9 : 9 + CY, :] + edge[h, 7 : 7 + CY, :] - 6.0 * delta[h]
            density = field[0, h, x]
            curvature = 34.0 + density * (192.0 * density - 192.0)
            work[0, h, x] += (
                delta[h] * curvature
                - 2.0 * total
                - DT * got(h, (SLOTS + 1) * CY, CY)
                - exists * value[h, x + 1, PAD : PAD + CY, :]
            )
            work[0, h, inner] -= delta[h]
            twelve.append(12.0 * delta[h])
        for s in range(1, NF):
            for h in BOTH:
                eta = field[s, h, x]
                change = DT * got(h, (s - 1) * CY, CY) + twelve[h] * (eta * eta - eta)
                work[s, h, x] += change
                if first_step:
                    sums[s - 1, h] += change
        store(slice(0, NF), x, slice(0, CY))
        store(0, inner, slice(0, CY))

    if first_step:
        for h in BOTH:
            for k in range(SLOTS + 2):
                s = k + 1 if k < SLOTS else 0
                depth = 1 if k == SLOTS + 1 else 0
                low, high = (work[s, h, x] for x in (depth, CX - 1 - depth))
                face_a[h, k * CY : (k + 1) * CY, :] = jnp.where(even_x, high, low)
                face_b[h, k * CY : (k + 1) * CY, :] = jnp.where(even_x, low, high)
                low, high = (work[s, h, :, y, :] for y in (depth, CY - 1 - depth))
                side_a[h, k * CX : (k + 1) * CX, :] = jnp.where(even_y, high, low)
                side_b[h, k * CX : (k + 1) * CX, :] = jnp.where(even_y, low, high)
    wait_all(stores)


def fix(place, value, field, got_faces, got_sides, base, out, sums=None):
    first_step = sums is not None
    args = [place, value, field, *got_faces, *got_sides, base, out]
    in_specs = [SM] + [VM] * 7 + [HBM]
    out_shape, out_specs = [BLOCK, WHOLE], [VM, HBM]
    aliases = {7: 0, 8: 1}
    if first_step:
        args.append(sums)
        in_specs.append(VM)
        out_shape += [SUMS] + [FACE_MESSAGE] * 2 + [SIDE_MESSAGE] * 2
        out_specs += [VM] * 5
        aliases[9] = 2
    return pl.pallas_call(
        functools.partial(fix_kernel, first_step),
        out_shape=out_shape,
        in_specs=in_specs,
        out_specs=out_specs,
        scratch_shapes=[pltpu.VMEM((HALF, ROWS, LN), F32), pltpu.SemaphoreType.DMA((16,))],
        input_output_aliases=aliases,
        compiler_params=pltpu.CompilerParams(vmem_limit_bytes=LIMIT),
        name="fix",
    )(*args)[1:]


def grain_kernel(groups, grains, sums, rows):
    rows[...] = jnp.zeros(rows.shape, F32)
    row = lax.broadcasted_iota(jnp.int32, (GRAIN_DEV, LN), 0)
    for t in range(CY // 8):
        for s in range(SLOTS):
            grain = grains[0, t, s]
            start = pl.multiple_of(grain // (GRAIN_DEV * groups) * GRAIN_DEV, GRAIN_DEV)
            chosen = row == grain % GRAIN_DEV
            for h in range(HALF):
                total = DT * jnp.sum(sums[s, h, t * 8 : t * 8 + 8, :], axis=0, keepdims=True)
                rows[pl.ds(start, GRAIN_DEV), lanes(h)] += jnp.where(chosen, total, 0.0)


def grain_rows(slot_grain, sums, peers, groups):
    return pl.pallas_call(
        functools.partial(grain_kernel, groups),
        out_shape=jax.ShapeDtypeStruct((peers * GRAIN_DEV, NZ), F32),
        in_specs=[SM, VM],
        out_specs=VM,
        compiler_params=pltpu.CompilerParams(vmem_limit_bytes=LIMIT),
        name="grain_rows",
    )(slot_grain, sums)


def swaps(axis, count, first, second):
    near = [(i, i ^ 1) for i in range(count)]
    far = [(i, ((i + 1) ^ 1) - 1) for i in range(1, count - 1)]
    return lax.ppermute(first, axis, near), lax.ppermute(second, axis, far)


def shards(n_gx, n_gy, cotangent, fields_one, fields_zero, slot_grain):
    gx, gy = lax.axis_index("gx"), lax.axis_index("gy")
    cotangent, fields_one, fields_zero = (
        pltpu.with_memory_space_constraint(array, pltpu.HBM)
        for array in (cotangent, fields_one, fields_zero)
    )
    place = jnp.stack(
        [gx % 2, gy % 2, gx > 0, gx < n_gx - 1, gy > 0, gy < n_gy - 1]
    ).astype(jnp.int32)

    def exchange(faces, sides):
        got_sides = swaps("gy", n_gy, *sides)
        faces = corner(place, got_sides, faces)
        return swaps("gx", n_gx, *faces), got_sides

    face_a, face_b, side_a, side_b = pack(place, cotangent)
    got_faces, got_sides = exchange((face_a, face_b), (side_a, side_b))
    out, value, field, base, sums = local_step(cotangent, fields_one, True)
    costate, sums, face_a, face_b, side_a, side_b = fix(
        place, value, field, got_faces, got_sides, base, out, sums
    )

    got_faces, got_sides = exchange((face_a, face_b), (side_a, side_b))
    rows = grain_rows(slot_grain, sums, n_gx, n_gy).reshape(n_gx, GRAIN_DEV, NZ)
    got_rows = lax.all_to_all(rows, "gx", split_axis=0, concat_axis=0, tiled=True)
    costate = pltpu.with_memory_space_constraint(costate, pltpu.HBM)
    out, value, field, base = local_step(costate, fields_zero, False)
    (adjoint,) = fix(place, value, field, got_faces, got_sides, base, out)
    got_rows, adjoint = lax.optimization_barrier((got_rows, adjoint))
    grain_grad = jnp.sum(got_rows.reshape(n_gx, GRAIN_DEV, NZ), axis=0)
    return adjoint, grain_grad


def solution(mesh):
    placed = (
        P(None, "gx", "gy", None),
        P(None, "gx", "gy", None),
        P(None, "gx", "gy", None),
        P("gx", "gy", None),
    )
    return jax.shard_map(
        functools.partial(shards, mesh.shape["gx"], mesh.shape["gy"]),
        mesh=mesh,
        in_specs=placed,
        out_specs=(P(None, "gx", "gy", None), P(("gx", "gy"), None)),
        check_vma=False,
    )
```

time: 87.3 us -> 59.2 us (0.68)
  local copies, waits for them, and re-layouts: 25.8 us -> 0.09 us
  Pallas kernels: 28.6 us -> 25.3 us
  waiting for transfers between devices: 3.9 us -> 5.3 us
    unnamed x52 -> x2, local copies, waits for them, and re-layouts: 25.7 us -> 0.01 us
    pallas_call x2, Pallas kernels: 7.7 us -> 5.11 us  [fix(): pl.pallas_call(functools.partial(fix_kernel, first_step), out_shape=out_s...]
    pallas_call x4, Pallas kernels: 17.2 us -> 15.6 us  [the longest x2 14.5 us: local_step(): pl.pallas_call(functools.partial(local_kernel, with_sums), out_shape=[WHO...]
    ppermute x8, waiting for transfers between devices: 3.9 us -> 5.3 us  [swaps(): return (lax.ppermute(first, axis, near), lax.ppermute(second, axis, far))]
    pallas_call x1, Pallas kernels: 1.46 us -> 2.83 us  [pack(): pl.pallas_call(pack_kernel, out_shape=[face, face, side, side], in_specs=...]
  transfers between devices with their start and end apart: 9 -> 9, of which waited for: 2 -> 3; matrix products, arithmetic and copies ran while one was open for 1% -> 0% of each run, Pallas kernels for 19% -> 32%
where the time goes in v2:
time: 59.2 us; the launch traced here: 58.7 us
  starting transfers between devices  26.6 us (45%)
  Pallas kernels  25.3 us (43%)
  waiting for transfers between devices  5.3 us (9%)
  between operations  0.82 us (1%)
  other arithmetic  0.63 us (1%)
    ppermute x8, starting transfers between devices, swaps(): return (lax.ppermute(first, axis, near), lax.ppermute(second, axis, far))  17.8 us
    pallas_call x2, Pallas kernels, local_step(): pl.pallas_call(functools.partial(local_kernel, with_sums), out_shape=[WHO...  14.5 us
    all_to_all x1, starting transfers between devices, shards(): lax.all_to_all(rows, 'gx', split_axis=0, concat_axis=0, tiled=True)  8.8 us
    ppermute x8, waiting for transfers between devices, swaps(): return (lax.ppermute(first, axis, near), lax.ppermute(second, axis, far))  5.3 us
    pallas_call x2, Pallas kernels, fix(): pl.pallas_call(functools.partial(fix_kernel, first_step), out_shape=out_s...  5.11 us
    pallas_call x1, Pallas kernels, pack(): pl.pallas_call(pack_kernel, out_shape=[face, face, side, side], in_specs=...  2.83 us
    pallas_call x1, Pallas kernels, grain_rows(): pl.pallas_call(functools.partial(grain_kernel, groups), out_shape=jax.Sha...  1.78 us
  transfers between devices with their start and end apart: 9, of which 3 were waited for; matrix products, arithmetic and copies ran while one was open for 0% of the time, Pallas kernels for 32%

profile of v2, /device:TPU:11, one launch (start us, length us, event | category | flops | bytes accessed | tf_op | source)
XLA Modules:
  0.0 58.7 jit_solution(9028961491025338841)
XLA Ops:
  0.7 0.1 stack.43.place
  0.7 2.8 %pack.1 = (f32[2,648,128]{2,1,0:T(8,128)S(1)}, f32[2,648,128]{2,1,0:T(8,128)S(1)}, f32[2,80,128]{2,1,0:T(8,128)S(1)}, f32[2,80,128]{2,1,0:T(8,128)S(1)}) custom-call(s32[6]{0:T(128)S(1)} %stack.43.place, f32[9,8,64,256]{3,2,1,0:T(8,128)} %cos.3), custom_call_target="tpu_custom_call" | custom-call | tf_op jit(solution)/shard_map/pack/pallas_call | solution.py:285
  3.6 0.3 collective-permute-start
  3.9 3.8 %collective-permute-start.1 = (f32[2,80,128]{2,1,0:T(8,128)S(1)}, f32[2,80,128]{2,1,0:T(8,128)S(1)}, u32[]{:S(2)}, u32[]{:S(2)}) collective-permute-start(f32[2,80,128]{2,1,0:T(8,128)S(1)} %get-tuple-element.31), channel_id=1, source_target_pairs={{1,2},{2,1},{5,6},{6,5},{9,10},{10,9},{13,14},{14,13},{17,18},{18,... | collective-permute-start | bytes 245768 | tf_op jit(solution)/shard_map/ppermute | solution.py:493
  7.7 0.0 collective-permute-done.got_a.got_sa
  7.7 1.8 %collective-permute-done.1.got_b.got_sb = f32[2,80,128]{2,1,0:T(8,128)S(1)} collective-permute-done((f32[2,80,128]{2,1,0:T(8,128)S(1)}, f32[2,80,128]{2,1,0:T(8,128)S(1)}, u32[]{:S(2)}, u32[]{:S(2)}) %collective-permute-start.1) | collective-permute-done | bytes 81952 | tf_op jit(solution)/shard_map/ppermute | solution.py:493
  9.5 0.6 corner.2
  10.1 1.9 %collective-permute-start.2 = (f32[2,648,128]{2,1,0:T(8,128)S(1)}, f32[2,648,128]{2,1,0:T(8,128)S(1)}, u32[]{:S(2)}, u32[]{:S(2)}) collective-permute-start(f32[2,648,128]{2,1,0:T(8,128)S(1)} %get-tuple-element.34), channel_id=1, source_target_pairs={{0,4},{4,0},{8,12},{12,8},{16,20},{20,16},{24,28},{28,24},{32,36},... | collective-permute-start | bytes 1990664 | tf_op jit(solution)/shard_map/ppermute | solution.py:493
  12.0 3.4 %collective-permute-start.3 = (f32[2,648,128]{2,1,0:T(8,128)S(1)}, f32[2,648,128]{2,1,0:T(8,128)S(1)}, u32[]{:S(2)}, u32[]{:S(2)}) collective-permute-start(f32[2,648,128]{2,1,0:T(8,128)S(1)} %get-tuple-element.35), channel_id=1, source_target_pairs={{4,8},{8,4},{12,16},{16,12},{20,24},{24,20},{28,32},{32,28},{36,40... | collective-permute-start | bytes 1990664 | tf_op jit(solution)/shard_map/ppermute | solution.py:493
  15.4 7.4 %local_step.2 = (f32[9,8,64,256]{3,2,1,0:T(8,128)}, f32[2,10,80,128]{3,2,1,0:T(8,128)S(1)}, f32[9,2,8,64,128]{4,3,2,1,0:T(8,128)S(1)}, f32[9,2,8,64,128]{4,3,2,1,0:T(8,128)S(1)}, f32[8,2,64,128]{3,2,1,0:T(8,128)S(1)}) custom-call(f32[9,8,64,256]{3,2,1,0:T(8,128)} %cos.3, f32[9,8,64,256]{3,2,1,0:T(8,128)} %fld.2), custom_call_target="tpu_custom_call" | custom-call | flops 32768000 | bytes 14155776 | tf_op jit(solution)/shard_map/local_step/pallas_call | solution.py:221
  22.9 0.0 collective-permute-done.2.got_fa
  22.9 1.4 %collective-permute-done.3.got_fb = f32[2,648,128]{2,1,0:T(8,128)S(1)} collective-permute-done((f32[2,648,128]{2,1,0:T(8,128)S(1)}, f32[2,648,128]{2,1,0:T(8,128)S(1)}, u32[]{:S(2)}, u32[]{:S(2)}) %collective-permute-start.3) | collective-permute-done | bytes 663584 | tf_op jit(solution)/shard_map/ppermute | solution.py:493
  24.2 0.0 copy-start
  24.2 2.5 %fix.2 = (f32[9,2,8,64,128]{4,3,2,1,0:T(8,128)S(1)}, f32[9,8,64,256]{3,2,1,0:T(8,128)}, f32[8,2,64,128]{3,2,1,0:T(8,128)S(1)}, f32[2,648,128]{2,1,0:T(8,128)S(1)...) custom-call(s32[6]{0:T(128)S(1)} %stack.43.place, ...), custom_call_target="tpu_custom_call", output_to_operand_aliasing={{0}: (7, {}), {1}: (8, {}), {2}: (9, {})} | custom-call | tf_op jit(solution)/shard_map/fix/pallas_call | solution.py:454
  26.8 0.1 collective-permute-start.4
  26.9 3.6 %collective-permute-start.5 = (f32[2,80,128]{2,1,0:T(8,128)S(1)}, f32[2,80,128]{2,1,0:T(8,128)S(1)}, u32[]{:S(2)}, u32[]{:S(2)}) collective-permute-start(f32[2,80,128]{2,1,0:T(8,128)S(1)} %get-tuple-element.44), channel_id=1, source_target_pairs={{1,2},{2,1},{5,6},{6,5},{9,10},{10,9},{13,14},{14,13},{17,18},{18,... | collective-permute-start | bytes 245768 | tf_op jit(solution)/shard_map/ppermute | solution.py:493
  30.5 0.0 collective-permute-done.4.got_a.got_sa
  30.5 2.1 %collective-permute-done.5.got_b.got_sb = f32[2,80,128]{2,1,0:T(8,128)S(1)} collective-permute-done((f32[2,80,128]{2,1,0:T(8,128)S(1)}, f32[2,80,128]{2,1,0:T(8,128)S(1)}, u32[]{:S(2)}, u32[]{:S(2)}) %collective-permute-start.5) | collective-permute-done | bytes 81952 | tf_op jit(solution)/shard_map/ppermute | solution.py:493
  32.6 0.6 corner.3
  33.2 2.7 %collective-permute-start.6 = (f32[2,648,128]{2,1,0:T(8,128)S(1)}, f32[2,648,128]{2,1,0:T(8,128)S(1)}, u32[]{:S(2)}, u32[]{:S(2)}) collective-permute-start(f32[2,648,128]{2,1,0:T(8,128)S(1)} %get-tuple-element.47), channel_id=1, source_target_pairs={{0,4},{4,0},{8,12},{12,8},{16,20},{20,16},{24,28},{28,24},{32,36},... | collective-permute-start | bytes 1990664 | tf_op jit(solution)/shard_map/ppermute | solution.py:493
  35.8 1.9 %collective-permute-start.7 = (f32[2,648,128]{2,1,0:T(8,128)S(1)}, f32[2,648,128]{2,1,0:T(8,128)S(1)}, u32[]{:S(2)}, u32[]{:S(2)}) collective-permute-start(f32[2,648,128]{2,1,0:T(8,128)S(1)} %get-tuple-element.48), channel_id=1, source_target_pairs={{4,8},{8,4},{12,16},{16,12},{20,24},{24,20},{28,32},{32,28},{36,40... | collective-permute-start | bytes 1990664 | tf_op jit(solution)/shard_map/ppermute | solution.py:493
  37.8 0.0 copy-done
  37.8 1.8 %grain_rows.1 = f32[256,256]{1,0:T(8,128)} custom-call(s32[1,8,8]{2,1,0:T(8,128)S(1)} %copy-done, f32[8,2,64,128]{3,2,1,0:T(8,128)S(1)} %get-tuple-element.39.sums), custom_call_target="tpu_custom_call" | custom-call | tf_op jit(solution)/shard_map/grain_rows/pallas_call | solution.py:480
  39.6 8.8 %all-to-all-start = ((f32[32,8,256]{2,1,0:T(8,128)}), f32[32,8,256]{2,1,0:T(8,128)S(1)}, u32[]{:S(2)}, u32[]{:S(2)}) async-start(f32[32,8,256]{2,1,0:T(8,128)} %bitcast.6), calls=%async_computation | async-start | bytes 524288 | tf_op jit(solution)/shard_map/all_to_all | solution.py:520
  48.4 7.0 %local_step.3 = (f32[9,8,64,256]{3,2,1,0:T(8,128)}, f32[2,10,80,128]{3,2,1,0:T(8,128)S(1)}, f32[9,2,8,64,128]{4,3,2,1,0:T(8,128)S(1)}, f32[9,2,8,64,128]{4,3,2,1,0:T(8,128)S(1)}) custom-call(f32[9,8,64,256]{3,2,1,0:T(8,128)} %get-tuple-element.40.cos, f32[9,8,64,256]{3,2,1,0:T(8,128)} %fld.3), custom_call_target="tpu_custom_call" | custom-call | flops 32768000 | bytes 14155776 | tf_op jit(solution)/shard_map/local_step/pallas_call | solution.py:221
  55.4 0.0 collective-permute-done.6.got_fa
  55.4 0.0 collective-permute-done.7.got_fb
  55.4 2.6 %fix.3 = (f32[9,2,8,64,128]{4,3,2,1,0:T(8,128)S(1)}, f32[9,8,64,256]{3,2,1,0:T(8,128)}) custom-call(s32[6]{0:T(128)S(1)} %stack.43.place, f32[2,10,80,128]{3,2,1,0:T(8,128)S(1)} %get-tuple-element.41.value, f32[9,2,8,64,128]{4,3,2,1,0:T(8,128)S(1)} %get-tuple-element.42.field, ...), custom_call_target="tpu_custom_call", output_to_operand_aliasing={{0}: (7, {}), {1}: (8, {})} | custom-call | tf_op jit(solution)/shard_map/fix/pallas_call | solution.py:454
  58.0 0.0 all-to-all-done
  58.0 0.6 %reduce_sum.9 = f32[8,256]{1,0:T(8,128)} reduce(f32[32,8,256]{2,1,0:T(8,128)S(1)} %all-to-all-done, f32[]{:T(128)} %constant.32.clone.1), dimensions={0}, to_apply=%region_0.1 | reduce | flops 63488 | bytes 270340 | tf_op jit(solution)/shard_map/reduce_sum | solution.py:525
Async XLA Ops:
  3.6 4.1 %collective-permute-start = (f32[2,80,128]{2,1,0:T(8,128)S(1)}, f32[2,80,128]{2,1,0:T(8,128)S(1)}, u32[]{:S(2)}, u32[]{:S(2)}) collective-permute-start(f32[2,80,128]{2,1,0:T(8,128)S(1)} %get-tuple-element.30), channel_id=1, source_target_pairs={{0,1},{1,0},{2,3},{3,2},{4,5},{5,4},{6,7},{7,6},{8,9},{9,8},{10,11... | collective-permute-start | bytes 245768 | tf_op jit(solution)/shard_map/ppermute | solution.py:493
  3.9 5.6 %collective-permute-start.1 = (f32[2,80,128]{2,1,0:T(8,128)S(1)}, f32[2,80,128]{2,1,0:T(8,128)S(1)}, u32[]{:S(2)}, u32[]{:S(2)}) collective-permute-start(f32[2,80,128]{2,1,0:T(8,128)S(1)} %get-tuple-element.31), channel_id=1, source_target_pairs={{1,2},{2,1},{5,6},{6,5},{9,10},{10,9},{13,14},{14,13},{17,18},{18,... | collective-permute-start | bytes 245768 | tf_op jit(solution)/shard_map/ppermute | solution.py:493
  10.1 12.8 %collective-permute-start.2 = (f32[2,648,128]{2,1,0:T(8,128)S(1)}, f32[2,648,128]{2,1,0:T(8,128)S(1)}, u32[]{:S(2)}, u32[]{:S(2)}) collective-permute-start(f32[2,648,128]{2,1,0:T(8,128)S(1)} %get-tuple-element.34), channel_id=1, source_target_pairs={{0,4},{4,0},{8,12},{12,8},{16,20},{20,16},{24,28},{28,24},{32,36},... | collective-permute-start | bytes 1990664 | tf_op jit(solution)/shard_map/ppermute | solution.py:493
  12.0 12.3 %collective-permute-start.3 = (f32[2,648,128]{2,1,0:T(8,128)S(1)}, f32[2,648,128]{2,1,0:T(8,128)S(1)}, u32[]{:S(2)}, u32[]{:S(2)}) collective-permute-start(f32[2,648,128]{2,1,0:T(8,128)S(1)} %get-tuple-element.35), channel_id=1, source_target_pairs={{4,8},{8,4},{12,16},{16,12},{20,24},{24,20},{28,32},{32,28},{36,40... | collective-permute-start | bytes 1990664 | tf_op jit(solution)/shard_map/ppermute | solution.py:493
  24.2 13.5 %copy-start = (s32[1,8,8]{2,1,0:T(8,128)S(1)}, s32[1,8,8]{2,1,0:T(8,128)}, u32[]{:S(2)}) copy-start(s32[1,8,8]{2,1,0:T(8,128)} %grains.1) | copy-start | bytes 772
  26.8 3.7 %collective-permute-start.4 = (f32[2,80,128]{2,1,0:T(8,128)S(1)}, f32[2,80,128]{2,1,0:T(8,128)S(1)}, u32[]{:S(2)}, u32[]{:S(2)}) collective-permute-start(f32[2,80,128]{2,1,0:T(8,128)S(1)} %get-tuple-element.43), channel_id=1, source_target_pairs={{0,1},{1,0},{2,3},{3,2},{4,5},{5,4},{6,7},{7,6},{8,9},{9,8},{10,11... | collective-permute-start | bytes 245768 | tf_op jit(solution)/shard_map/ppermute | solution.py:493
  26.9 5.8 %collective-permute-start.5 = (f32[2,80,128]{2,1,0:T(8,128)S(1)}, f32[2,80,128]{2,1,0:T(8,128)S(1)}, u32[]{:S(2)}, u32[]{:S(2)}) collective-permute-start(f32[2,80,128]{2,1,0:T(8,128)S(1)} %get-tuple-element.44), channel_id=1, source_target_pairs={{1,2},{2,1},{5,6},{6,5},{9,10},{10,9},{13,14},{14,13},{17,18},{18,... | collective-permute-start | bytes 245768 | tf_op jit(solution)/shard_map/ppermute | solution.py:493
  33.2 22.2 %collective-permute-start.6 = (f32[2,648,128]{2,1,0:T(8,128)S(1)}, f32[2,648,128]{2,1,0:T(8,128)S(1)}, u32[]{:S(2)}, u32[]{:S(2)}) collective-permute-start(f32[2,648,128]{2,1,0:T(8,128)S(1)} %get-tuple-element.47), channel_id=1, source_target_pairs={{0,4},{4,0},{8,12},{12,8},{16,20},{20,16},{24,28},{28,24},{32,36},... | collective-permute-start | bytes 1990664 | tf_op jit(solution)/shard_map/ppermute | solution.py:493
  35.8 19.6 %collective-permute-start.7 = (f32[2,648,128]{2,1,0:T(8,128)S(1)}, f32[2,648,128]{2,1,0:T(8,128)S(1)}, u32[]{:S(2)}, u32[]{:S(2)}) collective-permute-start(f32[2,648,128]{2,1,0:T(8,128)S(1)} %get-tuple-element.48), channel_id=1, source_target_pairs={{4,8},{8,4},{12,16},{16,12},{20,24},{24,20},{28,32},{32,28},{36,40... | collective-permute-start | bytes 1990664 | tf_op jit(solution)/shard_map/ppermute | solution.py:493
  39.6 18.5 %all-to-all-start = ((f32[32,8,256]{2,1,0:T(8,128)}), f32[32,8,256]{2,1,0:T(8,128)S(1)}, u32[]{:S(2)}, u32[]{:S(2)}) async-start(f32[32,8,256]{2,1,0:T(8,128)} %bitcast.6), calls=%async_computation | async-start | bytes 524288 | tf_op jit(solution)/shard_map/all_to_all | solution.py:520

commit v3 on v2

--- a/solution.py
+++ b/solution.py
@@ -17,8 +17,8 @@
 PAD = 8
 ROWS = CY + 2 * PAD
 FACE = (SLOTS + 2) * CY
-FACE_ROWS = FACE + 8
-SIDE_ROWS = (SLOTS + 2) * CX
+SIDE = (SLOTS + 2) * CX
+EXTRA = 8
 F32 = jnp.float32
 BOTH = range(HALF)
 LIMIT = 4 << 20
@@ -76,9 +76,11 @@
             ref[h, x, PAD + CY : ROWS, :] = tile
 
 
-def local_kernel(with_sums, cos, fld, out, density_value, field, result, *rest):
+def local_kernel(with_sums, cos, fld, *rest):
     if with_sums:
-        sums, *rest = rest
+        out, density_value, field, result, sums, *rest = rest
+    else:
+        corners, out, density_value, field, result, *rest = rest
     phases, potential, sem_c, sem_e, sem_f, sem_o, sem_d = rest
 
     def copy_c(h):
@@ -123,6 +125,10 @@
         sums[...] = jnp.zeros(sums.shape, F32)
     for h in BOTH:
         copy_c(h).wait()
+        if not with_sums:
+            for edge, y in ((0, PAD), (8, PAD + CY - 1)):
+                for k, x in ((0, 1), (1, CX)):
+                    density_value[h, x, y : y + 1, :] += corners[h, edge + k : edge + k + 1, :]
 
     def potential_plane(x, carry):
         for part in range(CY // 8):
@@ -216,12 +222,14 @@
 WHOLE = pltpu.HBM((NF, CX, CY, NZ), F32)
 
 
-def local_step(cos, fld, with_sums):
+def local_step(cos, fld, corners=None):
+    with_sums = corners is None
     extra = [SUMS] if with_sums else []
+    more = [] if with_sums else [corners]
     return pl.pallas_call(
         functools.partial(local_kernel, with_sums),
         out_shape=[WHOLE, PADDED, BLOCK, BLOCK] + extra,
-        in_specs=[HBM, HBM],
+        in_specs=[HBM, HBM] + [VM] * len(more),
         out_specs=[HBM, VM, VM, VM] + [VM] * len(extra),
         scratch_shapes=[
             pltpu.VMEM((SLOTS, HALF, CX + 2, ROWS, LN), F32),
@@ -237,7 +245,7 @@
             flops=250 * CX * CY * NZ, bytes_accessed=3 * 4 * NF * CX * CY * NZ, transcendentals=0
         ),
         name="local_step",
-    )(cos, fld)
+    )(cos, fld, *more)
 
 
 def pack_kernel(place, cos, face_a, face_b, side_a, side_b, tiles, sem_p, sem_t):
@@ -255,17 +263,16 @@
     )
     copies = []
     for which, face, outer, inner in ((0, face_a, out_a, in_a), (1, face_b, CX - 1 - out_a, CX - 1 - in_a)):
-        for h in range(HALF):
-            for k in range(SLOTS + 2):
-                s = k + 1 if k < SLOTS else 0
-                x = inner if k == SLOTS + 1 else outer
-                copies.append(
-                    pltpu.make_async_copy(
-                        cos.at[s, x, :, lanes(h)],
-                        face.at[h, k * CY : (k + 1) * CY, :],
-                        sem_p.at[which, h, k],
-                    )
-                )
+        for h in BOTH:
+            phases = face.at[h, 0 : SLOTS * CY, :].reshape(SLOTS, CY, LN)
+            parts = (
+                (cos.at[1:NF, outer, :, lanes(h)], phases),
+                (cos.at[0, outer, :, lanes(h)], face.at[h, SLOTS * CY : SLOTS * CY + CY, :]),
+                (cos.at[0, inner, :, lanes(h)], face.at[h, SLOTS * CY + CY : FACE, :]),
+            )
+            copies += [
+                pltpu.make_async_copy(*part, sem_p.at[which, h, k]) for k, part in enumerate(parts)
+            ]
     start_all(copies)
     wait_all(loads)
     for h in range(HALF):
@@ -279,17 +286,23 @@
     wait_all(copies)
 
 
+def face_message(extra):
+    return jax.ShapeDtypeStruct((HALF, FACE + extra, LN), F32)
+
+
+def side_message(extra):
+    return jax.ShapeDtypeStruct((HALF, SIDE + extra, LN), F32)
+
+
 def pack(place, cos):
-    face = jax.ShapeDtypeStruct((HALF, FACE_ROWS, LN), F32)
-    side = jax.ShapeDtypeStruct((HALF, SIDE_ROWS, LN), F32)
     return pl.pallas_call(
         pack_kernel,
-        out_shape=[face, face, side, side],
+        out_shape=[face_message(0)] * 2 + [side_message(0)] * 2,
         in_specs=[SM, HBM],
         out_specs=[VM] * 4,
         scratch_shapes=[
             pltpu.VMEM((2, NF, CX, 8, NZ), F32),
-            pltpu.SemaphoreType.DMA((2, HALF, SLOTS + 2)),
+            pltpu.SemaphoreType.DMA((2, HALF, 3)),
             pltpu.SemaphoreType.DMA((2,)),
         ],
         compiler_params=pltpu.CompilerParams(vmem_limit_bytes=8 << 20),
@@ -297,36 +310,58 @@
     )(place, cos)
 
 
-def corner_kernel(place, got_a, got_b, face_a, face_b, out_a, out_b):
-    del face_a, face_b
+def corner_kernel(place, first_a, first_b, order, got_a, got_b, face_a, face_b, *rest):
+    del order, got_a, got_b, face_a, face_b
+    side_a, side_b, out_a, out_b, corners = rest
     even_x = place[0] == 0
     even_y = place[1] == 0
-    row = lax.broadcasted_iota(jnp.int32, (8, LN), 0)
+    row = lax.broadcasted_iota(jnp.int32, (CX, LN), 0)
+    face = slice(SLOTS * CX, SLOTS * CX + CX)
+    start = SLOTS * CY
     for h in BOTH:
-        here = slice(SLOTS * CX, SLOTS * CX + CX)
-        first, second = got_a[h, here, :], got_b[h, here, :]
-        low = jnp.where(even_y, second, first)
-        high = jnp.where(even_y, first, second)
+        ends_a = first_a[h, start : start + 1, :], first_a[h, start + CY - 1 : start + CY, :]
+        ends_b = first_b[h, start : start + 1, :], first_b[h, start + CY - 1 : start + CY, :]
+        fixed = []
+        for ref, low_side in ((side_a, ~even_y), (side_b, even_y)):
+            end_a = jnp.where(low_side, ends_a[0], ends_a[1])
+            end_b = jnp.where(low_side, ends_b[0], ends_b[1])
+            at_low = jnp.where(even_x, end_b, end_a)
+            at_high = jnp.where(even_x, end_a, end_b)
+            term = jnp.where(row == 0, at_low, jnp.where(row == CX - 1, at_high, 0.0))
+            exists = jnp.where(low_side, place[4], place[5]).astype(F32)
+            value = ref[h, face, :] - (2.0 * DT * exists) * term
+            ref[h, face, :] = value
+            fixed.append(value)
+        low = jnp.where(even_y, fixed[1], fixed[0])
+        high = jnp.where(even_y, fixed[0], fixed[1])
+        beyond_a, beyond_b = side_a[h, SIDE : SIDE + 8, :], side_b[h, SIDE : SIDE + 8, :]
+        beyond_low = (-2.0 * DT) * jnp.where(even_y, beyond_b, beyond_a)
+        beyond_high = (-2.0 * DT) * jnp.where(even_y, beyond_a, beyond_b)
+        corners[h, 0:8, :] = beyond_low
+        corners[h, 8:16, :] = beyond_high
         at_low = jnp.where(row == 0, low[0:1, :], high[0:1, :])
         at_high = jnp.where(row == 0, low[CX - 1 : CX, :], high[CX - 1 : CX, :])
-        out_a[h, FACE:FACE_ROWS, :] = jnp.where(even_x, at_high, at_low)
-        out_b[h, FACE:FACE_ROWS, :] = jnp.where(even_x, at_low, at_high)
-
-
-FACE_MESSAGE = jax.ShapeDtypeStruct((HALF, FACE_ROWS, LN), F32)
-SIDE_MESSAGE = jax.ShapeDtypeStruct((HALF, SIDE_ROWS, LN), F32)
-
-
-def corner(place, got, faces):
+        for ref, high_face in ((out_a, even_x), (out_b, ~even_x)):
+            ref[h, FACE : FACE + 8, :] = jnp.where(high_face, at_high, at_low)
+            ref[h, start : start + 1, :] += jnp.where(high_face, beyond_low[1:2, :], beyond_low[0:1, :])
+            ref[h, start + CY - 1 : start + CY, :] += jnp.where(
+                high_face, beyond_high[1:2, :], beyond_high[0:1, :]
+            )
+
+
+CORNERS = jax.ShapeDtypeStruct((HALF, 16, LN), F32)
+
+
+def corner(place, first, order, got, faces):
     return pl.pallas_call(
         corner_kernel,
-        out_shape=[FACE_MESSAGE] * 2,
-        in_specs=[SM] + [VM] * 4,
-        out_specs=[VM] * 2,
-        input_output_aliases={3: 0, 4: 1},
+        out_shape=[side_message(EXTRA)] * 2 + [face_message(EXTRA)] * 2 + [CORNERS],
+        in_specs=[SM, VM, VM, HBM] + [VM] * 4,
+        out_specs=[VM] * 5,
+        input_output_aliases={4: 0, 5: 1, 6: 2, 7: 3},
         compiler_params=pltpu.CompilerParams(vmem_limit_bytes=LIMIT),
         name="corner",
-    )(place, *got, *faces)
+    )(place, *first, order, *got, *faces)
 
 
 def fix_kernel(first_step, place, value, field, got_fa, got_fb, got_sa, got_sb, *rest):
@@ -396,11 +431,15 @@
         delta = []
         for h in BOTH:
             d = DT * got(h, SLOTS * CY, CY)
-            ends = DT * got(h, FACE, 8)
             delta.append(d)
             edge[h, 8 : 8 + CY, :] = d
-            edge[h, 7:8, :] = ends[0:1, :]
-            edge[h, 8 + CY : 9 + CY, :] = ends[1:2, :]
+            if first_step:
+                edge[h, 0:8, :] = jnp.zeros((8, LN), F32)
+                edge[h, 8 + CY : 16 + CY, :] = jnp.zeros((8, LN), F32)
+            else:
+                ends = DT * got(h, FACE, 8)
+                edge[h, 7:8, :] = ends[0:1, :]
+                edge[h, 8 + CY : 9 + CY, :] = ends[1:2, :]
         along_z = z_sum(*delta)
         twelve = []
         for h in BOTH:
@@ -436,6 +475,14 @@
                 low, high = (work[s, h, :, y, :] for y in (depth, CY - 1 - depth))
                 side_a[h, k * CX : (k + 1) * CX, :] = jnp.where(even_y, high, low)
                 side_b[h, k * CX : (k + 1) * CX, :] = jnp.where(even_y, low, high)
+            start = SLOTS * CY
+            ends = []
+            for at in (start, start + CY - 1):
+                a, b = got_fa[h, at : at + 1, :], got_fb[h, at : at + 1, :]
+                at_low, at_high = jnp.where(even_x, b, a), jnp.where(even_x, a, b)
+                ends.append(jnp.where(row == 0, at_low, at_high))
+            side_a[h, SIDE : SIDE + 8, :] = jnp.where(even_y, ends[1], ends[0])
+            side_b[h, SIDE : SIDE + 8, :] = jnp.where(even_y, ends[0], ends[1])
     wait_all(stores)
 
 
@@ -448,7 +495,7 @@
     if first_step:
         args.append(sums)
         in_specs.append(VM)
-        out_shape += [SUMS] + [FACE_MESSAGE] * 2 + [SIDE_MESSAGE] * 2
+        out_shape += [SUMS] + [face_message(EXTRA)] * 2 + [side_message(EXTRA)] * 2
         out_specs += [VM] * 5
         aliases[9] = 2
     return pl.pallas_call(
@@ -503,24 +550,26 @@
         [gx % 2, gy % 2, gx > 0, gx < n_gx - 1, gy > 0, gy < n_gy - 1]
     ).astype(jnp.int32)
 
-    def exchange(faces, sides):
-        got_sides = swaps("gy", n_gy, *sides)
-        faces = corner(place, got_sides, faces)
-        return swaps("gx", n_gx, *faces), got_sides
-
     face_a, face_b, side_a, side_b = pack(place, cotangent)
-    got_faces, got_sides = exchange((face_a, face_b), (side_a, side_b))
-    out, value, field, base, sums = local_step(cotangent, fields_one, True)
+    first_faces = swaps("gx", n_gx, face_a, face_b)
+    got_sides = swaps("gy", n_gy, side_a, side_b)
+    out, value, field, base, sums = local_step(cotangent, fields_one)
     costate, sums, face_a, face_b, side_a, side_b = fix(
-        place, value, field, got_faces, got_sides, base, out, sums
-    )
-
-    got_faces, got_sides = exchange((face_a, face_b), (side_a, side_b))
-    rows = grain_rows(slot_grain, sums, n_gx, n_gy).reshape(n_gx, GRAIN_DEV, NZ)
-    got_rows = lax.all_to_all(rows, "gx", split_axis=0, concat_axis=0, tiled=True)
+        place, value, field, first_faces, got_sides, base, out, sums
+    )
+
+    got_sides = swaps("gy", n_gy, side_a, side_b)
+    rows = grain_rows(slot_grain, sums, n_gx, n_gy)
+    side_a, side_b, face_a, face_b, corners = corner(
+        place, first_faces, rows, got_sides, (face_a, face_b)
+    )
+    got_faces = swaps("gx", n_gx, face_a, face_b)
+    got_rows = lax.all_to_all(
+        rows.reshape(n_gx, GRAIN_DEV, NZ), "gx", split_axis=0, concat_axis=0, tiled=True
+    )
     costate = pltpu.with_memory_space_constraint(costate, pltpu.HBM)
-    out, value, field, base = local_step(costate, fields_zero, False)
-    (adjoint,) = fix(place, value, field, got_faces, got_sides, base, out)
+    out, value, field, base = local_step(costate, fields_zero, corners)
+    (adjoint,) = fix(place, value, field, got_faces, (side_a, side_b), base, out)
     got_rows, adjoint = lax.optimization_barrier((got_rows, adjoint))
     grain_grad = jnp.sum(got_rows.reshape(n_gx, GRAIN_DEV, NZ), axis=0)
     return adjoint, grain_grad

time: 59.2 us -> 52.3 us (0.88)
  waiting for transfers between devices: 5.3 us -> 1.57 us
  starting transfers between devices: 26.6 us -> 24.6 us
  Pallas kernels: 25.3 us -> 24.2 us
    ppermute x8, waiting for transfers between devices: 5.3 us -> 1.57 us  [swaps(): return (lax.ppermute(first, axis, near), lax.ppermute(second, axis, far))]
    ppermute x8, starting transfers between devices: 17.8 us -> 16.5 us  [swaps(): return (lax.ppermute(first, axis, near), lax.ppermute(second, axis, far))]
    pallas_call x3 -> x2, Pallas kernels: 3.93 us -> 2.89 us  [the longest x1 2.33 us: pack(): pl.pallas_call(pack_kernel, out_shape=[face_message(0)] * 2 + [side_messa...]
    all_to_all x1, starting transfers between devices: 8.8 us -> 8.14 us  [shards(): lax.all_to_all(rows.reshape(n_gx, GRAIN_DEV, NZ), 'gx', split_axis=0, con...]
  transfers between devices with their start and end apart: 9 -> 9, of which waited for: 3 -> 1; matrix products, arithmetic and copies ran while one was open for 0% -> 0% of each run, Pallas kernels for 32% -> 36%
where the time goes in v3:
time: 52.3 us; the launch traced here: 52 us
  starting transfers between devices  24.6 us (47%)
  Pallas kernels  24.2 us (46%)
  waiting for transfers between devices  1.57 us (3%)
  between operations  0.83 us (2%)
  other arithmetic  0.63 us (1%)
    ppermute x8, starting transfers between devices, swaps(): return (lax.ppermute(first, axis, near), lax.ppermute(second, axis, far))  16.5 us
    pallas_call x2, Pallas kernels, local_step(): pl.pallas_call(functools.partial(local_kernel, with_sums), out_shape=[WHO...  14.5 us
    all_to_all x1, starting transfers between devices, shards(): lax.all_to_all(rows.reshape(n_gx, GRAIN_DEV, NZ), 'gx', split_axis=0, con...  8.14 us
    pallas_call x2, Pallas kernels, fix(): pl.pallas_call(functools.partial(fix_kernel, first_step), out_shape=out_s...  5.09 us
    pallas_call x1, Pallas kernels, pack(): pl.pallas_call(pack_kernel, out_shape=[face_message(0)] * 2 + [side_messa...  2.33 us
    pallas_call x1, Pallas kernels, grain_rows(): pl.pallas_call(functools.partial(grain_kernel, groups), out_shape=jax.Sha...  1.78 us
    ppermute x8, waiting for transfers between devices, swaps(): return (lax.ppermute(first, axis, near), lax.ppermute(second, axis, far))  1.57 us
  transfers between devices with their start and end apart: 9, of which 1 were waited for; matrix products, arithmetic and copies ran while one was open for 0% of the time, Pallas kernels for 36%

profile of v3, /device:TPU:11, one launch (start us, length us, event | category | flops | bytes accessed | tf_op | source)
XLA Modules:
  0.0 52.0 jit_solution(7956540423638174916)
XLA Ops:
  0.7 0.1 stack.43.place
  0.7 2.3 %pack.1 = (f32[2,640,128]{2,1,0:T(8,128)S(1)}, f32[2,640,128]{2,1,0:T(8,128)S(1)}, f32[2,80,128]{2,1,0:T(8,128)S(1)}, f32[2,80,128]{2,1,0:T(8,128)S(1)}) custom-call(s32[6]{0:T(128)S(1)} %stack.43.place, f32[9,8,64,256]{3,2,1,0:T(8,128)} %cos.3), custom_call_target="tpu_custom_call" | custom-call | tf_op jit(solution)/shard_map/pack/pallas_call | solution.py:298
  3.1 0.8 %collective-permute-start = (f32[2,640,128]{2,1,0:T(8,128)S(1)}, f32[2,640,128]{2,1,0:T(8,128)S(1)}, u32[]{:S(2)}, u32[]{:S(2)}) collective-permute-start(f32[2,640,128]{2,1,0:T(8,128)S(1)} %get-tuple-element.31), channel_id=1, source_target_pairs={{0,4},{4,0},{8,12},{12,8},{16,20},{20,16},{24,28},{28,24},{32,36},... | collective-permute-start | bytes 1966088 | tf_op jit(solution)/shard_map/ppermute | solution.py:540
  3.8 3.4 %collective-permute-start.1 = (f32[2,640,128]{2,1,0:T(8,128)S(1)}, f32[2,640,128]{2,1,0:T(8,128)S(1)}, u32[]{:S(2)}, u32[]{:S(2)}) collective-permute-start(f32[2,640,128]{2,1,0:T(8,128)S(1)} %get-tuple-element.32), channel_id=1, source_target_pairs={{4,8},{8,4},{12,16},{16,12},{20,24},{24,20},{28,32},{32,28},{36,40... | collective-permute-start | bytes 1966088 | tf_op jit(solution)/shard_map/ppermute | solution.py:540
  7.3 0.3 collective-permute-start.2
  7.6 3.8 %collective-permute-start.3 = (f32[2,80,128]{2,1,0:T(8,128)S(1)}, f32[2,80,128]{2,1,0:T(8,128)S(1)}, u32[]{:S(2)}, u32[]{:S(2)}) collective-permute-start(f32[2,80,128]{2,1,0:T(8,128)S(1)} %get-tuple-element.34), channel_id=1, source_target_pairs={{1,2},{2,1},{5,6},{6,5},{9,10},{10,9},{13,14},{14,13},{17,18},{18,... | collective-permute-start | bytes 245768 | tf_op jit(solution)/shard_map/ppermute | solution.py:540
  11.4 7.4 %local_step.2 = (f32[9,8,64,256]{3,2,1,0:T(8,128)}, f32[2,10,80,128]{3,2,1,0:T(8,128)S(1)}, f32[9,2,8,64,128]{4,3,2,1,0:T(8,128)S(1)}, f32[9,2,8,64,128]{4,3,2,1,0:T(8,128)S(1)}, f32[8,2,64,128]{3,2,1,0:T(8,128)S(1)}) custom-call(f32[9,8,64,256]{3,2,1,0:T(8,128)} %cos.3, f32[9,8,64,256]{3,2,1,0:T(8,128)} %fld.2), custom_call_target="tpu_custom_call" | custom-call | flops 32768000 | bytes 14155776 | tf_op jit(solution)/shard_map/local_step/pallas_call | solution.py:229
  18.8 0.0 collective-permute-done.2.got_sa
  18.8 0.0 collective-permute-done.3.got_sb
  18.9 0.0 collective-permute-done.got_fa.first_a
  18.9 0.0 collective-permute-done.1.got_fb.first_b
  18.9 0.0 copy-start
  18.9 2.5 %fix.2 = (f32[9,2,8,64,128]{4,3,2,1,0:T(8,128)S(1)}, f32[9,8,64,256]{3,2,1,0:T(8,128)}, f32[8,2,64,128]{3,2,1,0:T(8,128)S(1)}, f32[2,648,128]{2,1,0:T(8,128)S(1)...) custom-call(s32[6]{0:T(128)S(1)} %stack.43.place, ...), custom_call_target="tpu_custom_call", output_to_operand_aliasing={{0}: (7, {}), {1}: (8, {}), {2}: (9, {})} | custom-call | tf_op jit(solution)/shard_map/fix/pallas_call | solution.py:501
  21.4 0.1 collective-permute-start.4
  21.5 1.9 %collective-permute-start.5 = (f32[2,88,128]{2,1,0:T(8,128)S(1)}, f32[2,88,128]{2,1,0:T(8,128)S(1)}, u32[]{:S(2)}, u32[]{:S(2)}) collective-permute-start(f32[2,88,128]{2,1,0:T(8,128)S(1)} %get-tuple-element.41), channel_id=1, source_target_pairs={{1,2},{2,1},{5,6},{6,5},{9,10},{10,9},{13,14},{14,13},{17,18},{18,... | collective-permute-start | bytes 270344 | tf_op jit(solution)/shard_map/ppermute | solution.py:540
  23.4 0.0 copy-done
  23.4 1.8 %grain_rows.1.order = f32[256,256]{1,0:T(8,128)} custom-call(s32[1,8,8]{2,1,0:T(8,128)S(1)} %copy-done, f32[8,2,64,128]{3,2,1,0:T(8,128)S(1)} %get-tuple-element.38.sums), custom_call_target="tpu_custom_call" | custom-call | tf_op jit(solution)/shard_map/grain_rows/pallas_call | solution.py:527
  25.2 0.0 collective-permute-done.4.got_a
  25.2 1.6 %collective-permute-done.5.got_b = f32[2,88,128]{2,1,0:T(8,128)S(1)} collective-permute-done((f32[2,88,128]{2,1,0:T(8,128)S(1)}, f32[2,88,128]{2,1,0:T(8,128)S(1)}, u32[]{:S(2)}, u32[]{:S(2)}) %collective-permute-start.5) | collective-permute-done | bytes 90144 | tf_op jit(solution)/shard_map/ppermute | solution.py:540
  26.8 0.6 %corner.1 = (f32[2,88,128]{2,1,0:T(8,128)S(1)}, f32[2,88,128]{2,1,0:T(8,128)S(1)}, f32[2,648,128]{2,1,0:T(8,128)S(1)}, f32[2,648,128]{2,1,0:T(8,128)S(1)}, f32[2,16,128]{2,1,0:T(8,128)S(1)}) custom-call(s32[6]{0:T(128)S(1)} %stack.43.place, ...), custom_call_target="tpu_custom_call", output_to_operand_aliasing={{0}: (4, {}), {1}: (5, {}), {2}: (6, {}), {3}: (7, {})} | custom-call | tf_op jit(solution)/shard_map/corner/pallas_call | solution.py:356
  27.3 4.3 %collective-permute-start.6 = (f32[2,648,128]{2,1,0:T(8,128)S(1)}, f32[2,648,128]{2,1,0:T(8,128)S(1)}, u32[]{:S(2)}, u32[]{:S(2)}) collective-permute-start(f32[2,648,128]{2,1,0:T(8,128)S(1)} %get-tuple-element.47), channel_id=1, source_target_pairs={{0,4},{4,0},{8,12},{12,8},{16,20},{20,16},{24,28},{28,24},{32,36},... | collective-permute-start | bytes 1990664 | tf_op jit(solution)/shard_map/ppermute | solution.py:540
  31.6 1.9 %collective-permute-start.7 = (f32[2,648,128]{2,1,0:T(8,128)S(1)}, f32[2,648,128]{2,1,0:T(8,128)S(1)}, u32[]{:S(2)}, u32[]{:S(2)}) collective-permute-start(f32[2,648,128]{2,1,0:T(8,128)S(1)} %get-tuple-element.48), channel_id=1, source_target_pairs={{4,8},{8,4},{12,16},{16,12},{20,24},{24,20},{28,32},{32,28},{36,40... | collective-permute-start | bytes 1990664 | tf_op jit(solution)/shard_map/ppermute | solution.py:540
  33.5 8.1 %all-to-all-start = ((f32[32,8,256]{2,1,0:T(8,128)}), f32[32,8,256]{2,1,0:T(8,128)S(1)}, u32[]{:S(2)}, u32[]{:S(2)}) async-start(f32[32,8,256]{2,1,0:T(8,128)} %bitcast.6), calls=%async_computation | async-start | bytes 524288 | tf_op jit(solution)/shard_map/all_to_all | solution.py:567
  41.7 7.1 %local_step.3 = (f32[9,8,64,256]{3,2,1,0:T(8,128)}, f32[2,10,80,128]{3,2,1,0:T(8,128)S(1)}, f32[9,2,8,64,128]{4,3,2,1,0:T(8,128)S(1)}, f32[9,2,8,64,128]{4,3,2,1,0:T(8,128)S(1)}) custom-call(f32[9,8,64,256]{3,2,1,0:T(8,128)} %get-tuple-element.39.cos, f32[9,8,64,256]{3,2,1,0:T(8,128)} %fld.3, f32[2,16,128]{2,1,0:T(8,128)S(1)} %get-tuple-element.44.rest_0_), custom_call_target="tpu_custom_call" | custom-call | flops 32768000 | bytes 14155776 | tf_op jit(solution)/shard_map/local_step/pallas_call | solution.py:229
  48.7 0.0 collective-permute-done.6.got_fa
  48.8 0.0 collective-permute-done.7.got_fb
  48.8 2.6 %fix.3 = (f32[9,2,8,64,128]{4,3,2,1,0:T(8,128)S(1)}, f32[9,8,64,256]{3,2,1,0:T(8,128)}) custom-call(s32[6]{0:T(128)S(1)} %stack.43.place, f32[2,10,80,128]{3,2,1,0:T(8,128)S(1)} %get-tuple-element.45.value, f32[9,2,8,64,128]{4,3,2,1,0:T(8,128)S(1)} %get-tuple-element.46.field, ...), custom_call_target="tpu_custom_call", output_to_operand_aliasing={{0}: (7, {}), {1}: (8, {})} | custom-call | tf_op jit(solution)/shard_map/fix/pallas_call | solution.py:501
  51.4 0.0 all-to-all-done
  51.4 0.6 %reduce_sum.9 = f32[8,256]{1,0:T(8,128)} reduce(f32[32,8,256]{2,1,0:T(8,128)S(1)} %all-to-all-done, f32[]{:T(128)} %constant.32.clone.1), dimensions={0}, to_apply=%region_0.1 | reduce | flops 63488 | bytes 270340 | tf_op jit(solution)/shard_map/reduce_sum | solution.py:574
Async XLA Ops:
  3.1 15.8 %collective-permute-start = (f32[2,640,128]{2,1,0:T(8,128)S(1)}, f32[2,640,128]{2,1,0:T(8,128)S(1)}, u32[]{:S(2)}, u32[]{:S(2)}) collective-permute-start(f32[2,640,128]{2,1,0:T(8,128)S(1)} %get-tuple-element.31), channel_id=1, source_target_pairs={{0,4},{4,0},{8,12},{12,8},{16,20},{20,16},{24,28},{28,24},{32,36},... | collective-permute-start | bytes 1966088 | tf_op jit(solution)/shard_map/ppermute | solution.py:540
  3.8 15.0 %collective-permute-start.1 = (f32[2,640,128]{2,1,0:T(8,128)S(1)}, f32[2,640,128]{2,1,0:T(8,128)S(1)}, u32[]{:S(2)}, u32[]{:S(2)}) collective-permute-start(f32[2,640,128]{2,1,0:T(8,128)S(1)} %get-tuple-element.32), channel_id=1, source_target_pairs={{4,8},{8,4},{12,16},{16,12},{20,24},{24,20},{28,32},{32,28},{36,40... | collective-permute-start | bytes 1966088 | tf_op jit(solution)/shard_map/ppermute | solution.py:540
  7.3 11.6 %collective-permute-start.2 = (f32[2,80,128]{2,1,0:T(8,128)S(1)}, f32[2,80,128]{2,1,0:T(8,128)S(1)}, u32[]{:S(2)}, u32[]{:S(2)}) collective-permute-start(f32[2,80,128]{2,1,0:T(8,128)S(1)} %get-tuple-element.33), channel_id=1, source_target_pairs={{0,1},{1,0},{2,3},{3,2},{4,5},{5,4},{6,7},{7,6},{8,9},{9,8},{10,11... | collective-permute-start | bytes 245768 | tf_op jit(solution)/shard_map/ppermute | solution.py:540
  7.6 11.2 %collective-permute-start.3 = (f32[2,80,128]{2,1,0:T(8,128)S(1)}, f32[2,80,128]{2,1,0:T(8,128)S(1)}, u32[]{:S(2)}, u32[]{:S(2)}) collective-permute-start(f32[2,80,128]{2,1,0:T(8,128)S(1)} %get-tuple-element.34), channel_id=1, source_target_pairs={{1,2},{2,1},{5,6},{6,5},{9,10},{10,9},{13,14},{14,13},{17,18},{18,... | collective-permute-start | bytes 245768 | tf_op jit(solution)/shard_map/ppermute | solution.py:540
  18.9 4.5 %copy-start = (s32[1,8,8]{2,1,0:T(8,128)S(1)}, s32[1,8,8]{2,1,0:T(8,128)}, u32[]{:S(2)}) copy-start(s32[1,8,8]{2,1,0:T(8,128)} %grains.1) | copy-start | bytes 772
  21.4 3.8 %collective-permute-start.4 = (f32[2,88,128]{2,1,0:T(8,128)S(1)}, f32[2,88,128]{2,1,0:T(8,128)S(1)}, u32[]{:S(2)}, u32[]{:S(2)}) collective-permute-start(f32[2,88,128]{2,1,0:T(8,128)S(1)} %get-tuple-element.40), channel_id=1, source_target_pairs={{0,1},{1,0},{2,3},{3,2},{4,5},{5,4},{6,7},{7,6},{8,9},{9,8},{10,11... | collective-permute-start | bytes 270344 | tf_op jit(solution)/shard_map/ppermute | solution.py:540
  21.5 5.3 %collective-permute-start.5 = (f32[2,88,128]{2,1,0:T(8,128)S(1)}, f32[2,88,128]{2,1,0:T(8,128)S(1)}, u32[]{:S(2)}, u32[]{:S(2)}) collective-permute-start(f32[2,88,128]{2,1,0:T(8,128)S(1)} %get-tuple-element.41), channel_id=1, source_target_pairs={{1,2},{2,1},{5,6},{6,5},{9,10},{10,9},{13,14},{14,13},{17,18},{18,... | collective-permute-start | bytes 270344 | tf_op jit(solution)/shard_map/ppermute | solution.py:540
  27.3 21.4 %collective-permute-start.6 = (f32[2,648,128]{2,1,0:T(8,128)S(1)}, f32[2,648,128]{2,1,0:T(8,128)S(1)}, u32[]{:S(2)}, u32[]{:S(2)}) collective-permute-start(f32[2,648,128]{2,1,0:T(8,128)S(1)} %get-tuple-element.47), channel_id=1, source_target_pairs={{0,4},{4,0},{8,12},{12,8},{16,20},{20,16},{24,28},{28,24},{32,36},... | collective-permute-start | bytes 1990664 | tf_op jit(solution)/shard_map/ppermute | solution.py:540
  31.6 17.1 %collective-permute-start.7 = (f32[2,648,128]{2,1,0:T(8,128)S(1)}, f32[2,648,128]{2,1,0:T(8,128)S(1)}, u32[]{:S(2)}, u32[]{:S(2)}) collective-permute-start(f32[2,648,128]{2,1,0:T(8,128)S(1)} %get-tuple-element.48), channel_id=1, source_target_pairs={{4,8},{8,4},{12,16},{16,12},{20,24},{24,20},{28,32},{32,28},{36,40... | collective-permute-start | bytes 1990664 | tf_op jit(solution)/shard_map/ppermute | solution.py:540
  33.5 17.8 %all-to-all-start = ((f32[32,8,256]{2,1,0:T(8,128)}), f32[32,8,256]{2,1,0:T(8,128)S(1)}, u32[]{:S(2)}, u32[]{:S(2)}) async-start(f32[32,8,256]{2,1,0:T(8,128)} %bitcast.6), calls=%async_computation | async-start | bytes 524288 | tf_op jit(solution)/shard_map/all_to_all | solution.py:567

commit v4 on v3

--- a/solution.py
+++ b/solution.py
@@ -40,6 +40,15 @@
     left = jnp.where(low, 0.0, from_low), jnp.where(low, from_low, pltpu.roll(second, 1, axis))
     right = jnp.where(high, from_high, pltpu.roll(first, LN - 1, axis)), jnp.where(high, 0.0, from_high)
     return left[0] + right[0], left[1] + right[1]
+
+
+def even_place():
+    return tuple(lax.rem(lax.axis_index(axis), 2) == 0 for axis in ("gx", "gy"))
+
+
+def has_neighbours(axis, count):
+    index = lax.axis_index(axis)
+    return tuple(jnp.where(beside, 1.0, 0.0) for beside in (index > 0, index < count - 1))
 
 
 def start_all(copies):
@@ -248,9 +257,8 @@
     )(cos, fld, *more)
 
 
-def pack_kernel(place, cos, face_a, face_b, side_a, side_b, tiles, sem_p, sem_t):
-    even_x = place[0] == 0
-    even_y = place[1] == 0
+def pack_kernel(cos, face_a, face_b, side_a, side_b, tiles, sem_p, sem_t):
+    even_x, even_y = even_place()
     out_a = jnp.where(even_x, CX - 1, 0)
     in_a = jnp.where(even_x, CX - 2, 1)
     loads = start_all(
@@ -294,11 +302,11 @@
     return jax.ShapeDtypeStruct((HALF, SIDE + extra, LN), F32)
 
 
-def pack(place, cos):
+def pack(cos):
     return pl.pallas_call(
         pack_kernel,
         out_shape=[face_message(0)] * 2 + [side_message(0)] * 2,
-        in_specs=[SM, HBM],
+        in_specs=[HBM],
         out_specs=[VM] * 4,
         scratch_shapes=[
             pltpu.VMEM((2, NF, CX, 8, NZ), F32),
@@ -307,14 +315,13 @@
         ],
         compiler_params=pltpu.CompilerParams(vmem_limit_bytes=8 << 20),
         name="pack",
-    )(place, cos)
-
-
-def corner_kernel(place, first_a, first_b, order, got_a, got_b, face_a, face_b, *rest):
+    )(cos)
+
+
+def corner_kernel(sizes, first_a, first_b, order, got_a, got_b, face_a, face_b, *rest):
     del order, got_a, got_b, face_a, face_b
     side_a, side_b, out_a, out_b, corners = rest
-    even_x = place[0] == 0
-    even_y = place[1] == 0
+    even_x, even_y = even_place()
     row = lax.broadcasted_iota(jnp.int32, (CX, LN), 0)
     face = slice(SLOTS * CX, SLOTS * CX + CX)
     start = SLOTS * CY
@@ -328,7 +335,7 @@
             at_low = jnp.where(even_x, end_b, end_a)
             at_high = jnp.where(even_x, end_a, end_b)
             term = jnp.where(row == 0, at_low, jnp.where(row == CX - 1, at_high, 0.0))
-            exists = jnp.where(low_side, place[4], place[5]).astype(F32)
+            exists = jnp.where(low_side, *has_neighbours("gy", sizes[1]))
             value = ref[h, face, :] - (2.0 * DT * exists) * term
             ref[h, face, :] = value
             fixed.append(value)
@@ -352,25 +359,26 @@
 CORNERS = jax.ShapeDtypeStruct((HALF, 16, LN), F32)
 
 
-def corner(place, first, order, got, faces):
+def corner(sizes, first, order, got, faces):
     return pl.pallas_call(
-        corner_kernel,
+        functools.partial(corner_kernel, sizes),
         out_shape=[side_message(EXTRA)] * 2 + [face_message(EXTRA)] * 2 + [CORNERS],
-        in_specs=[SM, VM, VM, HBM] + [VM] * 4,
+        in_specs=[VM, VM, HBM] + [VM] * 4,
         out_specs=[VM] * 5,
-        input_output_aliases={4: 0, 5: 1, 6: 2, 7: 3},
+        input_output_aliases={3: 0, 4: 1, 5: 2, 6: 3},
         compiler_params=pltpu.CompilerParams(vmem_limit_bytes=LIMIT),
         name="corner",
-    )(place, *first, order, *got, *faces)
-
-
-def fix_kernel(first_step, place, value, field, got_fa, got_fb, got_sa, got_sb, *rest):
+    )(*first, order, *got, *faces)
+
+
+def fix_kernel(sizes, first_step, value, field, got_fa, got_fb, got_sa, got_sb, *rest):
     if first_step:
         _, _, _, work, out, sums, face_a, face_b, side_a, side_b, edge, sem = rest
     else:
         _, _, work, out, edge, sem = rest
-    even_x = place[0] == 0
-    even_y = place[1] == 0
+    even_x, even_y = even_place()
+    near_x = has_neighbours("gx", sizes[0])
+    near_y = has_neighbours("gy", sizes[1])
     stores = []
 
     def store(*where):
@@ -382,14 +390,14 @@
             stores[-1].start()
 
     row = lax.broadcasted_iota(jnp.int32, (CX, LN), 0)
-    for y, inner, present in ((0, 1, place[4]), (CY - 1, CY - 2, place[5])):
+    for y, inner, present in ((0, 1, near_y[0]), (CY - 1, CY - 2, near_y[1])):
 
         def got(h, start):
             a = got_sa[h, start : start + CX, :]
             b = got_sb[h, start : start + CX, :]
             return jnp.where(even_y, b, a) if y == 0 else jnp.where(even_y, a, b)
 
-        exists = present.astype(F32) * DT
+        exists = present * DT
         delta = [DT * got(h, SLOTS * CX) for h in BOTH]
         along_z = z_sum(*delta)
         twelve = []
@@ -420,14 +428,14 @@
         store(slice(1, NF), slice(1, CX - 1), near)
         store(0, slice(2, CX - 2), near)
 
-    for x, inner, present in ((0, 1, place[2]), (CX - 1, CX - 2, place[3])):
+    for x, inner, present in ((0, 1, near_x[0]), (CX - 1, CX - 2, near_x[1])):
 
         def got(h, start, size):
             a = got_fa[h, start : start + size, :]
             b = got_fb[h, start : start + size, :]
             return jnp.where(even_x, b, a) if x == 0 else jnp.where(even_x, a, b)
 
-        exists = present.astype(F32) * DT
+        exists = present * DT
         delta = []
         for h in BOTH:
             d = DT * got(h, SLOTS * CY, CY)
@@ -486,20 +494,20 @@
     wait_all(stores)
 
 
-def fix(place, value, field, got_faces, got_sides, base, out, sums=None):
+def fix(sizes, value, field, got_faces, got_sides, base, out, sums=None):
     first_step = sums is not None
-    args = [place, value, field, *got_faces, *got_sides, base, out]
-    in_specs = [SM] + [VM] * 7 + [HBM]
+    args = [value, field, *got_faces, *got_sides, base, out]
+    in_specs = [VM] * 7 + [HBM]
     out_shape, out_specs = [BLOCK, WHOLE], [VM, HBM]
-    aliases = {7: 0, 8: 1}
+    aliases = {6: 0, 7: 1}
     if first_step:
         args.append(sums)
         in_specs.append(VM)
         out_shape += [SUMS] + [face_message(EXTRA)] * 2 + [side_message(EXTRA)] * 2
         out_specs += [VM] * 5
-        aliases[9] = 2
+        aliases[8] = 2
     return pl.pallas_call(
-        functools.partial(fix_kernel, first_step),
+        functools.partial(fix_kernel, sizes, first_step),
         out_shape=out_shape,
         in_specs=in_specs,
         out_specs=out_specs,
@@ -541,27 +549,23 @@
 
 
 def shards(n_gx, n_gy, cotangent, fields_one, fields_zero, slot_grain):
-    gx, gy = lax.axis_index("gx"), lax.axis_index("gy")
+    sizes = n_gx, n_gy
     cotangent, fields_one, fields_zero = (
         pltpu.with_memory_space_constraint(array, pltpu.HBM)
         for array in (cotangent, fields_one, fields_zero)
     )
-    place = jnp.stack(
-        [gx % 2, gy % 2, gx > 0, gx < n_gx - 1, gy > 0, gy < n_gy - 1]
-    ).astype(jnp.int32)
-
-    face_a, face_b, side_a, side_b = pack(place, cotangent)
+    face_a, face_b, side_a, side_b = pack(cotangent)
     first_faces = swaps("gx", n_gx, face_a, face_b)
     got_sides = swaps("gy", n_gy, side_a, side_b)
     out, value, field, base, sums = local_step(cotangent, fields_one)
     costate, sums, face_a, face_b, side_a, side_b = fix(
-        place, value, field, first_faces, got_sides, base, out, sums
+        sizes, value, field, first_faces, got_sides, base, out, sums
     )
 
     got_sides = swaps("gy", n_gy, side_a, side_b)
     rows = grain_rows(slot_grain, sums, n_gx, n_gy)
     side_a, side_b, face_a, face_b, corners = corner(
-        place, first_faces, rows, got_sides, (face_a, face_b)
+        sizes, first_faces, rows, got_sides, (face_a, face_b)
     )
     got_faces = swaps("gx", n_gx, face_a, face_b)
     got_rows = lax.all_to_all(
@@ -569,7 +573,7 @@
     )
     costate = pltpu.with_memory_space_constraint(costate, pltpu.HBM)
     out, value, field, base = local_step(costate, fields_zero, corners)
-    (adjoint,) = fix(place, value, field, got_faces, (side_a, side_b), base, out)
+    (adjoint,) = fix(sizes, value, field, got_faces, (side_a, side_b), base, out)
     got_rows, adjoint = lax.optimization_barrier((got_rows, adjoint))
     grain_grad = jnp.sum(got_rows.reshape(n_gx, GRAIN_DEV, NZ), axis=0)
     return adjoint, grain_grad

time: 52.3 us -> 49.9 us (0.954)
  Pallas kernels: 24.2 us -> 21.9 us
    pallas_call x3, Pallas kernels: 5.65 us -> 4.04 us  [the longest x2 4.02 us: fix(): pl.pallas_call(functools.partial(fix_kernel, sizes, first_step), out_shap...]
    pallas_call x1, Pallas kernels: 2.33 us -> 1.79 us  [pack(): pl.pallas_call(pack_kernel, out_shape=[face_message(0)] * 2 + [side_messa...]
where the time goes in v4:
time: 49.9 us; the launch traced here: 49.5 us
  starting transfers between devices  24.6 us (49%)
  Pallas kernels  21.9 us (44%)
  waiting for transfers between devices  1.57 us (3%)
  between operations  0.79 us (2%)
  other arithmetic  0.63 us (1%)
    ppermute x8, starting transfers between devices, swaps(): return (lax.ppermute(first, axis, near), lax.ppermute(second, axis, far))  16.5 us
    pallas_call x2, Pallas kernels, local_step(): pl.pallas_call(functools.partial(local_kernel, with_sums), out_shape=[WHO...  14.3 us
    all_to_all x1, starting transfers between devices, shards(): lax.all_to_all(rows.reshape(n_gx, GRAIN_DEV, NZ), 'gx', split_axis=0, con...  8.14 us
    pallas_call x2, Pallas kernels, fix(): pl.pallas_call(functools.partial(fix_kernel, sizes, first_step), out_shap...  4.02 us
    pallas_call x1, Pallas kernels, pack(): pl.pallas_call(pack_kernel, out_shape=[face_message(0)] * 2 + [side_messa...  1.79 us
    pallas_call x1, Pallas kernels, grain_rows(): pl.pallas_call(functools.partial(grain_kernel, groups), out_shape=jax.Sha...  1.78 us
    ppermute x8, waiting for transfers between devices, swaps(): return (lax.ppermute(first, axis, near), lax.ppermute(second, axis, far))  1.57 us
  transfers between devices with their start and end apart: 9, of which 1 were waited for; matrix products, arithmetic and copies ran while one was open for 0% of the time, Pallas kernels for 36%

profile of v4, /device:TPU:11, one launch (start us, length us, event | category | flops | bytes accessed | tf_op | source)
XLA Modules:
  0.0 49.5 jit_solution(49084333465050299)
XLA Ops:
  0.6 1.8 %pack.1 = (f32[2,640,128]{2,1,0:T(8,128)S(1)}, f32[2,640,128]{2,1,0:T(8,128)S(1)}, f32[2,80,128]{2,1,0:T(8,128)S(1)}, f32[2,80,128]{2,1,0:T(8,128)S(1)}) custom-call(f32[9,8,64,256]{3,2,1,0:T(8,128)} %cos.3), custom_call_target="tpu_custom_call" | custom-call | tf_op jit(solution)/shard_map/pack/pallas_call | solution.py:306
  2.4 0.8 %collective-permute-start = (f32[2,640,128]{2,1,0:T(8,128)S(1)}, f32[2,640,128]{2,1,0:T(8,128)S(1)}, u32[]{:S(2)}, u32[]{:S(2)}) collective-permute-start(f32[2,640,128]{2,1,0:T(8,128)S(1)} %get-tuple-element.31), channel_id=1, source_target_pairs={{0,4},{4,0},{8,12},{12,8},{16,20},{20,16},{24,28},{28,24},{32,36},... | collective-permute-start | bytes 1966088 | tf_op jit(solution)/shard_map/ppermute | solution.py:548
  3.2 3.4 %collective-permute-start.1 = (f32[2,640,128]{2,1,0:T(8,128)S(1)}, f32[2,640,128]{2,1,0:T(8,128)S(1)}, u32[]{:S(2)}, u32[]{:S(2)}) collective-permute-start(f32[2,640,128]{2,1,0:T(8,128)S(1)} %get-tuple-element.32), channel_id=1, source_target_pairs={{4,8},{8,4},{12,16},{16,12},{20,24},{24,20},{28,32},{32,28},{36,40... | collective-permute-start | bytes 1966088 | tf_op jit(solution)/shard_map/ppermute | solution.py:548
  6.6 0.3 collective-permute-start.2
  7.0 3.8 %collective-permute-start.3 = (f32[2,80,128]{2,1,0:T(8,128)S(1)}, f32[2,80,128]{2,1,0:T(8,128)S(1)}, u32[]{:S(2)}, u32[]{:S(2)}) collective-permute-start(f32[2,80,128]{2,1,0:T(8,128)S(1)} %get-tuple-element.34), channel_id=1, source_target_pairs={{1,2},{2,1},{5,6},{6,5},{9,10},{10,9},{13,14},{14,13},{17,18},{18,... | collective-permute-start | bytes 245768 | tf_op jit(solution)/shard_map/ppermute | solution.py:548
  10.7 7.2 %local_step.2 = (f32[9,8,64,256]{3,2,1,0:T(8,128)}, f32[2,10,80,128]{3,2,1,0:T(8,128)S(1)}, f32[9,2,8,64,128]{4,3,2,1,0:T(8,128)S(1)}, f32[9,2,8,64,128]{4,3,2,1,0:T(8,128)S(1)}, f32[8,2,64,128]{3,2,1,0:T(8,128)S(1)}) custom-call(f32[9,8,64,256]{3,2,1,0:T(8,128)} %cos.3, f32[9,8,64,256]{3,2,1,0:T(8,128)} %fld.2), custom_call_target="tpu_custom_call" | custom-call | flops 32768000 | bytes 14155776 | tf_op jit(solution)/shard_map/local_step/pallas_call | solution.py:238
  18.0 0.0 collective-permute-done.2.got_sa
  18.0 0.0 collective-permute-done.3.got_sb
  18.0 0.0 collective-permute-done.got_fa.first_a
  18.0 0.0 collective-permute-done.1.got_fb.first_b
  18.0 0.0 copy-start
  18.0 2.0 %fix.2 = (f32[9,2,8,64,128]{4,3,2,1,0:T(8,128)S(1)}, f32[9,8,64,256]{3,2,1,0:T(8,128)}, f32[8,2,64,128]{3,2,1,0:T(8,128)S(1)}, f32[2,648,128]{2,1,0:T(8,128)S(1)...) custom-call(f32[2,10,80,128]{3,2,1,0:T(8,128)S(1)} %get-tuple-elemen, ...), custom_call_target="tpu_custom_call", output_to_operand_aliasing={{0}: (6, {}), {1}: (7, {}), {2}: (8, {})} | custom-call | tf_op jit(solution)/shard_map/fix/pallas_call | solution.py:509
  20.1 0.1 collective-permute-start.4
  20.2 1.9 %collective-permute-start.5 = (f32[2,88,128]{2,1,0:T(8,128)S(1)}, f32[2,88,128]{2,1,0:T(8,128)S(1)}, u32[]{:S(2)}, u32[]{:S(2)}) collective-permute-start(f32[2,88,128]{2,1,0:T(8,128)S(1)} %get-tuple-element.41), channel_id=1, source_target_pairs={{1,2},{2,1},{5,6},{6,5},{9,10},{10,9},{13,14},{14,13},{17,18},{18,... | collective-permute-start | bytes 270344 | tf_op jit(solution)/shard_map/ppermute | solution.py:548
  22.1 0.0 copy-done
  22.1 1.8 %grain_rows.1.order = f32[256,256]{1,0:T(8,128)} custom-call(s32[1,8,8]{2,1,0:T(8,128)S(1)} %copy-done, f32[8,2,64,128]{3,2,1,0:T(8,128)S(1)} %get-tuple-element.38.sums), custom_call_target="tpu_custom_call" | custom-call | tf_op jit(solution)/shard_map/grain_rows/pallas_call | solution.py:535
  23.9 0.0 collective-permute-done.4.got_a
  23.9 1.6 %collective-permute-done.5.got_b = f32[2,88,128]{2,1,0:T(8,128)S(1)} collective-permute-done((f32[2,88,128]{2,1,0:T(8,128)S(1)}, f32[2,88,128]{2,1,0:T(8,128)S(1)}, u32[]{:S(2)}, u32[]{:S(2)}) %collective-permute-start.5) | collective-permute-done | bytes 90144 | tf_op jit(solution)/shard_map/ppermute | solution.py:548
  25.5 4.3 %collective-permute-start.6 = (f32[2,648,128]{2,1,0:T(8,128)S(1)}, f32[2,648,128]{2,1,0:T(8,128)S(1)}, u32[]{:S(2)}, u32[]{:S(2)}) collective-permute-start(f32[2,648,128]{2,1,0:T(8,128)S(1)} %get-tuple-element.47), channel_id=1, source_target_pairs={{0,4},{4,0},{8,12},{12,8},{16,20},{20,16},{24,28},{28,24},{32,36},... | collective-permute-start | bytes 1990664 | tf_op jit(solution)/shard_map/ppermute | solution.py:548
  29.7 1.9 %collective-permute-start.7 = (f32[2,648,128]{2,1,0:T(8,128)S(1)}, f32[2,648,128]{2,1,0:T(8,128)S(1)}, u32[]{:S(2)}, u32[]{:S(2)}) collective-permute-start(f32[2,648,128]{2,1,0:T(8,128)S(1)} %get-tuple-element.48), channel_id=1, source_target_pairs={{4,8},{8,4},{12,16},{16,12},{20,24},{24,20},{28,32},{32,28},{36,40... | collective-permute-start | bytes 1990664 | tf_op jit(solution)/shard_map/ppermute | solution.py:548
  31.7 8.1 %all-to-all-start = ((f32[32,8,256]{2,1,0:T(8,128)}), f32[32,8,256]{2,1,0:T(8,128)S(1)}, u32[]{:S(2)}, u32[]{:S(2)}) async-start(f32[32,8,256]{2,1,0:T(8,128)} %bitcast), calls=%async_computation | async-start | bytes 524288 | tf_op jit(solution)/shard_map/all_to_all | solution.py:571
  39.8 7.1 %local_step.3 = (f32[9,8,64,256]{3,2,1,0:T(8,128)}, f32[2,10,80,128]{3,2,1,0:T(8,128)S(1)}, f32[9,2,8,64,128]{4,3,2,1,0:T(8,128)S(1)}, f32[9,2,8,64,128]{4,3,2,1,0:T(8,128)S(1)}) custom-call(f32[9,8,64,256]{3,2,1,0:T(8,128)} %get-tuple-element.39.cos, f32[9,8,64,256]{3,2,1,0:T(8,128)} %fld.3, f32[2,16,128]{2,1,0:T(8,128)S(1)} %get-tuple-element.44.rest_0_), custom_call_target="tpu_custom_call" | custom-call | flops 32768000 | bytes 14155776 | tf_op jit(solution)/shard_map/local_step/pallas_call | solution.py:238
  46.9 0.0 collective-permute-done.6.got_fa
  46.9 0.0 collective-permute-done.7.got_fb
  46.9 2.0 %fix.3 = (f32[9,2,8,64,128]{4,3,2,1,0:T(8,128)S(1)}, f32[9,8,64,256]{3,2,1,0:T(8,128)}) custom-call(f32[2,10,80,128]{3,2,1,0:T(8,128)S(1)} %get-tuple-element.45.value, f32[9,2,8,64,128]{4,3,2,1,0:T(8,128)S(1)} %get-tuple-element.46.field, f32[2,648,128]{2,1,0:T(8,128)S(1)} %collective-permute-done.6.got_fa, ...), custom_call_target="tpu_custom_call", output_to_operand_aliasing={{0}: (6, {}), {1}: (7, {})} | custom-call | tf_op jit(solution)/shard_map/fix/pallas_call | solution.py:509
  48.9 0.0 all-to-all-done
  48.9 0.6 %reduce_sum.9 = f32[8,256]{1,0:T(8,128)} reduce(f32[32,8,256]{2,1,0:T(8,128)S(1)} %all-to-all-done, f32[]{:T(128)} %constant.0.clone.1), dimensions={0}, to_apply=%region_0.0 | reduce | flops 63488 | bytes 270340 | tf_op jit(solution)/shard_map/reduce_sum | solution.py:578
  (1 shorter events, 0.0 us)
Async XLA Ops:
  2.4 15.6 %collective-permute-start = (f32[2,640,128]{2,1,0:T(8,128)S(1)}, f32[2,640,128]{2,1,0:T(8,128)S(1)}, u32[]{:S(2)}, u32[]{:S(2)}) collective-permute-start(f32[2,640,128]{2,1,0:T(8,128)S(1)} %get-tuple-element.31), channel_id=1, source_target_pairs={{0,4},{4,0},{8,12},{12,8},{16,20},{20,16},{24,28},{28,24},{32,36},... | collective-permute-start | bytes 1966088 | tf_op jit(solution)/shard_map/ppermute | solution.py:548
  3.2 14.8 %collective-permute-start.1 = (f32[2,640,128]{2,1,0:T(8,128)S(1)}, f32[2,640,128]{2,1,0:T(8,128)S(1)}, u32[]{:S(2)}, u32[]{:S(2)}) collective-permute-start(f32[2,640,128]{2,1,0:T(8,128)S(1)} %get-tuple-element.32), channel_id=1, source_target_pairs={{4,8},{8,4},{12,16},{16,12},{20,24},{24,20},{28,32},{32,28},{36,40... | collective-permute-start | bytes 1966088 | tf_op jit(solution)/shard_map/ppermute | solution.py:548
  6.6 11.4 %collective-permute-start.2 = (f32[2,80,128]{2,1,0:T(8,128)S(1)}, f32[2,80,128]{2,1,0:T(8,128)S(1)}, u32[]{:S(2)}, u32[]{:S(2)}) collective-permute-start(f32[2,80,128]{2,1,0:T(8,128)S(1)} %get-tuple-element.33), channel_id=1, source_target_pairs={{0,1},{1,0},{2,3},{3,2},{4,5},{5,4},{6,7},{7,6},{8,9},{9,8},{10,11... | collective-permute-start | bytes 245768 | tf_op jit(solution)/shard_map/ppermute | solution.py:548
  7.0 11.0 %collective-permute-start.3 = (f32[2,80,128]{2,1,0:T(8,128)S(1)}, f32[2,80,128]{2,1,0:T(8,128)S(1)}, u32[]{:S(2)}, u32[]{:S(2)}) collective-permute-start(f32[2,80,128]{2,1,0:T(8,128)S(1)} %get-tuple-element.34), channel_id=1, source_target_pairs={{1,2},{2,1},{5,6},{6,5},{9,10},{10,9},{13,14},{14,13},{17,18},{18,... | collective-permute-start | bytes 245768 | tf_op jit(solution)/shard_map/ppermute | solution.py:548
  18.0 4.1 %copy-start = (s32[1,8,8]{2,1,0:T(8,128)S(1)}, s32[1,8,8]{2,1,0:T(8,128)}, u32[]{:S(2)}) copy-start(s32[1,8,8]{2,1,0:T(8,128)} %grains.1) | copy-start | bytes 772
  20.1 3.8 %collective-permute-start.4 = (f32[2,88,128]{2,1,0:T(8,128)S(1)}, f32[2,88,128]{2,1,0:T(8,128)S(1)}, u32[]{:S(2)}, u32[]{:S(2)}) collective-permute-start(f32[2,88,128]{2,1,0:T(8,128)S(1)} %get-tuple-element.40), channel_id=1, source_target_pairs={{0,1},{1,0},{2,3},{3,2},{4,5},{5,4},{6,7},{7,6},{8,9},{9,8},{10,11... | collective-permute-start | bytes 270344 | tf_op jit(solution)/shard_map/ppermute | solution.py:548
  20.2 5.3 %collective-permute-start.5 = (f32[2,88,128]{2,1,0:T(8,128)S(1)}, f32[2,88,128]{2,1,0:T(8,128)S(1)}, u32[]{:S(2)}, u32[]{:S(2)}) collective-permute-start(f32[2,88,128]{2,1,0:T(8,128)S(1)} %get-tuple-element.41), channel_id=1, source_target_pairs={{1,2},{2,1},{5,6},{6,5},{9,10},{10,9},{13,14},{14,13},{17,18},{18,... | collective-permute-start | bytes 270344 | tf_op jit(solution)/shard_map/ppermute | solution.py:548
  25.5 21.4 %collective-permute-start.6 = (f32[2,648,128]{2,1,0:T(8,128)S(1)}, f32[2,648,128]{2,1,0:T(8,128)S(1)}, u32[]{:S(2)}, u32[]{:S(2)}) collective-permute-start(f32[2,648,128]{2,1,0:T(8,128)S(1)} %get-tuple-element.47), channel_id=1, source_target_pairs={{0,4},{4,0},{8,12},{12,8},{16,20},{20,16},{24,28},{28,24},{32,36},... | collective-permute-start | bytes 1990664 | tf_op jit(solution)/shard_map/ppermute | solution.py:548
  29.7 17.1 %collective-permute-start.7 = (f32[2,648,128]{2,1,0:T(8,128)S(1)}, f32[2,648,128]{2,1,0:T(8,128)S(1)}, u32[]{:S(2)}, u32[]{:S(2)}) collective-permute-start(f32[2,648,128]{2,1,0:T(8,128)S(1)} %get-tuple-element.48), channel_id=1, source_target_pairs={{4,8},{8,4},{12,16},{16,12},{20,24},{24,20},{28,32},{32,28},{36,40... | collective-permute-start | bytes 1990664 | tf_op jit(solution)/shard_map/ppermute | solution.py:548
  31.7 17.2 %all-to-all-start = ((f32[32,8,256]{2,1,0:T(8,128)}), f32[32,8,256]{2,1,0:T(8,128)S(1)}, u32[]{:S(2)}, u32[]{:S(2)}) async-start(f32[32,8,256]{2,1,0:T(8,128)} %bitcast), calls=%async_computation | async-start | bytes 524288 | tf_op jit(solution)/shard_map/all_to_all | solution.py:571

commit v5 on v4

--- a/solution.py
+++ b/solution.py
@@ -371,11 +371,30 @@
     )(*first, order, *got, *faces)
 
 
-def fix_kernel(sizes, first_step, value, field, got_fa, got_fb, got_sa, got_sb, *rest):
-    if first_step:
-        _, _, _, work, out, sums, face_a, face_b, side_a, side_b, edge, sem = rest
+def grain_rows(groups, grains, sums, rows):
+    rows[...] = jnp.zeros(rows.shape, F32)
+    row = lax.broadcasted_iota(jnp.int32, (GRAIN_DEV, LN), 0)
+    for t in range(CY // 8):
+        for s in range(SLOTS):
+            grain = grains[0, t, s]
+            start = pl.multiple_of(grain // (GRAIN_DEV * groups) * GRAIN_DEV, GRAIN_DEV)
+            chosen = row == grain % GRAIN_DEV
+            for h in range(HALF):
+                total = DT * jnp.sum(sums[s, h, t * 8 : t * 8 + 8, :], axis=0, keepdims=True)
+                rows[pl.ds(start, GRAIN_DEV), lanes(h)] += jnp.where(chosen, total, 0.0)
+
+
+def fix_kernel(sizes, stage, *refs):
+    sums = None
+    if stage == "early":
+        value, field, got_fa, got_fb, got_sa, got_sb, _, _, work, sums, side_a, side_b, edge = refs
+        spans = (slice(0, 8), slice(CY - 8, CY))
+    elif stage == "late":
+        grains, value, field, got_fa, got_fb, _, _, _, work, out, sums, face_a, face_b, rows, edge, sem = refs
+        spans = (slice(8, CY - 8),)
     else:
-        _, _, work, out, edge, sem = rest
+        value, field, got_fa, got_fb, got_sa, got_sb, _, _, work, out, edge, sem = refs
+        spans = (slice(0, CY),)
     even_x, even_y = even_place()
     near_x = has_neighbours("gx", sizes[0])
     near_y = has_neighbours("gy", sizes[1])
@@ -383,7 +402,7 @@
 
     def store(*where):
         s, x, y = where
-        for h in BOTH:
+        for h in BOTH if stage != "early" else ():
             stores.append(
                 pltpu.make_async_copy(work.at[s, h, x, y, :], out.at[s, x, y, lanes(h)], sem.at[len(stores)])
             )
@@ -391,6 +410,11 @@
 
     row = lax.broadcasted_iota(jnp.int32, (CX, LN), 0)
     for y, inner, present in ((0, 1, near_y[0]), (CY - 1, CY - 2, near_y[1])):
+        near = slice(0, 8) if y == 0 else slice(CY - 8, CY)
+        if stage == "late":
+            store(slice(1, NF), slice(1, CX - 1), near)
+            store(0, slice(2, CX - 2), near)
+            continue
 
         def got(h, start):
             a = got_sa[h, start : start + CX, :]
@@ -422,9 +446,8 @@
                 eta = field[s, h, :, y, :]
                 change = DT * got(h, (s - 1) * CX) + twelve[h] * (eta * eta - eta)
                 work[s, h, :, y, :] = work[s, h, :, y, :] + change
-                if first_step:
+                if sums is not None:
                     sums[s - 1, h, y : y + 1, :] += jnp.sum(change, axis=0, keepdims=True)
-        near = slice(0, 8) if y == 0 else slice(CY - 8, CY)
         store(slice(1, NF), slice(1, CX - 1), near)
         store(0, slice(2, CX - 2), near)
 
@@ -441,48 +464,55 @@
             d = DT * got(h, SLOTS * CY, CY)
             delta.append(d)
             edge[h, 8 : 8 + CY, :] = d
-            if first_step:
+            if sums is not None:
                 edge[h, 0:8, :] = jnp.zeros((8, LN), F32)
                 edge[h, 8 + CY : 16 + CY, :] = jnp.zeros((8, LN), F32)
             else:
                 ends = DT * got(h, FACE, 8)
                 edge[h, 7:8, :] = ends[0:1, :]
                 edge[h, 8 + CY : 9 + CY, :] = ends[1:2, :]
-        along_z = z_sum(*delta)
-        twelve = []
-        for h in BOTH:
-            total = along_z[h] + edge[h, 9 : 9 + CY, :] + edge[h, 7 : 7 + CY, :] - 6.0 * delta[h]
-            density = field[0, h, x]
-            curvature = 34.0 + density * (192.0 * density - 192.0)
-            work[0, h, x] += (
-                delta[h] * curvature
-                - 2.0 * total
-                - DT * got(h, (SLOTS + 1) * CY, CY)
-                - exists * value[h, x + 1, PAD : PAD + CY, :]
-            )
-            work[0, h, inner] -= delta[h]
-            twelve.append(12.0 * delta[h])
-        for s in range(1, NF):
+        for span in spans:
+            size = span.stop - span.start
+            part = [d[span] for d in delta]
+            along_z = z_sum(*part)
+            twelve = []
             for h in BOTH:
-                eta = field[s, h, x]
-                change = DT * got(h, (s - 1) * CY, CY) + twelve[h] * (eta * eta - eta)
-                work[s, h, x] += change
-                if first_step:
-                    sums[s - 1, h] += change
+                above = edge[h, 9 + span.start : 9 + span.stop, :]
+                below = edge[h, 7 + span.start : 7 + span.stop, :]
+                total = along_z[h] + above + below - 6.0 * part[h]
+                density = field[0, h, x, span, :]
+                curvature = 34.0 + density * (192.0 * density - 192.0)
+                work[0, h, x, span, :] += (
+                    part[h] * curvature
+                    - 2.0 * total
+                    - DT * got(h, (SLOTS + 1) * CY + span.start, size)
+                    - exists * value[h, x + 1, PAD + span.start : PAD + span.stop, :]
+                )
+                work[0, h, inner, span, :] -= part[h]
+                twelve.append(12.0 * part[h])
+            for s in range(1, NF):
+                for h in BOTH:
+                    eta = field[s, h, x, span, :]
+                    change = DT * got(h, (s - 1) * CY + span.start, size) + twelve[h] * (eta * eta - eta)
+                    work[s, h, x, span, :] += change
+                    if sums is not None:
+                        sums[s - 1, h, span, :] += change
         store(slice(0, NF), x, slice(0, CY))
         store(0, inner, slice(0, CY))
 
-    if first_step:
-        for h in BOTH:
-            for k in range(SLOTS + 2):
-                s = k + 1 if k < SLOTS else 0
-                depth = 1 if k == SLOTS + 1 else 0
+    for h in BOTH:
+        for k in range(SLOTS + 2):
+            s = k + 1 if k < SLOTS else 0
+            depth = 1 if k == SLOTS + 1 else 0
+            if stage == "late":
                 low, high = (work[s, h, x] for x in (depth, CX - 1 - depth))
                 face_a[h, k * CY : (k + 1) * CY, :] = jnp.where(even_x, high, low)
                 face_b[h, k * CY : (k + 1) * CY, :] = jnp.where(even_x, low, high)
+            if stage == "early":
                 low, high = (work[s, h, :, y, :] for y in (depth, CY - 1 - depth))
                 side_a[h, k * CX : (k + 1) * CX, :] = jnp.where(even_y, high, low)
                 side_b[h, k * CX : (k + 1) * CX, :] = jnp.where(even_y, low, high)
+        if stage == "early":
             start = SLOTS * CY
             ends = []
             for at in (start, start + CY - 1):
@@ -491,55 +521,53 @@
                 ends.append(jnp.where(row == 0, at_low, at_high))
             side_a[h, SIDE : SIDE + 8, :] = jnp.where(even_y, ends[1], ends[0])
             side_b[h, SIDE : SIDE + 8, :] = jnp.where(even_y, ends[0], ends[1])
+    if stage == "late":
+        grain_rows(sizes[1], grains, sums, rows)
     wait_all(stores)
 
 
-def fix(sizes, value, field, got_faces, got_sides, base, out, sums=None):
-    first_step = sums is not None
-    args = [value, field, *got_faces, *got_sides, base, out]
-    in_specs = [VM] * 7 + [HBM]
-    out_shape, out_specs = [BLOCK, WHOLE], [VM, HBM]
-    aliases = {6: 0, 7: 1}
-    if first_step:
-        args.append(sums)
-        in_specs.append(VM)
-        out_shape += [SUMS] + [face_message(EXTRA)] * 2 + [side_message(EXTRA)] * 2
-        out_specs += [VM] * 5
-        aliases[8] = 2
+EDGE = pltpu.VMEM((HALF, ROWS, LN), F32)
+STORES = pltpu.SemaphoreType.DMA((16,))
+
+
+def fix_early(sizes, value, field, got_faces, got_sides, base, sums):
     return pl.pallas_call(
-        functools.partial(fix_kernel, sizes, first_step),
-        out_shape=out_shape,
-        in_specs=in_specs,
-        out_specs=out_specs,
-        scratch_shapes=[pltpu.VMEM((HALF, ROWS, LN), F32), pltpu.SemaphoreType.DMA((16,))],
-        input_output_aliases=aliases,
+        functools.partial(fix_kernel, sizes, "early"),
+        out_shape=[BLOCK, SUMS] + [side_message(EXTRA)] * 2,
+        in_specs=[VM] * 8,
+        out_specs=[VM] * 4,
+        scratch_shapes=[EDGE],
+        input_output_aliases={6: 0, 7: 1},
         compiler_params=pltpu.CompilerParams(vmem_limit_bytes=LIMIT),
-        name="fix",
-    )(*args)[1:]
-
-
-def grain_kernel(groups, grains, sums, rows):
-    rows[...] = jnp.zeros(rows.shape, F32)
-    row = lax.broadcasted_iota(jnp.int32, (GRAIN_DEV, LN), 0)
-    for t in range(CY // 8):
-        for s in range(SLOTS):
-            grain = grains[0, t, s]
-            start = pl.multiple_of(grain // (GRAIN_DEV * groups) * GRAIN_DEV, GRAIN_DEV)
-            chosen = row == grain % GRAIN_DEV
-            for h in range(HALF):
-                total = DT * jnp.sum(sums[s, h, t * 8 : t * 8 + 8, :], axis=0, keepdims=True)
-                rows[pl.ds(start, GRAIN_DEV), lanes(h)] += jnp.where(chosen, total, 0.0)
-
-
-def grain_rows(slot_grain, sums, peers, groups):
+        name="fix_early",
+    )(value, field, *got_faces, *got_sides, base, sums)
+
+
+def fix_late(sizes, slot_grain, value, field, got_faces, base, out, sums):
+    rows = jax.ShapeDtypeStruct((sizes[0] * GRAIN_DEV, NZ), F32)
     return pl.pallas_call(
-        functools.partial(grain_kernel, groups),
-        out_shape=jax.ShapeDtypeStruct((peers * GRAIN_DEV, NZ), F32),
-        in_specs=[SM, VM],
-        out_specs=VM,
+        functools.partial(fix_kernel, sizes, "late"),
+        out_shape=[BLOCK, WHOLE, SUMS] + [face_message(EXTRA)] * 2 + [rows],
+        in_specs=[SM] + [VM] * 5 + [HBM, VM],
+        out_specs=[VM, HBM] + [VM] * 4,
+        scratch_shapes=[EDGE, STORES],
+        input_output_aliases={5: 0, 6: 1, 7: 2},
         compiler_params=pltpu.CompilerParams(vmem_limit_bytes=LIMIT),
-        name="grain_rows",
-    )(slot_grain, sums)
+        name="fix_late",
+    )(slot_grain, value, field, *got_faces, base, out, sums)
+
+
+def fix_whole(sizes, value, field, got_faces, got_sides, base, out):
+    return pl.pallas_call(
+        functools.partial(fix_kernel, sizes, "whole"),
+        out_shape=[BLOCK, WHOLE],
+        in_specs=[VM] * 7 + [HBM],
+        out_specs=[VM, HBM],
+        scratch_shapes=[EDGE, STORES],
+        input_output_aliases={6: 0, 7: 1},
+        compiler_params=pltpu.CompilerParams(vmem_limit_bytes=LIMIT),
+        name="fix_whole",
+    )(value, field, *got_faces, *got_sides, base, out)[1]
 
 
 def swaps(axis, count, first, second):
@@ -558,12 +586,12 @@
     first_faces = swaps("gx", n_gx, face_a, face_b)
     got_sides = swaps("gy", n_gy, side_a, side_b)
     out, value, field, base, sums = local_step(cotangent, fields_one)
-    costate, sums, face_a, face_b, side_a, side_b = fix(
-        sizes, value, field, first_faces, got_sides, base, out, sums
+    base, sums, side_a, side_b = fix_early(sizes, value, field, first_faces, got_sides, base, sums)
+
+    got_sides = swaps("gy", n_gy, side_a, side_b)
+    _, costate, _, face_a, face_b, rows = fix_late(
+        sizes, slot_grain, value, field, first_faces, base, out, sums
     )
-
-    got_sides = swaps("gy", n_gy, side_a, side_b)
-    rows = grain_rows(slot_grain, sums, n_gx, n_gy)
     side_a, side_b, face_a, face_b, corners = corner(
         sizes, first_faces, rows, got_sides, (face_a, face_b)
     )
@@ -573,7 +601,7 @@
     )
     costate = pltpu.with_memory_space_constraint(costate, pltpu.HBM)
     out, value, field, base = local_step(costate, fields_zero, corners)
-    (adjoint,) = fix(sizes, value, field, got_faces, (side_a, side_b), base, out)
+    adjoint = fix_whole(sizes, value, field, got_faces, (side_a, side_b), base, out)
     got_rows, adjoint = lax.optimization_barrier((got_rows, adjoint))
     grain_grad = jnp.sum(got_rows.reshape(n_gx, GRAIN_DEV, NZ), axis=0)
     return adjoint, grain_grad

time: 49.9 us -> 48.5 us (0.972)
  waiting for transfers between devices: 1.57 us -> 0.5 us
    ppermute x8, waiting for transfers between devices: 1.57 us -> 0.5 us  [swaps(): return (lax.ppermute(first, axis, near), lax.ppermute(second, axis, far))]
  transfers between devices with their start and end apart: 9 -> 9, of which waited for: 1 -> 1; matrix products, arithmetic and copies ran while one was open for 0% -> 0% of each run, Pallas kernels for 36% -> 40%
where the time goes in v5:
time: 48.5 us; the launch traced here: 48.2 us
  starting transfers between devices  24.6 us (51%)
  Pallas kernels  21.6 us (45%)
  between operations  0.81 us (2%)
  other arithmetic  0.63 us (1%)
  waiting for transfers between devices  0.5 us (1%)
    ppermute x8, starting transfers between devices, swaps(): return (lax.ppermute(first, axis, near), lax.ppermute(second, axis, far))  16.5 us
    pallas_call x2, Pallas kernels, local_step(): pl.pallas_call(functools.partial(local_kernel, with_sums), out_shape=[WHO...  14.3 us
    all_to_all x1, starting transfers between devices, shards(): lax.all_to_all(rows.reshape(n_gx, GRAIN_DEV, NZ), 'gx', split_axis=0, con...  8.15 us
    pallas_call x1, Pallas kernels, fix_late(): pl.pallas_call(functools.partial(fix_kernel, sizes, 'late'), out_shape=[B...  2.84 us
    pallas_call x1, Pallas kernels, fix_whole(): pl.pallas_call(functools.partial(fix_kernel, sizes, 'whole'), out_shape=[...  2 us
    pallas_call x1, Pallas kernels, pack(): pl.pallas_call(pack_kernel, out_shape=[face_message(0)] * 2 + [side_messa...  1.79 us
  transfers between devices with their start and end apart: 9, of which 1 were waited for; matrix products, arithmetic and copies ran while one was open for 0% of the time, Pallas kernels for 40%

profile of v5, /device:TPU:11, one launch (start us, length us, event | category | flops | bytes accessed | tf_op | source)
XLA Modules:
  0.0 48.2 jit_solution(1736031129569631315)
XLA Ops:
  0.6 1.8 %pack.1 = (f32[2,640,128]{2,1,0:T(8,128)S(1)}, f32[2,640,128]{2,1,0:T(8,128)S(1)}, f32[2,80,128]{2,1,0:T(8,128)S(1)}, f32[2,80,128]{2,1,0:T(8,128)S(1)}) custom-call(f32[9,8,64,256]{3,2,1,0:T(8,128)} %cos.3), custom_call_target="tpu_custom_call" | custom-call | tf_op jit(solution)/shard_map/pack/pallas_call | solution.py:306
  2.4 0.8 %collective-permute-start = (f32[2,640,128]{2,1,0:T(8,128)S(1)}, f32[2,640,128]{2,1,0:T(8,128)S(1)}, u32[]{:S(2)}, u32[]{:S(2)}) collective-permute-start(f32[2,640,128]{2,1,0:T(8,128)S(1)} %get-tuple-element.33), channel_id=1, source_target_pairs={{0,4},{4,0},{8,12},{12,8},{16,20},{20,16},{24,28},{28,24},{32,36},... | collective-permute-start | bytes 1966088 | tf_op jit(solution)/shard_map/ppermute | solution.py:576
  3.2 3.4 %collective-permute-start.1 = (f32[2,640,128]{2,1,0:T(8,128)S(1)}, f32[2,640,128]{2,1,0:T(8,128)S(1)}, u32[]{:S(2)}, u32[]{:S(2)}) collective-permute-start(f32[2,640,128]{2,1,0:T(8,128)S(1)} %get-tuple-element.34), channel_id=1, source_target_pairs={{4,8},{8,4},{12,16},{16,12},{20,24},{24,20},{28,32},{32,28},{36,40... | collective-permute-start | bytes 1966088 | tf_op jit(solution)/shard_map/ppermute | solution.py:576
  6.6 0.3 collective-permute-start.2
  7.0 3.8 %collective-permute-start.3 = (f32[2,80,128]{2,1,0:T(8,128)S(1)}, f32[2,80,128]{2,1,0:T(8,128)S(1)}, u32[]{:S(2)}, u32[]{:S(2)}) collective-permute-start(f32[2,80,128]{2,1,0:T(8,128)S(1)} %get-tuple-element.36), channel_id=1, source_target_pairs={{1,2},{2,1},{5,6},{6,5},{9,10},{10,9},{13,14},{14,13},{17,18},{18,... | collective-permute-start | bytes 245768 | tf_op jit(solution)/shard_map/ppermute | solution.py:576
  10.7 7.2 %local_step.2 = (f32[9,8,64,256]{3,2,1,0:T(8,128)}, f32[2,10,80,128]{3,2,1,0:T(8,128)S(1)}, f32[9,2,8,64,128]{4,3,2,1,0:T(8,128)S(1)}, f32[9,2,8,64,128]{4,3,2,1,0:T(8,128)S(1)}, f32[8,2,64,128]{3,2,1,0:T(8,128)S(1)}) custom-call(f32[9,8,64,256]{3,2,1,0:T(8,128)} %cos.3, f32[9,8,64,256]{3,2,1,0:T(8,128)} %fld.2), custom_call_target="tpu_custom_call" | custom-call | flops 32768000 | bytes 14155776 | tf_op jit(solution)/shard_map/local_step/pallas_call | solution.py:238
  18.0 0.0 collective-permute-done.2.refs_4_
  18.0 0.0 collective-permute-done.3.refs_5_
  18.0 0.0 collective-permute-done.refs_2_.refs_3_.first_a
  18.0 0.0 collective-permute-done.1.refs_3_.refs_4_.first_b
  18.0 0.0 copy-start
  18.0 0.7 %fix_early.1 = (f32[9,2,8,64,128]{4,3,2,1,0:T(8,128)S(1)}, f32[8,2,64,128]{3,2,1,0:T(8,128)S(1)}, f32[2,88,128]{2,1,0:T(8,128)S(1)}, f32[2,88,128]{2,1,0:T(8,128)S(1)}) custom-call(f32[2,10,80,128]{3,2,1,0:T(8,128)S(1)} %get-tuple-element.31.refs_0_.refs_1_, ...), custom_call_target="tpu_custom_call", output_to_operand_aliasing={{0}: (6, {}), {1}: (7, {})} | custom-call | tf_op jit(solution)/shard_map/fix_early/pallas_call | solution.py:534
  18.7 0.1 collective-permute-start.4
  18.8 1.9 %collective-permute-start.5 = (f32[2,88,128]{2,1,0:T(8,128)S(1)}, f32[2,88,128]{2,1,0:T(8,128)S(1)}, u32[]{:S(2)}, u32[]{:S(2)}) collective-permute-start(f32[2,88,128]{2,1,0:T(8,128)S(1)} %get-tuple-element.45), channel_id=1, source_target_pairs={{1,2},{2,1},{5,6},{6,5},{9,10},{10,9},{13,14},{14,13},{17,18},{18,... | collective-permute-start | bytes 270344 | tf_op jit(solution)/shard_map/ppermute | solution.py:576
  20.8 0.0 copy-done
  20.8 2.8 %fix_late.1 = (f32[9,2,8,64,128]{4,3,2,1,0:T(8,128)S(1)}, f32[9,8,64,256]{3,2,1,0:T(8,128)}, f32[8,2,64,128]{3,2,1,0:T(8,128)S(1)}, f32[2,648,128]{2,1,0:T(8,128...) custom-call(s32[1,8,8]{2,1,0:T(8,128)S(1)} %copy-done, ...), custom_call_target="tpu_custom_call", output_to_operand_aliasing={{0}: (5, {}), {1}: (6, {}), {2}: (7, {})} | custom-call | tf_op jit(solution)/shard_map/fix_late/pallas_call | solution.py:548
  23.6 0.0 collective-permute-done.4.got_a
  23.6 0.5 collective-permute-done.5.got_b
  24.1 4.3 %collective-permute-start.6 = (f32[2,648,128]{2,1,0:T(8,128)S(1)}, f32[2,648,128]{2,1,0:T(8,128)S(1)}, u32[]{:S(2)}, u32[]{:S(2)}) collective-permute-start(f32[2,648,128]{2,1,0:T(8,128)S(1)} %get-tuple-element.51), channel_id=1, source_target_pairs={{0,4},{4,0},{8,12},{12,8},{16,20},{20,16},{24,28},{28,24},{32,36},... | collective-permute-start | bytes 1990664 | tf_op jit(solution)/shard_map/ppermute | solution.py:576
  28.4 1.9 %collective-permute-start.7 = (f32[2,648,128]{2,1,0:T(8,128)S(1)}, f32[2,648,128]{2,1,0:T(8,128)S(1)}, u32[]{:S(2)}, u32[]{:S(2)}) collective-permute-start(f32[2,648,128]{2,1,0:T(8,128)S(1)} %get-tuple-element.52), channel_id=1, source_target_pairs={{4,8},{8,4},{12,16},{16,12},{20,24},{24,20},{28,32},{32,28},{36,40... | collective-permute-start | bytes 1990664 | tf_op jit(solution)/shard_map/ppermute | solution.py:576
  30.3 8.1 %all-to-all-start = ((f32[32,8,256]{2,1,0:T(8,128)}), f32[32,8,256]{2,1,0:T(8,128)S(1)}, u32[]{:S(2)}, u32[]{:S(2)}) async-start(f32[32,8,256]{2,1,0:T(8,128)} %bitcast), calls=%async_computation | async-start | bytes 524288 | tf_op jit(solution)/shard_map/all_to_all | solution.py:599
  38.5 7.1 %local_step.3 = (f32[9,8,64,256]{3,2,1,0:T(8,128)}, f32[2,10,80,128]{3,2,1,0:T(8,128)S(1)}, f32[9,2,8,64,128]{4,3,2,1,0:T(8,128)S(1)}, f32[9,2,8,64,128]{4,3,2,1,0:T(8,128)S(1)}) custom-call(f32[9,8,64,256]{3,2,1,0:T(8,128)} %get-tuple-element.43.cos, f32[9,8,64,256]{3,2,1,0:T(8,128)} %fld.3, f32[2,16,128]{2,1,0:T(8,128)S(1)} %get-tuple-element.48.rest_0_), custom_call_target="tpu_custom_call" | custom-call | flops 32768000 | bytes 14155776 | tf_op jit(solution)/shard_map/local_step/pallas_call | solution.py:238
  45.5 0.0 collective-permute-done.6.refs_2_
  45.6 0.0 collective-permute-done.7.refs_3_
  45.6 2.0 %fix_whole.1 = (f32[9,2,8,64,128]{4,3,2,1,0:T(8,128)S(1)}, f32[9,8,64,256]{3,2,1,0:T(8,128)}) custom-call(f32[2,10,80,128]{3,2,1,0:T(8,128)S(1)} %get-tuple-element.49.refs_0_, f32[9,2,8,64,128]{4,3,2,1,0:T(8,128)S(1)} %get-tuple-element.50.refs_1_, f32[2,648,128]{2,1,0:T(8,128)S(1)} %collective-permute-done.6.refs_2_, ...), custom_call_target="tpu_custom_call", output_to_operand_aliasing={{0}: (6, {}), {1}: (7, {})} | custom-call | tf_op jit(solution)/shard_map/fix_whole/pallas_call | solution.py:561
  47.6 0.0 all-to-all-done
  47.6 0.6 %reduce_sum.9 = f32[8,256]{1,0:T(8,128)} reduce(f32[32,8,256]{2,1,0:T(8,128)S(1)} %all-to-all-done, f32[]{:T(128)} %constant.0.clone.1), dimensions={0}, to_apply=%region_0.0 | reduce | flops 63488 | bytes 270340 | tf_op jit(solution)/shard_map/reduce_sum | solution.py:606
  (1 shorter events, 0.0 us)
Async XLA Ops:
  2.4 15.6 %collective-permute-start = (f32[2,640,128]{2,1,0:T(8,128)S(1)}, f32[2,640,128]{2,1,0:T(8,128)S(1)}, u32[]{:S(2)}, u32[]{:S(2)}) collective-permute-start(f32[2,640,128]{2,1,0:T(8,128)S(1)} %get-tuple-element.33), channel_id=1, source_target_pairs={{0,4},{4,0},{8,12},{12,8},{16,20},{20,16},{24,28},{28,24},{32,36},... | collective-permute-start | bytes 1966088 | tf_op jit(solution)/shard_map/ppermute | solution.py:576
  3.2 14.8 %collective-permute-start.1 = (f32[2,640,128]{2,1,0:T(8,128)S(1)}, f32[2,640,128]{2,1,0:T(8,128)S(1)}, u32[]{:S(2)}, u32[]{:S(2)}) collective-permute-start(f32[2,640,128]{2,1,0:T(8,128)S(1)} %get-tuple-element.34), channel_id=1, source_target_pairs={{4,8},{8,4},{12,16},{16,12},{20,24},{24,20},{28,32},{32,28},{36,40... | collective-permute-start | bytes 1966088 | tf_op jit(solution)/shard_map/ppermute | solution.py:576
  6.6 11.3 %collective-permute-start.2 = (f32[2,80,128]{2,1,0:T(8,128)S(1)}, f32[2,80,128]{2,1,0:T(8,128)S(1)}, u32[]{:S(2)}, u32[]{:S(2)}) collective-permute-start(f32[2,80,128]{2,1,0:T(8,128)S(1)} %get-tuple-element.35), channel_id=1, source_target_pairs={{0,1},{1,0},{2,3},{3,2},{4,5},{5,4},{6,7},{7,6},{8,9},{9,8},{10,11... | collective-permute-start | bytes 245768 | tf_op jit(solution)/shard_map/ppermute | solution.py:576
  7.0 11.0 %collective-permute-start.3 = (f32[2,80,128]{2,1,0:T(8,128)S(1)}, f32[2,80,128]{2,1,0:T(8,128)S(1)}, u32[]{:S(2)}, u32[]{:S(2)}) collective-permute-start(f32[2,80,128]{2,1,0:T(8,128)S(1)} %get-tuple-element.36), channel_id=1, source_target_pairs={{1,2},{2,1},{5,6},{6,5},{9,10},{10,9},{13,14},{14,13},{17,18},{18,... | collective-permute-start | bytes 245768 | tf_op jit(solution)/shard_map/ppermute | solution.py:576
  18.0 2.8 %copy-start = (s32[1,8,8]{2,1,0:T(8,128)S(1)}, s32[1,8,8]{2,1,0:T(8,128)}, u32[]{:S(2)}) copy-start(s32[1,8,8]{2,1,0:T(8,128)} %refs_0_.1) | copy-start | bytes 772
  18.7 4.9 %collective-permute-start.4 = (f32[2,88,128]{2,1,0:T(8,128)S(1)}, f32[2,88,128]{2,1,0:T(8,128)S(1)}, u32[]{:S(2)}, u32[]{:S(2)}) collective-permute-start(f32[2,88,128]{2,1,0:T(8,128)S(1)} %get-tuple-element.44), channel_id=1, source_target_pairs={{0,1},{1,0},{2,3},{3,2},{4,5},{5,4},{6,7},{7,6},{8,9},{9,8},{10,11... | collective-permute-start | bytes 270344 | tf_op jit(solution)/shard_map/ppermute | solution.py:576
  18.8 5.3 %collective-permute-start.5 = (f32[2,88,128]{2,1,0:T(8,128)S(1)}, f32[2,88,128]{2,1,0:T(8,128)S(1)}, u32[]{:S(2)}, u32[]{:S(2)}) collective-permute-start(f32[2,88,128]{2,1,0:T(8,128)S(1)} %get-tuple-element.45), channel_id=1, source_target_pairs={{1,2},{2,1},{5,6},{6,5},{9,10},{10,9},{13,14},{14,13},{17,18},{18,... | collective-permute-start | bytes 270344 | tf_op jit(solution)/shard_map/ppermute | solution.py:576
  24.1 21.4 %collective-permute-start.6 = (f32[2,648,128]{2,1,0:T(8,128)S(1)}, f32[2,648,128]{2,1,0:T(8,128)S(1)}, u32[]{:S(2)}, u32[]{:S(2)}) collective-permute-start(f32[2,648,128]{2,1,0:T(8,128)S(1)} %get-tuple-element.51), channel_id=1, source_target_pairs={{0,4},{4,0},{8,12},{12,8},{16,20},{20,16},{24,28},{28,24},{32,36},... | collective-permute-start | bytes 1990664 | tf_op jit(solution)/shard_map/ppermute | solution.py:576
  28.4 17.1 %collective-permute-start.7 = (f32[2,648,128]{2,1,0:T(8,128)S(1)}, f32[2,648,128]{2,1,0:T(8,128)S(1)}, u32[]{:S(2)}, u32[]{:S(2)}) collective-permute-start(f32[2,648,128]{2,1,0:T(8,128)S(1)} %get-tuple-element.52), channel_id=1, source_target_pairs={{4,8},{8,4},{12,16},{16,12},{20,24},{24,20},{28,32},{32,28},{36,40... | collective-permute-start | bytes 1990664 | tf_op jit(solution)/shard_map/ppermute | solution.py:576
  30.3 17.2 %all-to-all-start = ((f32[32,8,256]{2,1,0:T(8,128)}), f32[32,8,256]{2,1,0:T(8,128)S(1)}, u32[]{:S(2)}, u32[]{:S(2)}) async-start(f32[32,8,256]{2,1,0:T(8,128)} %bitcast), calls=%async_computation | async-start | bytes 524288 | tf_op jit(solution)/shard_map/all_to_all | solution.py:599

commit v6 on v5

--- a/solution.py
+++ b/solution.py
@@ -139,24 +139,22 @@
                 for k, x in ((0, 1), (1, CX)):
                     density_value[h, x, y : y + 1, :] += corners[h, edge + k : edge + k + 1, :]
 
-    def potential_plane(x, carry):
+    def potential_plane(x):
         for part in range(CY // 8):
             row = PAD + part * 8
             own, total = around(density_value, x, row)
             for h in BOTH:
                 potential[h, x + 1, row : row + 8, :] = DT * total[h] - (6.0 * DT) * own[h]
-        return carry
-
-    lax.fori_loop(0, CX, potential_plane, 0)
+
+    for x in range(CX):
+        potential_plane(x)
 
     for h in BOTH:
         copy_e(0, h).wait()
 
-    def step_plane(x, carry):
-        @pl.when(x < CX - 1)
-        def _():
-            for h in BOTH:
-                copy_e(x + 1, h).wait()
+    def step_plane(x):
+        for h in BOTH if x < CX - 1 else ():
+            copy_e(x + 1, h).wait()
 
         for h in BOTH:
             copy_f(x, h).wait()
@@ -205,19 +203,14 @@
                     if with_sums:
                         sums[s, h, here, :] += lam[h] + new
 
-        @pl.when((x > 0) & (x < CX - 1))
-        def _():
-            for h in BOTH:
-                copy_o(x, h).start()
-
-        @pl.when((x > 1) & (x < CX - 2))
-        def _():
-            for h in BOTH:
-                copy_d(x, h).start()
-
-        return carry
-
-    lax.fori_loop(0, CX, step_plane, 0)
+        for h in BOTH if 0 < x < CX - 1 else ():
+            copy_o(x, h).start()
+
+        for h in BOTH if 1 < x < CX - 2 else ():
+            copy_d(x, h).start()
+
+    for x in range(CX):
+        step_plane(x)
     for h in BOTH:
         for x in range(1, CX - 1):
             copy_o(x, h).wait()

time: 48.5 us -> 47.6 us (0.981); the launches traced: 48.2 us -> 46.8 us
  Pallas kernels: 21.6 us -> 20.2 us
    pallas_call x2, Pallas kernels: 14.3 us -> 12.9 us  [local_step(): pl.pallas_call(functools.partial(local_kernel, with_sums), out_shape=[WHO...]
  transfers between devices with their start and end apart: 9 -> 9, of which waited for: 1 -> 1; matrix products, arithmetic and copies ran while one was open for 0% -> 0% of each run, Pallas kernels for 40% -> 38%
where the time goes in v6:
time: 47.6 us; the launch traced here: 46.8 us
  starting transfers between devices  24.8 us (52%)
  Pallas kernels  20.2 us (42%)
  between operations  0.81 us (2%)
  other arithmetic  0.63 us (1%)
    ppermute x8, starting transfers between devices, swaps(): return (lax.ppermute(first, axis, near), lax.ppermute(second, axis, far))  16.6 us
    pallas_call x2, Pallas kernels, local_step(): pl.pallas_call(functools.partial(local_kernel, with_sums), out_shape=[WHO...  12.9 us
    all_to_all x1, starting transfers between devices, shards(): lax.all_to_all(rows.reshape(n_gx, GRAIN_DEV, NZ), 'gx', split_axis=0, con...  8.15 us
    pallas_call x1, Pallas kernels, fix_late(): pl.pallas_call(functools.partial(fix_kernel, sizes, 'late'), out_shape=[B...  2.84 us
    pallas_call x1, Pallas kernels, fix_whole(): pl.pallas_call(functools.partial(fix_kernel, sizes, 'whole'), out_shape=[...  2 us
    pallas_call x1, Pallas kernels, pack(): pl.pallas_call(pack_kernel, out_shape=[face_message(0)] * 2 + [side_messa...  1.79 us
  transfers between devices with their start and end apart: 9, of which 1 were waited for; matrix products, arithmetic and copies ran while one was open for 0% of the time, Pallas kernels for 38%

profile of v6, /device:TPU:11, one launch (start us, length us, event | category | flops | bytes accessed | tf_op | source)
XLA Modules:
  0.0 46.8 jit_solution(15261827926542577151)
XLA Ops:
  0.6 1.8 %pack.1 = (f32[2,640,128]{2,1,0:T(8,128)S(1)}, f32[2,640,128]{2,1,0:T(8,128)S(1)}, f32[2,80,128]{2,1,0:T(8,128)S(1)}, f32[2,80,128]{2,1,0:T(8,128)S(1)}) custom-call(f32[9,8,64,256]{3,2,1,0:T(8,128)} %cos.3), custom_call_target="tpu_custom_call" | custom-call | tf_op jit(solution)/shard_map/pack/pallas_call | solution.py:299
  2.4 0.8 %collective-permute-start = (f32[2,640,128]{2,1,0:T(8,128)S(1)}, f32[2,640,128]{2,1,0:T(8,128)S(1)}, u32[]{:S(2)}, u32[]{:S(2)}) collective-permute-start(f32[2,640,128]{2,1,0:T(8,128)S(1)} %get-tuple-element.33), channel_id=1, source_target_pairs={{0,4},{4,0},{8,12},{12,8},{16,20},{20,16},{24,28},{28,24},{32,36},... | collective-permute-start | bytes 1966088 | tf_op jit(solution)/shard_map/ppermute | solution.py:569
  3.2 3.4 %collective-permute-start.1 = (f32[2,640,128]{2,1,0:T(8,128)S(1)}, f32[2,640,128]{2,1,0:T(8,128)S(1)}, u32[]{:S(2)}, u32[]{:S(2)}) collective-permute-start(f32[2,640,128]{2,1,0:T(8,128)S(1)} %get-tuple-element.34), channel_id=1, source_target_pairs={{4,8},{8,4},{12,16},{16,12},{20,24},{24,20},{28,32},{32,28},{36,40... | collective-permute-start | bytes 1966088 | tf_op jit(solution)/shard_map/ppermute | solution.py:569
  6.6 0.3 collective-permute-start.2
  7.0 3.8 %collective-permute-start.3 = (f32[2,80,128]{2,1,0:T(8,128)S(1)}, f32[2,80,128]{2,1,0:T(8,128)S(1)}, u32[]{:S(2)}, u32[]{:S(2)}) collective-permute-start(f32[2,80,128]{2,1,0:T(8,128)S(1)} %get-tuple-element.36), channel_id=1, source_target_pairs={{1,2},{2,1},{5,6},{6,5},{9,10},{10,9},{13,14},{14,13},{17,18},{18,... | collective-permute-start | bytes 245768 | tf_op jit(solution)/shard_map/ppermute | solution.py:569
  10.7 6.5 %local_step.2 = (f32[9,8,64,256]{3,2,1,0:T(8,128)}, f32[2,10,80,128]{3,2,1,0:T(8,128)S(1)}, f32[9,2,8,64,128]{4,3,2,1,0:T(8,128)S(1)}, f32[9,2,8,64,128]{4,3,2,1,0:T(8,128)S(1)}, f32[8,2,64,128]{3,2,1,0:T(8,128)S(1)}) custom-call(f32[9,8,64,256]{3,2,1,0:T(8,128)} %cos.3, f32[9,8,64,256]{3,2,1,0:T(8,128)} %fld.2), custom_call_target="tpu_custom_call" | custom-call | flops 32768000 | bytes 14155776 | tf_op jit(solution)/shard_map/local_step/pallas_call | solution.py:231
  17.3 0.0 collective-permute-done.2.refs_4_
  17.3 0.0 collective-permute-done.3.refs_5_
  17.3 0.0 collective-permute-done.refs_2_.refs_3_.first_a
  17.3 0.0 collective-permute-done.1.refs_3_.refs_4_.first_b
  17.3 0.0 copy-start
  17.3 0.7 %fix_early.1 = (f32[9,2,8,64,128]{4,3,2,1,0:T(8,128)S(1)}, f32[8,2,64,128]{3,2,1,0:T(8,128)S(1)}, f32[2,88,128]{2,1,0:T(8,128)S(1)}, f32[2,88,128]{2,1,0:T(8,128)S(1)}) custom-call(f32[2,10,80,128]{3,2,1,0:T(8,128)S(1)} %get-tuple-element.31.refs_0_.refs_1_, ...), custom_call_target="tpu_custom_call", output_to_operand_aliasing={{0}: (6, {}), {1}: (7, {})} | custom-call | tf_op jit(solution)/shard_map/fix_early/pallas_call | solution.py:527
  18.0 0.1 collective-permute-start.4
  18.1 2.1 %collective-permute-start.5 = (f32[2,88,128]{2,1,0:T(8,128)S(1)}, f32[2,88,128]{2,1,0:T(8,128)S(1)}, u32[]{:S(2)}, u32[]{:S(2)}) collective-permute-start(f32[2,88,128]{2,1,0:T(8,128)S(1)} %get-tuple-element.45), channel_id=1, source_target_pairs={{1,2},{2,1},{5,6},{6,5},{9,10},{10,9},{13,14},{14,13},{17,18},{18,... | collective-permute-start | bytes 270344 | tf_op jit(solution)/shard_map/ppermute | solution.py:569
  20.2 0.0 copy-done
  20.2 2.8 %fix_late.1 = (f32[9,2,8,64,128]{4,3,2,1,0:T(8,128)S(1)}, f32[9,8,64,256]{3,2,1,0:T(8,128)}, f32[8,2,64,128]{3,2,1,0:T(8,128)S(1)}, f32[2,648,128]{2,1,0:T(8,128...) custom-call(s32[1,8,8]{2,1,0:T(8,128)S(1)} %copy-done, ...), custom_call_target="tpu_custom_call", output_to_operand_aliasing={{0}: (5, {}), {1}: (6, {}), {2}: (7, {})} | custom-call | tf_op jit(solution)/shard_map/fix_late/pallas_call | solution.py:541
  23.1 0.0 collective-permute-done.4.got_a
  23.1 0.3 collective-permute-done.5.got_b
  23.4 4.3 %collective-permute-start.6 = (f32[2,648,128]{2,1,0:T(8,128)S(1)}, f32[2,648,128]{2,1,0:T(8,128)S(1)}, u32[]{:S(2)}, u32[]{:S(2)}) collective-permute-start(f32[2,648,128]{2,1,0:T(8,128)S(1)} %get-tuple-element.51), channel_id=1, source_target_pairs={{0,4},{4,0},{8,12},{12,8},{16,20},{20,16},{24,28},{28,24},{32,36},... | collective-permute-start | bytes 1990664 | tf_op jit(solution)/shard_map/ppermute | solution.py:569
  27.7 1.9 %collective-permute-start.7 = (f32[2,648,128]{2,1,0:T(8,128)S(1)}, f32[2,648,128]{2,1,0:T(8,128)S(1)}, u32[]{:S(2)}, u32[]{:S(2)}) collective-permute-start(f32[2,648,128]{2,1,0:T(8,128)S(1)} %get-tuple-element.52), channel_id=1, source_target_pairs={{4,8},{8,4},{12,16},{16,12},{20,24},{24,20},{28,32},{32,28},{36,40... | collective-permute-start | bytes 1990664 | tf_op jit(solution)/shard_map/ppermute | solution.py:569
  29.6 8.2 %all-to-all-start = ((f32[32,8,256]{2,1,0:T(8,128)}), f32[32,8,256]{2,1,0:T(8,128)S(1)}, u32[]{:S(2)}, u32[]{:S(2)}) async-start(f32[32,8,256]{2,1,0:T(8,128)} %bitcast), calls=%async_computation | async-start | bytes 524288 | tf_op jit(solution)/shard_map/all_to_all | solution.py:592
  37.8 6.3 %local_step.3 = (f32[9,8,64,256]{3,2,1,0:T(8,128)}, f32[2,10,80,128]{3,2,1,0:T(8,128)S(1)}, f32[9,2,8,64,128]{4,3,2,1,0:T(8,128)S(1)}, f32[9,2,8,64,128]{4,3,2,1,0:T(8,128)S(1)}) custom-call(f32[9,8,64,256]{3,2,1,0:T(8,128)} %get-tuple-element.43.cos, f32[9,8,64,256]{3,2,1,0:T(8,128)} %fld.3, f32[2,16,128]{2,1,0:T(8,128)S(1)} %get-tuple-element.48.rest_0_), custom_call_target="tpu_custom_call" | custom-call | flops 32768000 | bytes 14155776 | tf_op jit(solution)/shard_map/local_step/pallas_call | solution.py:231
  44.1 0.0 collective-permute-done.6.refs_2_
  44.2 0.0 collective-permute-done.7.refs_3_
  44.2 2.0 %fix_whole.1 = (f32[9,2,8,64,128]{4,3,2,1,0:T(8,128)S(1)}, f32[9,8,64,256]{3,2,1,0:T(8,128)}) custom-call(f32[2,10,80,128]{3,2,1,0:T(8,128)S(1)} %get-tuple-element.49.refs_0_, f32[9,2,8,64,128]{4,3,2,1,0:T(8,128)S(1)} %get-tuple-element.50.refs_1_, f32[2,648,128]{2,1,0:T(8,128)S(1)} %collective-permute-done.6.refs_2_, ...), custom_call_target="tpu_custom_call", output_to_operand_aliasing={{0}: (6, {}), {1}: (7, {})} | custom-call | tf_op jit(solution)/shard_map/fix_whole/pallas_call | solution.py:554
  46.2 0.0 all-to-all-done
  46.2 0.6 %reduce_sum.9 = f32[8,256]{1,0:T(8,128)} reduce(f32[32,8,256]{2,1,0:T(8,128)S(1)} %all-to-all-done, f32[]{:T(128)} %constant.0.clone.1), dimensions={0}, to_apply=%region_0.0 | reduce | flops 63488 | bytes 270340 | tf_op jit(solution)/shard_map/reduce_sum | solution.py:599
  (1 shorter events, 0.0 us)
Async XLA Ops:
  2.4 14.9 %collective-permute-start = (f32[2,640,128]{2,1,0:T(8,128)S(1)}, f32[2,640,128]{2,1,0:T(8,128)S(1)}, u32[]{:S(2)}, u32[]{:S(2)}) collective-permute-start(f32[2,640,128]{2,1,0:T(8,128)S(1)} %get-tuple-element.33), channel_id=1, source_target_pairs={{0,4},{4,0},{8,12},{12,8},{16,20},{20,16},{24,28},{28,24},{32,36},... | collective-permute-start | bytes 1966088 | tf_op jit(solution)/shard_map/ppermute | solution.py:569
  3.2 14.1 %collective-permute-start.1 = (f32[2,640,128]{2,1,0:T(8,128)S(1)}, f32[2,640,128]{2,1,0:T(8,128)S(1)}, u32[]{:S(2)}, u32[]{:S(2)}) collective-permute-start(f32[2,640,128]{2,1,0:T(8,128)S(1)} %get-tuple-element.34), channel_id=1, source_target_pairs={{4,8},{8,4},{12,16},{16,12},{20,24},{24,20},{28,32},{32,28},{36,40... | collective-permute-start | bytes 1966088 | tf_op jit(solution)/shard_map/ppermute | solution.py:569
  6.6 10.6 %collective-permute-start.2 = (f32[2,80,128]{2,1,0:T(8,128)S(1)}, f32[2,80,128]{2,1,0:T(8,128)S(1)}, u32[]{:S(2)}, u32[]{:S(2)}) collective-permute-start(f32[2,80,128]{2,1,0:T(8,128)S(1)} %get-tuple-element.35), channel_id=1, source_target_pairs={{0,1},{1,0},{2,3},{3,2},{4,5},{5,4},{6,7},{7,6},{8,9},{9,8},{10,11... | collective-permute-start | bytes 245768 | tf_op jit(solution)/shard_map/ppermute | solution.py:569
  7.0 10.3 %collective-permute-start.3 = (f32[2,80,128]{2,1,0:T(8,128)S(1)}, f32[2,80,128]{2,1,0:T(8,128)S(1)}, u32[]{:S(2)}, u32[]{:S(2)}) collective-permute-start(f32[2,80,128]{2,1,0:T(8,128)S(1)} %get-tuple-element.36), channel_id=1, source_target_pairs={{1,2},{2,1},{5,6},{6,5},{9,10},{10,9},{13,14},{14,13},{17,18},{18,... | collective-permute-start | bytes 245768 | tf_op jit(solution)/shard_map/ppermute | solution.py:569
  17.3 2.9 %copy-start = (s32[1,8,8]{2,1,0:T(8,128)S(1)}, s32[1,8,8]{2,1,0:T(8,128)}, u32[]{:S(2)}) copy-start(s32[1,8,8]{2,1,0:T(8,128)} %refs_0_.1) | copy-start | bytes 772
  18.0 5.0 %collective-permute-start.4 = (f32[2,88,128]{2,1,0:T(8,128)S(1)}, f32[2,88,128]{2,1,0:T(8,128)S(1)}, u32[]{:S(2)}, u32[]{:S(2)}) collective-permute-start(f32[2,88,128]{2,1,0:T(8,128)S(1)} %get-tuple-element.44), channel_id=1, source_target_pairs={{0,1},{1,0},{2,3},{3,2},{4,5},{5,4},{6,7},{7,6},{8,9},{9,8},{10,11... | collective-permute-start | bytes 270344 | tf_op jit(solution)/shard_map/ppermute | solution.py:569
  18.1 5.3 %collective-permute-start.5 = (f32[2,88,128]{2,1,0:T(8,128)S(1)}, f32[2,88,128]{2,1,0:T(8,128)S(1)}, u32[]{:S(2)}, u32[]{:S(2)}) collective-permute-start(f32[2,88,128]{2,1,0:T(8,128)S(1)} %get-tuple-element.45), channel_id=1, source_target_pairs={{1,2},{2,1},{5,6},{6,5},{9,10},{10,9},{13,14},{14,13},{17,18},{18,... | collective-permute-start | bytes 270344 | tf_op jit(solution)/shard_map/ppermute | solution.py:569
  23.4 20.7 %collective-permute-start.6 = (f32[2,648,128]{2,1,0:T(8,128)S(1)}, f32[2,648,128]{2,1,0:T(8,128)S(1)}, u32[]{:S(2)}, u32[]{:S(2)}) collective-permute-start(f32[2,648,128]{2,1,0:T(8,128)S(1)} %get-tuple-element.51), channel_id=1, source_target_pairs={{0,4},{4,0},{8,12},{12,8},{16,20},{20,16},{24,28},{28,24},{32,36},... | collective-permute-start | bytes 1990664 | tf_op jit(solution)/shard_map/ppermute | solution.py:569
  27.7 16.4 %collective-permute-start.7 = (f32[2,648,128]{2,1,0:T(8,128)S(1)}, f32[2,648,128]{2,1,0:T(8,128)S(1)}, u32[]{:S(2)}, u32[]{:S(2)}) collective-permute-start(f32[2,648,128]{2,1,0:T(8,128)S(1)} %get-tuple-element.52), channel_id=1, source_target_pairs={{4,8},{8,4},{12,16},{16,12},{20,24},{24,20},{28,32},{32,28},{36,40... | collective-permute-start | bytes 1990664 | tf_op jit(solution)/shard_map/ppermute | solution.py:569
  29.6 16.5 %all-to-all-start = ((f32[32,8,256]{2,1,0:T(8,128)}), f32[32,8,256]{2,1,0:T(8,128)S(1)}, u32[]{:S(2)}, u32[]{:S(2)}) async-start(f32[32,8,256]{2,1,0:T(8,128)} %bitcast), calls=%async_computation | async-start | bytes 524288 | tf_op jit(solution)/shard_map/all_to_all | solution.py:592

commit v7 on v6

--- a/solution.py
+++ b/solution.py
@@ -43,7 +43,7 @@
 
 
 def even_place():
-    return tuple(lax.rem(lax.axis_index(axis), 2) == 0 for axis in ("gx", "gy"))
+    return lax.rem(lax.axis_index("gx"), 2) == 1, lax.rem(lax.axis_index("gy"), 2) == 1
 
 
 def has_neighbours(axis, count):
@@ -483,6 +483,8 @@
                 )
                 work[0, h, inner, span, :] -= part[h]
                 twelve.append(12.0 * part[h])
+            store(0, x, slice(0, CY))
+            store(0, inner, slice(0, CY))
             for s in range(1, NF):
                 for h in BOTH:
                     eta = field[s, h, x, span, :]
@@ -490,8 +492,8 @@
                     work[s, h, x, span, :] += change
                     if sums is not None:
                         sums[s - 1, h, span, :] += change
-        store(slice(0, NF), x, slice(0, CY))
-        store(0, inner, slice(0, CY))
+                if s % 4 == 0:
+                    store(slice(s - 3, s + 1), x, slice(0, CY))
 
     for h in BOTH:
         for k in range(SLOTS + 2):
@@ -520,7 +522,7 @@
 
 
 EDGE = pltpu.VMEM((HALF, ROWS, LN), F32)
-STORES = pltpu.SemaphoreType.DMA((16,))
+STORES = pltpu.SemaphoreType.DMA((24,))
 
 
 def fix_early(sizes, value, field, got_faces, got_sides, base, sums):
@@ -566,7 +568,8 @@
 def swaps(axis, count, first, second):
     near = [(i, i ^ 1) for i in range(count)]
     far = [(i, ((i + 1) ^ 1) - 1) for i in range(1, count - 1)]
-    return lax.ppermute(first, axis, near), lax.ppermute(second, axis, far)
+    pairs = far, near
+    return lax.ppermute(first, axis, pairs[0]), lax.ppermute(second, axis, pairs[1])
 
 
 def shards(n_gx, n_gy, cotangent, fields_one, fields_zero, slot_grain):

time: 47.6 us -> 47.4 us (level)
  the two profiles are of different devices: /device:TPU:11 before, /device:TPU:1 now
where the time goes in v7:
time: 47.4 us; the launch traced here: 47.2 us
  starting transfers between devices  24.8 us (52%)
  Pallas kernels  20.2 us (43%)
  between operations  0.81 us (2%)
  waiting for transfers between devices  0.68 us (1%)
  other arithmetic  0.63 us (1%)
    pallas_call x2, Pallas kernels, local_step(): pl.pallas_call(functools.partial(local_kernel, with_sums), out_shape=[WHO...  12.8 us
    ppermute x4, starting transfers between devices, swaps(): lax.ppermute(first, axis, pairs[0])  11 us
    all_to_all x1, starting transfers between devices, shards(): lax.all_to_all(rows.reshape(n_gx, GRAIN_DEV, NZ), 'gx', split_axis=0, con...  8.25 us
    ppermute x4, starting transfers between devices, swaps(): lax.ppermute(second, axis, pairs[1])  5.52 us
    pallas_call x1, Pallas kernels, fix_late(): pl.pallas_call(functools.partial(fix_kernel, sizes, 'late'), out_shape=[B...  2.91 us
    pallas_call x1, Pallas kernels, fix_whole(): pl.pallas_call(functools.partial(fix_kernel, sizes, 'whole'), out_shape=[...  1.95 us
    pallas_call x1, Pallas kernels, pack(): pl.pallas_call(pack_kernel, out_shape=[face_message(0)] * 2 + [side_messa...  1.79 us
  transfers between devices with their start and end apart: 9, of which 1 were waited for; matrix products, arithmetic and copies ran while one was open for 0% of the time, Pallas kernels for 37%

profile of v7, /device:TPU:1, one launch (start us, length us, event | category | flops | bytes accessed | tf_op | source)
XLA Modules:
  0.0 47.2 jit_solution(4741228756113275247)
XLA Ops:
  0.6 1.8 %pack.1 = (f32[2,640,128]{2,1,0:T(8,128)S(1)}, f32[2,640,128]{2,1,0:T(8,128)S(1)}, f32[2,80,128]{2,1,0:T(8,128)S(1)}, f32[2,80,128]{2,1,0:T(8,128)S(1)}) custom-call(f32[9,8,64,256]{3,2,1,0:T(8,128)} %cos.3), custom_call_target="tpu_custom_call" | custom-call | tf_op jit(solution)/shard_map/pack/pallas_call | solution.py:299
  2.4 4.9 %collective-permute-start = (f32[2,640,128]{2,1,0:T(8,128)S(1)}, f32[2,640,128]{2,1,0:T(8,128)S(1)}, u32[]{:S(2)}, u32[]{:S(2)}) collective-permute-start(f32[2,640,128]{2,1,0:T(8,128)S(1)} %get-tuple-element.33), channel_id=1, source_target_pairs={{4,8},{8,4},{12,16},{16,12},{20,24},{24,20},{28,32},{32,28},{36,40... | collective-permute-start | bytes 1966088 | tf_op jit(solution)/shard_map/ppermute | solution.py:572
  7.4 0.1 collective-permute-start.1
  7.5 0.7 %collective-permute-start.2 = (f32[2,80,128]{2,1,0:T(8,128)S(1)}, f32[2,80,128]{2,1,0:T(8,128)S(1)}, u32[]{:S(2)}, u32[]{:S(2)}) collective-permute-start(f32[2,80,128]{2,1,0:T(8,128)S(1)} %get-tuple-element.35), channel_id=1, source_target_pairs={{1,2},{2,1},{5,6},{6,5},{9,10},{10,9},{13,14},{14,13},{17,18},{18,... | collective-permute-start | bytes 245768 | tf_op jit(solution)/shard_map/ppermute | solution.py:572
  8.1 3.7 %collective-permute-start.3 = (f32[2,80,128]{2,1,0:T(8,128)S(1)}, f32[2,80,128]{2,1,0:T(8,128)S(1)}, u32[]{:S(2)}, u32[]{:S(2)}) collective-permute-start(f32[2,80,128]{2,1,0:T(8,128)S(1)} %get-tuple-element.36), channel_id=1, source_target_pairs={{0,1},{1,0},{2,3},{3,2},{4,5},{5,4},{6,7},{7,6},{8,9},{9,8},{10,11... | collective-permute-start | bytes 245768 | tf_op jit(solution)/shard_map/ppermute | solution.py:572
  11.9 6.5 %local_step.2 = (f32[9,8,64,256]{3,2,1,0:T(8,128)}, f32[2,10,80,128]{3,2,1,0:T(8,128)S(1)}, f32[9,2,8,64,128]{4,3,2,1,0:T(8,128)S(1)}, f32[9,2,8,64,128]{4,3,2,1,0:T(8,128)S(1)}, f32[8,2,64,128]{3,2,1,0:T(8,128)S(1)}) custom-call(f32[9,8,64,256]{3,2,1,0:T(8,128)} %cos.3, f32[9,8,64,256]{3,2,1,0:T(8,128)} %fld.2), custom_call_target="tpu_custom_call" | custom-call | flops 32768000 | bytes 14155776 | tf_op jit(solution)/shard_map/local_step/pallas_call | solution.py:231
  18.4 0.0 collective-permute-done.2.refs_4_
  18.4 0.0 collective-permute-done.3.refs_5_
  18.4 0.0 collective-permute-done.refs_2_.refs_3_.first_a
  18.4 0.0 collective-permute-done.1.refs_3_.refs_4_.first_b
  18.4 0.0 copy-start
  18.4 0.7 %fix_early.1 = (f32[9,2,8,64,128]{4,3,2,1,0:T(8,128)S(1)}, f32[8,2,64,128]{3,2,1,0:T(8,128)S(1)}, f32[2,88,128]{2,1,0:T(8,128)S(1)}, f32[2,88,128]{2,1,0:T(8,128)S(1)}) custom-call(f32[2,10,80,128]{3,2,1,0:T(8,128)S(1)} %get-tuple-element.31.refs_0_.refs_1_, ...), custom_call_target="tpu_custom_call", output_to_operand_aliasing={{0}: (6, {}), {1}: (7, {})} | custom-call | tf_op jit(solution)/shard_map/fix_early/pallas_call | solution.py:529
  19.2 0.7 %collective-permute-start.4 = (f32[2,88,128]{2,1,0:T(8,128)S(1)}, f32[2,88,128]{2,1,0:T(8,128)S(1)}, u32[]{:S(2)}, u32[]{:S(2)}) collective-permute-start(f32[2,88,128]{2,1,0:T(8,128)S(1)} %get-tuple-element.44), channel_id=1, source_target_pairs={{1,2},{2,1},{5,6},{6,5},{9,10},{10,9},{13,14},{14,13},{17,18},{18,... | collective-permute-start | bytes 270344 | tf_op jit(solution)/shard_map/ppermute | solution.py:572
  19.8 1.6 %collective-permute-start.5 = (f32[2,88,128]{2,1,0:T(8,128)S(1)}, f32[2,88,128]{2,1,0:T(8,128)S(1)}, u32[]{:S(2)}, u32[]{:S(2)}) collective-permute-start(f32[2,88,128]{2,1,0:T(8,128)S(1)} %get-tuple-element.45), channel_id=1, source_target_pairs={{0,1},{1,0},{2,3},{3,2},{4,5},{5,4},{6,7},{7,6},{8,9},{9,8},{10,11... | collective-permute-start | bytes 270344 | tf_op jit(solution)/shard_map/ppermute | solution.py:572
  21.4 0.0 copy-done
  21.4 2.9 %fix_late.1 = (f32[9,2,8,64,128]{4,3,2,1,0:T(8,128)S(1)}, f32[9,8,64,256]{3,2,1,0:T(8,128)}, f32[8,2,64,128]{3,2,1,0:T(8,128)S(1)}, f32[2,648,128]{2,1,0:T(8,128...) custom-call(s32[1,8,8]{2,1,0:T(8,128)S(1)} %copy-done, ...), custom_call_target="tpu_custom_call", output_to_operand_aliasing={{0}: (5, {}), {1}: (6, {}), {2}: (7, {})} | custom-call | tf_op jit(solution)/shard_map/fix_late/pallas_call | solution.py:543
  24.4 0.0 collective-permute-done.4.got_a
  24.4 0.0 collective-permute-done.5.got_b
  24.4 4.8 %collective-permute-start.6 = (f32[2,648,128]{2,1,0:T(8,128)S(1)}, f32[2,648,128]{2,1,0:T(8,128)S(1)}, u32[]{:S(2)}, u32[]{:S(2)}) collective-permute-start(f32[2,648,128]{2,1,0:T(8,128)S(1)} %get-tuple-element.51), channel_id=1, source_target_pairs={{4,8},{8,4},{12,16},{16,12},{20,24},{24,20},{28,32},{32,28},{36,40... | collective-permute-start | bytes 1990664 | tf_op jit(solution)/shard_map/ppermute | solution.py:572
  29.2 0.1 collective-permute-start.7
  29.3 8.3 %all-to-all-start = ((f32[32,8,256]{2,1,0:T(8,128)}), f32[32,8,256]{2,1,0:T(8,128)S(1)}, u32[]{:S(2)}, u32[]{:S(2)}) async-start(f32[32,8,256]{2,1,0:T(8,128)} %bitcast), calls=%async_computation | async-start | bytes 524288 | tf_op jit(solution)/shard_map/all_to_all | solution.py:595
  37.5 6.3 %local_step.3 = (f32[9,8,64,256]{3,2,1,0:T(8,128)}, f32[2,10,80,128]{3,2,1,0:T(8,128)S(1)}, f32[9,2,8,64,128]{4,3,2,1,0:T(8,128)S(1)}, f32[9,2,8,64,128]{4,3,2,1,0:T(8,128)S(1)}) custom-call(f32[9,8,64,256]{3,2,1,0:T(8,128)} %get-tuple-element.43.cos, f32[9,8,64,256]{3,2,1,0:T(8,128)} %fld.3, f32[2,16,128]{2,1,0:T(8,128)S(1)} %get-tuple-element.48.rest_0_), custom_call_target="tpu_custom_call" | custom-call | flops 32768000 | bytes 14155776 | tf_op jit(solution)/shard_map/local_step/pallas_call | solution.py:231
  43.9 0.0 collective-permute-done.6.refs_2_
  43.9 0.0 collective-permute-done.7.refs_3_
  43.9 1.9 %fix_whole.1 = (f32[9,2,8,64,128]{4,3,2,1,0:T(8,128)S(1)}, f32[9,8,64,256]{3,2,1,0:T(8,128)}) custom-call(f32[2,10,80,128]{3,2,1,0:T(8,128)S(1)} %get-tuple-element.49.refs_0_, f32[9,2,8,64,128]{4,3,2,1,0:T(8,128)S(1)} %get-tuple-element.50.refs_1_, f32[2,648,128]{2,1,0:T(8,128)S(1)} %collective-permute-done.6.refs_2_, ...), custom_call_target="tpu_custom_call", output_to_operand_aliasing={{0}: (6, {}), {1}: (7, {})} | custom-call | tf_op jit(solution)/shard_map/fix_whole/pallas_call | solution.py:556
  45.9 0.7 %all-to-all-done = f32[32,8,256]{2,1,0:T(8,128)S(1)} async-done(((f32[32,8,256]{2,1,0:T(8,128)}), f32[32,8,256]{2,1,0:T(8,128)S(1)}, u32[]{:S(2)}, u32[]{:S(2)}) %all-to-all-start) | async-done | bytes 262176 | tf_op jit(solution)/shard_map/all_to_all | solution.py:595
  46.5 0.6 %reduce_sum.9 = f32[8,256]{1,0:T(8,128)} reduce(f32[32,8,256]{2,1,0:T(8,128)S(1)} %all-to-all-done, f32[]{:T(128)} %constant.0.clone.1), dimensions={0}, to_apply=%region_0.0 | reduce | flops 63488 | bytes 270340 | tf_op jit(solution)/shard_map/reduce_sum | solution.py:602
  (1 shorter events, 0.0 us)
Async XLA Ops:
  2.4 16.0 %collective-permute-start = (f32[2,640,128]{2,1,0:T(8,128)S(1)}, f32[2,640,128]{2,1,0:T(8,128)S(1)}, u32[]{:S(2)}, u32[]{:S(2)}) collective-permute-start(f32[2,640,128]{2,1,0:T(8,128)S(1)} %get-tuple-element.33), channel_id=1, source_target_pairs={{4,8},{8,4},{12,16},{16,12},{20,24},{24,20},{28,32},{32,28},{36,40... | collective-permute-start | bytes 1966088 | tf_op jit(solution)/shard_map/ppermute | solution.py:572
  7.4 11.0 %collective-permute-start.1 = (f32[2,640,128]{2,1,0:T(8,128)S(1)}, f32[2,640,128]{2,1,0:T(8,128)S(1)}, u32[]{:S(2)}, u32[]{:S(2)}) collective-permute-start(f32[2,640,128]{2,1,0:T(8,128)S(1)} %get-tuple-element.34), channel_id=1, source_target_pairs={{0,4},{4,0},{8,12},{12,8},{16,20},{20,16},{24,28},{28,24},{32,36},... | collective-permute-start | bytes 1966088 | tf_op jit(solution)/shard_map/ppermute | solution.py:572
  7.5 10.9 %collective-permute-start.2 = (f32[2,80,128]{2,1,0:T(8,128)S(1)}, f32[2,80,128]{2,1,0:T(8,128)S(1)}, u32[]{:S(2)}, u32[]{:S(2)}) collective-permute-start(f32[2,80,128]{2,1,0:T(8,128)S(1)} %get-tuple-element.35), channel_id=1, source_target_pairs={{1,2},{2,1},{5,6},{6,5},{9,10},{10,9},{13,14},{14,13},{17,18},{18,... | collective-permute-start | bytes 245768 | tf_op jit(solution)/shard_map/ppermute | solution.py:572
  8.1 10.3 %collective-permute-start.3 = (f32[2,80,128]{2,1,0:T(8,128)S(1)}, f32[2,80,128]{2,1,0:T(8,128)S(1)}, u32[]{:S(2)}, u32[]{:S(2)}) collective-permute-start(f32[2,80,128]{2,1,0:T(8,128)S(1)} %get-tuple-element.36), channel_id=1, source_target_pairs={{0,1},{1,0},{2,3},{3,2},{4,5},{5,4},{6,7},{7,6},{8,9},{9,8},{10,11... | collective-permute-start | bytes 245768 | tf_op jit(solution)/shard_map/ppermute | solution.py:572
  18.4 3.0 %copy-start = (s32[1,8,8]{2,1,0:T(8,128)S(1)}, s32[1,8,8]{2,1,0:T(8,128)}, u32[]{:S(2)}) copy-start(s32[1,8,8]{2,1,0:T(8,128)} %refs_0_.1) | copy-start | bytes 772
  19.2 5.2 %collective-permute-start.4 = (f32[2,88,128]{2,1,0:T(8,128)S(1)}, f32[2,88,128]{2,1,0:T(8,128)S(1)}, u32[]{:S(2)}, u32[]{:S(2)}) collective-permute-start(f32[2,88,128]{2,1,0:T(8,128)S(1)} %get-tuple-element.44), channel_id=1, source_target_pairs={{1,2},{2,1},{5,6},{6,5},{9,10},{10,9},{13,14},{14,13},{17,18},{18,... | collective-permute-start | bytes 270344 | tf_op jit(solution)/shard_map/ppermute | solution.py:572
  19.8 4.5 %collective-permute-start.5 = (f32[2,88,128]{2,1,0:T(8,128)S(1)}, f32[2,88,128]{2,1,0:T(8,128)S(1)}, u32[]{:S(2)}, u32[]{:S(2)}) collective-permute-start(f32[2,88,128]{2,1,0:T(8,128)S(1)} %get-tuple-element.45), channel_id=1, source_target_pairs={{0,1},{1,0},{2,3},{3,2},{4,5},{5,4},{6,7},{7,6},{8,9},{9,8},{10,11... | collective-permute-start | bytes 270344 | tf_op jit(solution)/shard_map/ppermute | solution.py:572
  24.4 19.5 %collective-permute-start.6 = (f32[2,648,128]{2,1,0:T(8,128)S(1)}, f32[2,648,128]{2,1,0:T(8,128)S(1)}, u32[]{:S(2)}, u32[]{:S(2)}) collective-permute-start(f32[2,648,128]{2,1,0:T(8,128)S(1)} %get-tuple-element.51), channel_id=1, source_target_pairs={{4,8},{8,4},{12,16},{16,12},{20,24},{24,20},{28,32},{32,28},{36,40... | collective-permute-start | bytes 1990664 | tf_op jit(solution)/shard_map/ppermute | solution.py:572
  29.2 14.7 %collective-permute-start.7 = (f32[2,648,128]{2,1,0:T(8,128)S(1)}, f32[2,648,128]{2,1,0:T(8,128)S(1)}, u32[]{:S(2)}, u32[]{:S(2)}) collective-permute-start(f32[2,648,128]{2,1,0:T(8,128)S(1)} %get-tuple-element.52), channel_id=1, source_target_pairs={{0,4},{4,0},{8,12},{12,8},{16,20},{20,16},{24,28},{28,24},{32,36},... | collective-permute-start | bytes 1990664 | tf_op jit(solution)/shard_map/ppermute | solution.py:572
  29.3 17.2 %all-to-all-start = ((f32[32,8,256]{2,1,0:T(8,128)}), f32[32,8,256]{2,1,0:T(8,128)S(1)}, u32[]{:S(2)}, u32[]{:S(2)}) async-start(f32[32,8,256]{2,1,0:T(8,128)} %bitcast), calls=%async_computation | async-start | bytes 524288 | tf_op jit(solution)/shard_map/all_to_all | solution.py:595
